TPU v7x, 32 devices: a whole 2x2x4 slice. The times are simulated.
32 devices in a mesh: groups: 2 (over y), space: 4 (over z), chan: 4 (over x, core).
Axes of the slice: x: 2, y: 2, z: 4, core: 2. Of those that a mesh axis runs over, the one named last changes fastest.
Arguments:
- image: bfloat16 [384, 64, 256], P('chan', ('groups', 'space')), parts along dimension 1, may hold values from -6 to 6
- dw_weight: bfloat16 [384, 49], P('chan'), may hold values from -0.875 to 0.875
- ln_gain: float32 [384], P('chan'), may hold values from 0.1 to 1.9
- ln_shift: float32 [384], P('chan'), may hold values from -3 to 3
- w_in: bfloat16 [384, 1536], P(None, 'chan'), may hold values from -0.3125 to 0.3125
- b_in: float32 [1536], P('chan'), may hold values from -3 to 3
- w_out: bfloat16 [1536, 384], P('chan'), may hold values from -0.15625 to 0.15625
- layer_scale: float32 [384], P('chan'), may hold values from 0.3 to 1
- cotangent: bfloat16 [384, 64, 256], P('chan', ('groups', 'space')), parts along dimension 1, may hold values from -6 to 6
Outputs:
- output: bfloat16 [384, 64, 256], P('chan', ('groups', 'space')), parts along dimension 1
- d_image: bfloat16 [384, 64, 256], P('chan', ('groups', 'space')), parts along dimension 1
- d_kernel: float32 [384, 98], P('chan', 'groups'), parts along dimension 1
- d_gain: float32 [768], P(('groups', 'chan')), parts along dimension 0
- d_shift: float32 [768], P(('groups', 'chan')), parts along dimension 0
- d_w_in: float32 [384, 3072], P('space', ('groups', 'chan')), parts along dimension 1
- d_b_in: float32 [3072], P(('groups', 'chan')), parts along dimension 0
- d_w_out: float32 [3072, 384], P(('groups', 'chan'), 'space'), parts along dimension 0
- d_scale: float32 [768], P(('groups', 'chan')), parts along dimension 0
There are 2 independent parts, one for each index of `groups`. A program takes and returns all parts, laid end to end along the dimension named above; an argument that names none is the same for every part. Nothing has to cross between parts.
All inputs are finite; a program needn't handle non-finite values.
Results may differ from a plain program's by a relative error of at most 0.012.
Values may be sent and summed in bfloat16 or wider, within the bound.
No kernel may reach another device: no remote copies, remote signals or barrier semaphores. Data moves between devices by JAX's collectives and lax.ppermute only.
A program may use at most 64 MiB of HBM per device.

v0:
```python
import jax
import jax.numpy as jnp
from jax import lax
from jax.sharding import PartitionSpec as P

D = 384


grad_scale = 1.0 / 128.0


def padded_2(shard, sides, width):
    for axis, dim in sides:
        size, length = (lax.axis_size(axis), shard.shape[dim])
        up = [(i, (i + 1) % size) for i in range(size - 1)]
        down = [(j, i) for i, j in up]
        last = lax.slice_in_dim(shard, length - width, length, axis=dim)
        initial = lax.slice_in_dim(shard, 0, width, axis=dim)
        before = lax.ppermute(last, axis, up)
        after = lax.ppermute(initial, axis, down)
        shard = jnp.concatenate([before, shard, after], axis=dim)
    return shard


def depthwise(padded, kernel, height, width):
    total = jnp.zeros((padded.shape[0], height, width), jnp.float32)
    for row_tap in range(7):
        for col_tap in range(7):
            weight = kernel[:, row_tap * 7 + col_tap][:, None, None]
            total = (
                total + weight * padded[:, row_tap : row_tap + height, col_tap : col_tap + width]
            )
    return total


def flipped(padded, kernel, height, width):
    total = jnp.zeros((padded.shape[0], height, width), jnp.float32)
    for row_tap in range(7):
        for col_tap in range(7):
            weight = kernel[:, row_tap * 7 + col_tap][:, None, None]
            total = (
                total
                + weight
                * padded[:, 6 - row_tap : 6 - row_tap + height, 6 - col_tap : 6 - col_tap + width]
            )
    return total


def kernel_grad(grad, padded, height, width):
    columns = []
    for row_tap in range(7):
        for col_tap in range(7):
            window = padded[:, row_tap : row_tap + height, col_tap : col_tap + width]
            columns.append(jnp.sum(grad * window, axis=(1, 2)))
    return jnp.stack(columns, axis=1)


def gelu_tanh(values):
    return jax.nn.gelu(values, approximate=True)


def per_device(image, dw_weight, ln_gain, ln_shift, w_in, b_in, w_out, layer_scale, cotangent):
    local_ch, height, width = image.shape
    pixels = height * width
    kernel = dw_weight.astype(jnp.float32)
    rim = padded_2(image, (("space", 1),), 3)
    padded = jnp.pad(rim.astype(jnp.float32), ((0, 0), (0, 0), (3, 3)))
    conv = depthwise(padded, kernel, height, width).reshape(local_ch, pixels)
    average = lax.psum(jnp.sum(conv, axis=0), "chan") / D
    centered = conv - average
    variance = lax.psum(jnp.sum(centered * centered, axis=0), "chan") / D
    inv_std = lax.rsqrt(variance + 1e-06)
    standard = centered * inv_std
    normed = (standard * ln_gain[:, None] + ln_shift[:, None]).astype(jnp.bfloat16)
    rows = w_in
    pre = jnp.einsum(
        "ck,cp->kp",
        rows,
        lax.all_gather(normed, "chan", axis=0, tiled=True),
        preferred_element_type=jnp.float32,
    )
    pre = pre + b_in[:, None]
    active = gelu_tanh(pre).astype(jnp.bfloat16)
    branch = lax.psum_scatter(
        jnp.einsum("kc,kp->cp", w_out, active, preferred_element_type=jnp.float32).astype(
            jnp.bfloat16
        ),
        "chan",
        scatter_dimension=0,
        tiled=True,
    ).astype(jnp.float32)
    source = image.astype(jnp.float32)
    output = (source + (layer_scale[:, None] * branch).reshape(local_ch, height, width)).astype(
        jnp.bfloat16
    )
    upstream = cotangent.astype(jnp.float32).reshape(local_ch, pixels)
    d_scale = jnp.sum(upstream * branch, axis=1)
    dbranch = (upstream * layer_scale[:, None]).astype(jnp.bfloat16)
    dfull = lax.all_gather(dbranch, "chan", axis=0, tiled=True)
    d_w_out = jnp.einsum("kp,cp->kc", active, dfull, preferred_element_type=jnp.float32)
    dactive = jnp.einsum("kc,cp->kp", w_out, dfull, preferred_element_type=jnp.float32)
    unused, pullback = jax.vjp(gelu_tanh, pre)
    dpre = pullback(dactive)[0]
    d_b_in = jnp.sum(dpre, axis=1)
    dpre_half = dpre.astype(jnp.bfloat16)
    d_w_in = jnp.einsum(
        "cp,kp->ck",
        lax.all_gather(normed, "chan", axis=0, tiled=True),
        dpre_half,
        preferred_element_type=jnp.float32,
    )
    rows = w_in
    dnormed = lax.psum_scatter(
        jnp.einsum("ck,kp->cp", rows, dpre_half, preferred_element_type=jnp.float32).astype(
            jnp.bfloat16
        ),
        "chan",
        scatter_dimension=0,
        tiled=True,
    ).astype(jnp.float32)
    d_shift = jnp.sum(dnormed, axis=1)
    d_gain = jnp.sum(dnormed * standard, axis=1)
    dstandard = dnormed * ln_gain[:, None]
    first, second = lax.psum(
        (jnp.sum(dstandard, axis=0), jnp.sum(dstandard * standard, axis=0)), "chan"
    )
    first = first / D
    second = second / D
    dconv = (
        (inv_std * (dstandard - first - standard * second))
        .astype(jnp.bfloat16)
        .reshape(local_ch, height, width)
    )
    grad_rows = padded_2(dconv, (("space", 1),), 3)
    grad_pad = jnp.pad(grad_rows.astype(jnp.float32), ((0, 0), (0, 0), (3, 3)))
    dsource = flipped(grad_pad, kernel, height, width)
    d_kernel = kernel_grad(dconv.astype(jnp.float32), padded, height, width)
    d_image = (cotangent.astype(jnp.float32) + dsource).astype(jnp.bfloat16)
    d_kernel, d_gain, d_shift, d_scale, d_b_in = lax.psum(
        (d_kernel, d_gain, d_shift, d_scale, d_b_in), "space"
    )
    d_w_in, d_w_out = (
        lax.psum_scatter(
            d_w_in.astype(jnp.bfloat16), "space", scatter_dimension=0, tiled=True
        ).astype(jnp.float32),
        lax.psum_scatter(
            d_w_out.astype(jnp.bfloat16), "space", scatter_dimension=1, tiled=True
        ).astype(jnp.float32),
    )
    return (
        output,
        d_image,
        d_kernel * grad_scale,
        d_gain * grad_scale,
        d_shift * grad_scale,
        d_w_in * grad_scale,
        d_b_in * grad_scale,
        d_w_out * grad_scale,
        d_scale * grad_scale,
    )


def solution(mesh):
    return jax.shard_map(
        per_device,
        mesh=mesh,
        in_specs=(
            P("chan", ("groups", "space"), None),
            P("chan", None),
            P("chan"),
            P("chan"),
            P(None, "chan"),
            P("chan"),
            P("chan", None),
            P("chan"),
            P("chan", ("groups", "space"), None),
        ),
        out_specs=(
            P("chan", ("groups", "space"), None),
            P("chan", ("groups", "space"), None),
            P("chan", "groups"),
            P(("groups", "chan")),
            P(("groups", "chan")),
            P("space", ("groups", "chan")),
            P(("groups", "chan")),
            P(("groups", "chan"), "space"),
            P(("groups", "chan")),
        ),
        check_vma=False,
    )
```

profile of v0, /device:TPU:0, one launch (start us, length us, event | category | flops | bytes accessed | tf_op | source)
XLA Modules:
  0.0 300.1 jit_solution(4644755886840996888)
XLA Ops:
  7.2 1.3 fusion.169
  8.5 4.9 %collective-permute-start = (bf16[96,3,256]{2,1,0:T(4,128)(2,1)S(1)}, bf16[96,3,256]{2,1,0:T(4,128)(2,1)S(1)}, u32[]{:S(2)}, u32[]{:S(2)}) collective-permute-start(bf16[96,3,256]{2,1,0:T(4,128)(2,1)S(1)} %get-tuple-element.76), channel_id=1, source_target_pairs={{0,4},{4,8},{8,12},{1,5},{5,9},{9,13},{2,6},{6,10},{10,14},{3,7},{... | collective-permute-start | bytes 442376 | tf_op jit(solution)/shard_map/ppermute | solution.py:19
  13.5 1.3 collective-permute-start.1
  14.8 0.7 convert_element_type.74
  15.8 1.8 collective-permute-done
  17.6 4.1 %collective-permute-done.1 = bf16[96,3,256]{2,1,0:T(4,128)(2,1)S(1)} collective-permute-done((bf16[96,3,256]{2,1,0:T(4,128)(2,1)S(1)}, bf16[96,3,256]{2,1,0:T(4,128)(2,1)S(1)}, u32[]{:S(2)}, u32[]{:S(2)}) %collective-permute-start.1) | collective-permute-done | bytes 147488 | tf_op jit(solution)/shard_map/ppermute | solution.py:20
  21.7 1.4 maximum_convert_fusion
  23.2 15.3 %fusion.167 = (f32[8,256]{1,0:T(8,128)S(1)}, f32[96,8,256]{2,1,0:T(8,128)S(1)}) fusion(f32[96]{0:T(128)S(1)} %get-tuple-element.79, f32[96]{0:T(128)S(1)} %get-tuple-element.80, f32[96]{0:T(128)S(1)} %get-tuple-element.81, f32[96,14,256]{2,1,0:T(8,128)S(1)} %maximum_convert_fusion, f32[96]{0:T(128)S(1)} %get-tuple-element.82, f32[96]{0:T(128)S(1)} %get-tuple-element.83, ...), kind=kLoop, calls=%fused_computation.388 | loop fusion | flops 19265536 | bytes 7897600 | tf_op jit(solution)/shard_map/reduce_sum | solution.py:69
  38.7 5.8 %psum.63 = f32[2048]{0:T(1024)S(1)} all-reduce(f32[2048]{0:T(1024)S(1)} %bitcast.263), channel_id=1, replica_groups=mesh['groups'=2,'space'=4,'chan'=4] {'chan'}, use_global_device_ids=true, to_apply=%region_1.2 | all-reduce | flops 2048 | bytes 16384 | tf_op jit(solution)/shard_map/psum | solution.py:69
  44.7 6.7 %psum.64 = f32[2048]{0:T(1024)S(1)} all-reduce(f32[2048]{0:T(1024)S(1)} %bitcast.264), channel_id=1, replica_groups=mesh['groups'=2,'space'=4,'chan'=4] {'chan'}, use_global_device_ids=true, to_apply=%region_3.4 | all-reduce | flops 2048 | bytes 16384 | tf_op jit(solution)/shard_map/psum | solution.py:71
  51.7 1.6 add_convert_fusion.1
  53.3 19.4 %all-gather.3.cloned.1.call-done = bf16[384,2048]{1,0:T(8,128)(2,1)} async-done(((bf16[96,2048]{1,0:T(8,128)(2,1)}), bf16[384,2048]{1,0:T(8,128)(2,1)}) %all-gather.3.cloned.1.call-update) | async-done | bytes 1572880 | tf_op jit(solution)/shard_map/all_gather | solution.py:79
  72.8 2.6 convolution_add_fusion
  75.4 1.7 copy-done.1
  77.0 2.5 fusion.10
  79.5 2.7 copy.29
  82.3 1.3 copy.26
  83.6 26.9 %reduce-scatter.13.cloned.1.call-done = bf16[96,2048]{1,0:T(8,128)(2,1)} async-done(((bf16[384,2048]{1,0:T(8,128)(2,1)}), bf16[96,2048]{1,0:T(8,128)(2,1)}) %reduce-scatter.13.cloned.1.call-update) | async-done | bytes 393232
  110.5 1.3 copy.30
  111.8 2.6 fusion.15
  114.4 2.0 copy.27
  116.5 19.8 %all-gather.5.cloned.1.call-done = bf16[384,2048]{1,0:T(8,128)(2,1)} async-done(((bf16[96,2048]{1,0:T(8,128)(2,1)}), bf16[384,2048]{1,0:T(8,128)(2,1)}) %all-gather.5.cloned.1.call-update) | async-done | bytes 1572880 | tf_op jit(solution)/shard_map/all_gather | solution.py:99
  136.3 4.4 %convolution_convert_fusion.2 = bf16[384,384]{0,1:T(8,128)(2,1)} fusion(bf16[384,2048]{1,0:T(8,128)(2,1)} %all-gather.5.cloned.1.call-done, f32[2048,384]{1,0:T(8,128)} %copy-done.1), kind=kOutput, calls=%fused_computation.155 | convolution fusion | flops 611205120 | bytes 5013504 | tf_op jit(solution)/shard_map/kp,cp->kc/dot_general | solution.py:100
  140.9 5.4 %fusion.170 = (f32[384]{0:T(512)S(1)}, bf16[384,2048]{0,1:T(8,128)(2,1)S(1)}) fusion(f32[2048,384]{1,0:T(8,128)} %copy-done.1, bf16[384,2048]{1,0:T(8,128)(2,1)} %all-gather.5.cloned.1.call-done, bf16[384,384]{1,0:T(8,128)(2,1)S(1)} %copy-done), kind=kOutput, calls=%fused_computation.391 | convolution fusion | flops 620494464 | bytes 6587904 | tf_op jit(solution)/shard_map/kc,cp->kp/dot_general | solution.py:101
  146.4 1.1 copy-done.6
  147.5 1.7 convolution_convert_fusion.3
  149.3 3.7 %fusion.11 = bf16[384,2048]{0,1:T(8,128)(2,1)} fusion(bf16[384,384]{1,0:T(8,128)(2,1)S(1)} %copy-done.7, bf16[384,2048]{0,1:T(8,128)(2,1)} %copy-done.6), kind=kOutput, calls=%fused_computation.152 | convolution fusion | flops 604766208 | bytes 3440640 | tf_op jit(solution)/shard_map/ck,kp->cp/dot_general | solution.py:114
  153.0 2.6 copy.31
  155.6 2.5 copy.25
  158.1 2.0 add_convert_fusion
  160.1 0.6 reduce-scatter.11.cloned.1.call-done
  160.7 1.6 convert_multiply_fusion.53
  162.3 19.4 %reduce-scatter.9.cloned.1.call-done = bf16[96,384]{1,0:T(8,128)(2,1)} async-done(((bf16[384,384]{1,0:T(8,128)(2,1)}), bf16[96,384]{1,0:T(8,128)(2,1)}) %reduce-scatter.9.cloned.1.call-update) | async-done | bytes 73744 | tf_op jit(solution)/shard_map/reduce_scatter | solution.py:143
  181.7 1.6 convert_multiply_fusion.54
  183.3 27.4 %reduce-scatter.15.cloned.1.call-done = bf16[96,2048]{1,0:T(8,128)(2,1)} async-done(((bf16[384,2048]{1,0:T(8,128)(2,1)}), bf16[96,2048]{1,0:T(8,128)(2,1)}) %reduce-scatter.15.cloned.1.call-update) | async-done | bytes 393232 | tf_op jit(solution)/shard_map/reduce_scatter | solution.py:113
  210.7 1.4 fusion.21
  212.1 10.4 %all-reduce.2 = (f32[2048]{0:T(1024)S(1)}, f32[2048]{0:T(1024)S(1)}) all-reduce(f32[2048]{0:T(1024)S(1)} %get-tuple-element.59, f32[2048]{0:T(1024)S(1)} %get-tuple-element.60), channel_id=1, replica_groups=mesh['groups'=2,'space'=4,'chan'=4] {'chan'}, use_global_device_ids=true, to_apply=%region_9.10 | all-reduce | flops 4096 | bytes 32768 | tf_op jit(solution)/shard_map/psum | solution.py:124
  222.5 1.2 fusion.19
  223.8 4.8 %fusion.68 = (f32[96]{0:T(128)S(1)}, f32[96]{0:T(128)S(1)}, f32[96]{0:T(128)S(1)}, f32[96]{0:T(128)S(1)}, f32[96]{0:T(128)S(1)}, /*index=5*/f32[96]{0:T(128)S(1)...) fusion(f32[96,14,256]{2,1,0:T(8,128)S(1)} %maximum_convert_fusi, ...), kind=kLoop, calls=%fused_computation.217 | loop fusion | flops 5307168 | bytes 6689664 | tf_op jit(solution)/shard_map/reduce_sum | solution.py:54
  228.5 8.7 %fusion.69 = (f32[96]{0:T(128)S(1)}, f32[96]{0:T(128)S(1)}, f32[96]{0:T(128)S(1)}, f32[96]{0:T(128)S(1)}, f32[96]{0:T(128)S(1)}, /*index=5*/f32[96]{0:T(128)S(1)...) fusion(f32[96,14,256]{2,1,0:T(8,128)S(1)} %maximum_convert_fusi, ...), kind=kLoop, calls=%fused_computation.218 | loop fusion | flops 7272768 | bytes 1776384 | tf_op jit(solution)/shard_map/reduce_sum | solution.py:54
  237.3 8.6 %fusion.70 = (f32[96]{0:T(128)S(1)}, f32[96]{0:T(128)S(1)}, f32[96]{0:T(128)S(1)}, f32[96]{0:T(128)S(1)}, f32[96]{0:T(128)S(1)}, /*index=5*/f32[96]{0:T(128)S(1)...) fusion(f32[96,14,256]{2,1,0:T(8,128)S(1)} %maximum_convert_fusi, ...), kind=kLoop, calls=%fused_computation.219 | loop fusion | flops 7272768 | bytes 2759424 | tf_op jit(solution)/shard_map/reduce_sum | solution.py:54
  246.3 19.0 %all-reduce.3 = (f32[96,49]{0,1:T(8,128)S(1)}, f32[96]{0:T(128)S(1)}, f32[96]{0:T(128)S(1)}, f32[384]{0:T(512)S(1)}, f32[96]{0:T(128)S(1)}) all-reduce(f32[96,49]{0,1:T(8,128)S(1)} %stack.199, f32[96]{0:T(128)S(1)} %get-tuple-element.58, f32[96]{0:T(128)S(1)} %get-tuple-element.61, ...), channel_id=1, replica_groups=mesh['groups'=2,'space'=4,'chan'=4] {'space'}, use_global_device_ids=true, to_apply=%region_59.60 | all-reduce | flops 5376 | bytes 43008 | tf_op jit(solution)/shard_map/psum | solution.py:139
  265.3 0.6 broadcast_multiply_fusion
  267.6 1.3 collective-permute-start.2
  268.9 1.3 collective-permute-start.3
  270.8 1.3 collective-permute-done.2
  272.1 4.4 %collective-permute-done.3 = bf16[96,3,256]{2,1,0:T(4,128)(2,1)S(1)} collective-permute-done((bf16[96,3,256]{2,1,0:T(4,128)(2,1)S(1)}, bf16[96,3,256]{2,1,0:T(4,128)(2,1)S(1)}, u32[]{:S(2)}, u32[]{:S(2)}) %collective-permute-start.3) | collective-permute-done | bytes 147488 | tf_op jit(solution)/shard_map/ppermute | solution.py:20
  277.2 16.1 %fusion.158 = bf16[96,8,256]{2,1,0:T(8,128)(2,1)} fusion(f32[96,14,256]{2,1,0:T(8,128)S(1)} %maximum_convert_fusion.1, f32[96]{0:T(128)S(1)} %get-tuple-element.79, f32[96]{0:T(128)S(1)} %get-tuple-element.80, f32[96]{0:T(128)S(1)} %copy-done.11, f32[96]{0:T(128)S(1)} %copy-done.13, f32[96]{0:T(128)S(1)} %copy-done.15, f32[96]{0:T(128)S(1)} %copy-done.17, ...), kind=kLoop, calls=%fused_computation.307 | loop fusion | flops 19660800 | bytes 7889408 | tf_op jit(solution)/shard_map/convert_element_type | solution.py:138
  (159 shorter events, 4.1 us)
Async XLA Ops:
  7.2 69.9 %copy-start = (bf16[384,384]{1,0:T(8,128)(2,1)S(1)}, bf16[384,384]{1,0:T(8,128)(2,1)}, u32[]{:S(2)}) copy-start(bf16[384,384]{1,0:T(8,128)(2,1)} %param.15) | copy-start | bytes 884740
  7.2 65.6 %all-gather.3.cloned.1.call-start = ((), (), s32[]{:S(2)}) async-start(), calls=%async_computation.4 | async-start | bytes 1966080 | tf_op jit(solution)/shard_map/all_gather | solution.py:79
  8.5 9.1 %collective-permute-start = (bf16[96,3,256]{2,1,0:T(4,128)(2,1)S(1)}, bf16[96,3,256]{2,1,0:T(4,128)(2,1)S(1)}, u32[]{:S(2)}, u32[]{:S(2)}) collective-permute-start(bf16[96,3,256]{2,1,0:T(4,128)(2,1)S(1)} %get-tuple-element.76), channel_id=1, source_target_pairs={{0,4},{4,8},{8,12},{1,5},{5,9},{9,13},{2,6},{6,10},{10,14},{3,7},{... | collective-permute-start | bytes 442376 | tf_op jit(solution)/shard_map/ppermute | solution.py:19
  13.5 8.3 %collective-permute-start.1 = (bf16[96,3,256]{2,1,0:T(4,128)(2,1)S(1)}, bf16[96,3,256]{2,1,0:T(4,128)(2,1)S(1)}, u32[]{:S(2)}, u32[]{:S(2)}) collective-permute-start(bf16[96,3,256]{2,1,0:T(4,128)(2,1)S(1)} %get-tuple-element.77), channel_id=1, source_target_pairs={{4,0},{8,4},{12,8},{5,1},{9,5},{13,9},{6,2},{10,6},{14,10},{7,3},{... | collective-permute-start | bytes 442376 | tf_op jit(solution)/shard_map/ppermute | solution.py:20
  15.6 22.9 %copy-start.10 = (f32[96]{0:T(128)}, f32[96]{0:T(128)S(1)}, u32[]{:S(2)}) copy-start(f32[96]{0:T(128)S(1)} %get-tuple-element.81) | copy-start | bytes 1156
  15.6 22.9 %copy-start.12 = (f32[96]{0:T(128)}, f32[96]{0:T(128)S(1)}, u32[]{:S(2)}) copy-start(f32[96]{0:T(128)S(1)} %get-tuple-element.82) | copy-start | bytes 1156
  15.6 22.9 %copy-start.14 = (f32[96]{0:T(128)}, f32[96]{0:T(128)S(1)}, u32[]{:S(2)}) copy-start(f32[96]{0:T(128)S(1)} %get-tuple-element.83) | copy-start | bytes 1156
  15.6 22.9 %copy-start.16 = (f32[96]{0:T(128)}, f32[96]{0:T(128)S(1)}, u32[]{:S(2)}) copy-start(f32[96]{0:T(128)S(1)} %get-tuple-element.84) | copy-start | bytes 1156
  15.6 22.9 %copy-start.18 = (f32[96]{0:T(128)}, f32[96]{0:T(128)S(1)}, u32[]{:S(2)}) copy-start(f32[96]{0:T(128)S(1)} %get-tuple-element.85) | copy-start | bytes 1156
  15.6 22.9 %copy-start.20 = (f32[96]{0:T(128)}, f32[96]{0:T(128)S(1)}, u32[]{:S(2)}) copy-start(f32[96]{0:T(128)S(1)} %get-tuple-element.86) | copy-start | bytes 1156
  15.6 22.9 %copy-start.26 = (f32[96]{0:T(128)}, f32[96]{0:T(128)S(1)}, u32[]{:S(2)}) copy-start(f32[96]{0:T(128)S(1)} %get-tuple-element.89) | copy-start | bytes 1156
  38.7 34.0 %copy-start.8 = (f32[384]{0:T(512)S(1)}, f32[384]{0:T(512)}, u32[]{:S(2)}) copy-start(f32[384]{0:T(512)} %param.14) | copy-start | bytes 4612
  53.3 57.2 %reduce-scatter.13.cloned.1.call-start = ((), (), s32[]{:S(2)}) async-start(), calls=%async_computation.8 | async-start | bytes 1966080
  82.2 29.6 %copy-start.64 = (f32[96]{0:T(128)S(1)}, f32[96]{0:T(128)}, u32[]{:S(2)}) copy-start(f32[96]{0:T(128)} %param.16) | copy-start | bytes 1156
  82.2 54.1 %all-gather.5.cloned.1.call-start = ((), (), s32[]{:S(2)}) async-start(), calls=%async_computation.5 | async-start | bytes 1966080 | tf_op jit(solution)/shard_map/all_gather | solution.py:99
  116.5 44.3 %reduce-scatter.11.cloned.1.call-start = ((), (), s32[]{:S(2)}) async-start(), calls=%async_computation.7 | async-start | bytes 368640 | tf_op jit(solution)/shard_map/reduce_scatter | solution.py:146
  140.7 41.0 %reduce-scatter.9.cloned.1.call-start = ((), (), s32[]{:S(2)}) async-start(), calls=%async_computation.6 | async-start | bytes 368640 | tf_op jit(solution)/shard_map/reduce_scatter | solution.py:143
  149.2 61.5 %reduce-scatter.15.cloned.1.call-start = ((), (), s32[]{:S(2)}) async-start(), calls=%async_computation.9 | async-start | bytes 1966080 | tf_op jit(solution)/shard_map/reduce_scatter | solution.py:113
  245.8 31.1 %copy-start.5 = (bf16[96,8,256]{2,1,0:T(8,128)(2,1)S(1)}, bf16[96,8,256]{2,1,0:T(8,128)(2,1)}, u32[]{:S(2)}) copy-start(bf16[96,8,256]{2,1,0:T(8,128)(2,1)} %param.17) | copy-start | bytes 1179652
  245.9 31.1 %copy-start.11 = (f32[96]{0:T(128)S(1)}, f32[96]{0:T(128)}, u32[]{:S(2)}) copy-start(f32[96]{0:T(128)} %copy-done.10) | copy-start | bytes 1156
  245.9 31.1 %copy-start.13 = (f32[96]{0:T(128)S(1)}, f32[96]{0:T(128)}, u32[]{:S(2)}) copy-start(f32[96]{0:T(128)} %copy-done.12) | copy-start | bytes 1156
  245.9 31.1 %copy-start.15 = (f32[96]{0:T(128)S(1)}, f32[96]{0:T(128)}, u32[]{:S(2)}) copy-start(f32[96]{0:T(128)} %copy-done.14) | copy-start | bytes 1156
  245.9 31.1 %copy-start.17 = (f32[96]{0:T(128)S(1)}, f32[96]{0:T(128)}, u32[]{:S(2)}) copy-start(f32[96]{0:T(128)} %copy-done.16) | copy-start | bytes 1156
  245.9 31.1 %copy-start.19 = (f32[96]{0:T(128)S(1)}, f32[96]{0:T(128)}, u32[]{:S(2)}) copy-start(f32[96]{0:T(128)} %copy-done.18) | copy-start | bytes 1156
  245.9 31.1 %copy-start.21 = (f32[96]{0:T(128)S(1)}, f32[96]{0:T(128)}, u32[]{:S(2)}) copy-start(f32[96]{0:T(128)} %copy-done.20) | copy-start | bytes 1156
  245.9 31.1 %copy-start.23 = (f32[96]{0:T(128)S(1)}, f32[96]{0:T(128)}, u32[]{:S(2)}) copy-start(f32[96]{0:T(128)} %copy-done.22) | copy-start | bytes 1156
  245.9 31.1 %copy-start.25 = (f32[96]{0:T(128)S(1)}, f32[96]{0:T(128)}, u32[]{:S(2)}) copy-start(f32[96]{0:T(128)} %copy-done.24) | copy-start | bytes 1156
  245.9 31.1 %copy-start.27 = (f32[96]{0:T(128)S(1)}, f32[96]{0:T(128)}, u32[]{:S(2)}) copy-start(f32[96]{0:T(128)} %copy-done.26) | copy-start | bytes 1156
  245.9 31.1 %copy-start.29 = (f32[96]{0:T(128)S(1)}, f32[96]{0:T(128)}, u32[]{:S(2)}) copy-start(f32[96]{0:T(128)} %copy-done.28) | copy-start | bytes 1156
  246.0 31.1 %copy-start.31 = (f32[96]{0:T(128)S(1)}, f32[96]{0:T(128)}, u32[]{:S(2)}) copy-start(f32[96]{0:T(128)} %copy-done.30) | copy-start | bytes 1156
  246.0 31.1 %copy-start.33 = (f32[96]{0:T(128)S(1)}, f32[96]{0:T(128)}, u32[]{:S(2)}) copy-start(f32[96]{0:T(128)} %copy-done.32) | copy-start | bytes 1156
  246.0 31.1 %copy-start.35 = (f32[96]{0:T(128)S(1)}, f32[96]{0:T(128)}, u32[]{:S(2)}) copy-start(f32[96]{0:T(128)} %copy-done.34) | copy-start | bytes 1156
  246.0 31.1 %copy-start.37 = (f32[96]{0:T(128)S(1)}, f32[96]{0:T(128)}, u32[]{:S(2)}) copy-start(f32[96]{0:T(128)} %copy-done.36) | copy-start | bytes 1156
  246.0 31.1 %copy-start.39 = (f32[96]{0:T(128)S(1)}, f32[96]{0:T(128)}, u32[]{:S(2)}) copy-start(f32[96]{0:T(128)} %copy-done.38) | copy-start | bytes 1156
  246.0 31.1 %copy-start.41 = (f32[96]{0:T(128)S(1)}, f32[96]{0:T(128)}, u32[]{:S(2)}) copy-start(f32[96]{0:T(128)} %copy-done.40) | copy-start | bytes 1156
  246.0 31.1 %copy-start.43 = (f32[96]{0:T(128)S(1)}, f32[96]{0:T(128)}, u32[]{:S(2)}) copy-start(f32[96]{0:T(128)} %copy-done.42) | copy-start | bytes 1156
  246.0 31.1 %copy-start.45 = (f32[96]{0:T(128)S(1)}, f32[96]{0:T(128)}, u32[]{:S(2)}) copy-start(f32[96]{0:T(128)} %copy-done.44) | copy-start | bytes 1156
  246.0 31.1 %copy-start.47 = (f32[96]{0:T(128)S(1)}, f32[96]{0:T(128)}, u32[]{:S(2)}) copy-start(f32[96]{0:T(128)} %copy-done.46) | copy-start | bytes 1156
  246.0 31.1 %copy-start.49 = (f32[96]{0:T(128)S(1)}, f32[96]{0:T(128)}, u32[]{:S(2)}) copy-start(f32[96]{0:T(128)} %copy-done.48) | copy-start | bytes 1156
  246.1 31.1 %copy-start.51 = (f32[96]{0:T(128)S(1)}, f32[96]{0:T(128)}, u32[]{:S(2)}) copy-start(f32[96]{0:T(128)} %copy-done.50) | copy-start | bytes 1156
  246.1 31.1 %copy-start.53 = (f32[96]{0:T(128)S(1)}, f32[96]{0:T(128)}, u32[]{:S(2)}) copy-start(f32[96]{0:T(128)} %copy-done.52) | copy-start | bytes 1156
  246.1 31.1 %copy-start.55 = (f32[96]{0:T(128)S(1)}, f32[96]{0:T(128)}, u32[]{:S(2)}) copy-start(f32[96]{0:T(128)} %copy-done.54) | copy-start | bytes 1156
  246.1 31.1 %copy-start.57 = (f32[96]{0:T(128)S(1)}, f32[96]{0:T(128)}, u32[]{:S(2)}) copy-start(f32[96]{0:T(128)} %copy-done.56) | copy-start | bytes 1156
  246.1 31.1 %copy-start.59 = (f32[96]{0:T(128)S(1)}, f32[96]{0:T(128)}, u32[]{:S(2)}) copy-start(f32[96]{0:T(128)} %copy-done.58) | copy-start | bytes 1156
  246.1 31.1 %copy-start.61 = (f32[96]{0:T(128)S(1)}, f32[96]{0:T(128)}, u32[]{:S(2)}) copy-start(f32[96]{0:T(128)} %copy-done.60) | copy-start | bytes 1156
  246.1 31.1 %copy-start.63 = (f32[96]{0:T(128)S(1)}, f32[96]{0:T(128)}, u32[]{:S(2)}) copy-start(f32[96]{0:T(128)} %copy-done.62) | copy-start | bytes 1156
  267.6 4.5 %collective-permute-start.2 = (bf16[96,3,256]{2,1,0:T(4,128)(2,1)S(1)}, bf16[96,3,256]{2,1,0:T(4,128)(2,1)S(1)}, u32[]{:S(2)}, u32[]{:S(2)}) collective-permute-start(bf16[96,3,256]{2,1,0:T(4,128)(2,1)S(1)} %get-tuple-element.74), channel_id=1, source_target_pairs={{0,4},{4,8},{8,12},{1,5},{5,9},{9,13},{2,6},{6,10},{10,14},{3,7},{... | collective-permute-start | bytes 442376 | tf_op jit(solution)/shard_map/ppermute | solution.py:19
  268.9 7.6 %collective-permute-start.3 = (bf16[96,3,256]{2,1,0:T(4,128)(2,1)S(1)}, bf16[96,3,256]{2,1,0:T(4,128)(2,1)S(1)}, u32[]{:S(2)}, u32[]{:S(2)}) collective-permute-start(bf16[96,3,256]{2,1,0:T(4,128)(2,1)S(1)} %get-tuple-element.75), channel_id=1, source_target_pairs={{4,0},{8,4},{12,8},{5,1},{9,5},{13,9},{6,2},{10,6},{14,10},{7,3},{... | collective-permute-start | bytes 442376 | tf_op jit(solution)/shard_map/ppermute | solution.py:20
  (27 other events, 456.7 us)
Sparse Core Ops, SparseCore 0:
  53.4 19.3 all-gather.2
  82.3 28.1 reduce-scatter.12
  116.6 19.6 all-gather.4
  140.8 19.8 reduce-scatter.10
  163.5 18.1 reduce-scatter.8
  184.3 26.3 reduce-scatter.14
where the time goes:
time: 301 us; the launch traced here: 300 us
  waiting for transfers between devices  125 us (42%)
  other arithmetic  70.7 us (23%)
  blocking collectives  41.8 us (14%)
  matrix products  20.2 us (7%)
  local copies, waits for them, and re-layouts  17.4 us (6%)
  between operations  15.3 us (5%)
  starting transfers between devices  9.25 us (3%)
    reduce_scatter x1, waiting for transfers between devices, per_device(): lax.psum_scatter(jnp.einsum('ck,kp->cp', rows, dpre_half, preferred_eleme...  27.4 us
    unnamed x7, waiting for transfers between devices  27 us
    reduce_sum x3, other arithmetic, kernel_grad(): columns.append(jnp.sum(grad * window, axis=(1, 2)))  22 us
    all_gather x1, waiting for transfers between devices, per_device(): dfull = lax.all_gather(dbranch, 'chan', axis=0, tiled=True)  19.8 us
    all_gather x1, waiting for transfers between devices, per_device(): lax.all_gather(normed, 'chan', axis=0, tiled=True)  19.4 us
    reduce_scatter x1, waiting for transfers between devices, per_device(): lax.psum_scatter(d_w_in.astype(jnp.bfloat16), 'space', scatter_dimension=...  19.4 us
    psum x1, blocking collectives, per_device(): lax.psum((d_kernel, d_gain, d_shift, d_scale, d_b_in), 'space')  19 us
    convert_element_type x1, other arithmetic, per_device(): d_image = (cotangent.astype(jnp.float32) + dsource).astype(jnp.bfloat16)  16.1 us
  transfers between devices with their start and end apart: 10, of which 10 were waited for; matrix products, arithmetic and copies ran while one was open for 8% of the time, Pallas kernels for 0%

commit v1 on v0

v1 whole, which is shorter than its diff:
```python
import functools

import jax
import jax.numpy as jnp
import numpy as np
from jax import lax
from jax.experimental import pallas as pl
from jax.experimental.pallas import tpu as pltpu
from jax.sharding import PartitionSpec as P

BF = jnp.bfloat16
F32 = jnp.float32
grad_scale = 1.0 / 128.0
SLOTS = 16
VMEM = pl.BlockSpec(memory_space=pltpu.VMEM)
SMEM = pl.BlockSpec(memory_space=pltpu.SMEM)
PARAMS = pltpu.CompilerParams(vmem_limit_bytes=40 << 20)
HI = lax.Precision.HIGHEST
NT = (((1,), (1,)), ((), ()))


def slot_row(slot, height):
    if slot < height:
        return slot
    if slot < height + 3:
        return slot - height - 3
    if slot < height + 6:
        return slot - 3
    return None


def tap_table(height, flip):
    table = np.zeros((height, 64, 8 * SLOTS), np.float32)
    for h in range(height):
        for s in range(7):
            for slot in range(SLOTS):
                row = slot_row(slot, height)
                if row is None:
                    continue
                r = h + 3 - row if flip else row - h + 3
                if 0 <= r < 7:
                    table[h, 7 * r + s, s * SLOTS + slot] = 1.0
    return table.astype(BF)


def shifted(tile, by):
    width = tile.shape[1]
    if by == 0:
        return tile
    lane = lax.broadcasted_iota(jnp.int32, tile.shape, 1)
    inside = lane < width - by if by > 0 else lane >= -by
    return jnp.where(inside, pltpu.roll(tile, (-by) % width, 1), 0.0)


def stack_shifts(tile, sign):
    parts = [shifted(tile, sign * (s - 3)).astype(BF) for s in range(7)]
    parts.append(jnp.zeros(tile.shape, BF))
    return jnp.concatenate(parts, axis=0)


def spread_taps(weight_ref, table_ref, taps_ref, height, local):
    for h in range(height):
        taps_ref[pl.ds(h * local, local), :] = jnp.dot(
            weight_ref[...], table_ref[h], preferred_element_type=F32
        )


def conv_kernel(core_ref, image_ref, halo_ref, weight_ref, table_ref, own_ref, send_ref, taps_ref, acc_ref):
    local, height, width = image_ref.shape
    spread_taps(weight_ref, table_ref, taps_ref, height, local)

    def body(i, carry):
        for u in range(8):
            ch = i * 8 + u
            tile = jnp.concatenate([image_ref[ch].astype(F32), halo_ref[ch].astype(F32)], axis=0)
            taps = taps_ref[pl.ds(ch, height, stride=local), :].astype(BF)
            value = jnp.dot(taps, stack_shifts(tile, 1), preferred_element_type=F32)
            for half in range(2):
                lanes = slice(half * 128, half * 128 + 128)
                acc_ref[half, pl.ds(ch, height, stride=local), :] = value[:, lanes]
        return carry

    lax.fori_loop(0, local // 8, body, 0)
    core = core_ref[0]
    rows = height // 2 * local
    for half in range(2):
        lanes = slice(half * 128, half * 128 + 128)
        mine = pl.multiple_of(core * rows, 16)
        theirs = pl.multiple_of((1 - core) * rows, 16)
        own_ref[:, lanes] = acc_ref[half, pl.ds(mine, rows), :].astype(BF)
        send_ref[:, lanes] = acc_ref[half, pl.ds(theirs, rows), :].astype(BF)


def conv_forward(core, image, halo, weight, table):
    local, height, width = image.shape
    rows = height // 2 * local
    return pl.pallas_call(
        conv_kernel,
        out_shape=[jax.ShapeDtypeStruct((rows, width), BF)] * 2,
        in_specs=[SMEM, VMEM, VMEM, VMEM, VMEM],
        out_specs=[VMEM, VMEM],
        scratch_shapes=[
            pltpu.VMEM((height * local, 8 * SLOTS), F32),
            pltpu.VMEM((2, height * local, 128), F32),
        ],
        compiler_params=PARAMS,
        name="conv_forward",
    )(core, image, halo, weight, table)


def mlp_kernel(blocks, me_ref, *refs):
    conv_refs = refs[:blocks]
    ct_refs = refs[blocks : 2 * blocks]
    (gain_ref, shift_ref, w_in_ref, w_inx_ref, w_int_ref, w_intx_ref, w_out_ref, w_outx_ref,
     w_outt_ref, w_outtx_ref, b_ref, bx_ref) = refs[2 * blocks : 2 * blocks + 12]
    (branch_ref, dn_ref, dn_own_ref, stand_ref, inv_ref, q_ref, own_ref, send_ref, db_ref,
     normed, centred, dbranch, acc_ref, bias_ref) = refs[2 * blocks + 12 :]
    step = pl.program_id(0)
    me = me_ref[0]
    local = conv_refs[0].shape[0]
    width = conv_refs[0].shape[1]
    channels = blocks * local
    hid = w_in_ref.shape[1]

    @pl.when(step == 0)
    def _():
        acc_ref[...] = jnp.zeros_like(acc_ref)
        bias_ref[...] = jnp.zeros_like(bias_ref)

    def where(j):
        return pl.ds(pl.multiple_of((me ^ j) * local, 16), local)

    total = jnp.zeros((1, width), F32)
    for j in range(blocks):
        value = conv_refs[j][...].astype(F32)
        centred[where(j), :] = value
        total = total + jnp.sum(value, axis=0, keepdims=True)
        dbranch[where(j), :] = ct_refs[j][...]
    average = total / channels
    value = centred[...] - average
    variance = jnp.sum(value * value, axis=0, keepdims=True) / channels
    inv_std = lax.rsqrt(variance + 1e-06)
    inv_ref[0] = inv_std
    for j in range(blocks):
        stand = (centred[where(j), :] - average) * inv_std
        rows = pl.ds(j * local, local)
        normed[where(j), :] = (stand * gain_ref[rows, :] + shift_ref[rows, :]).astype(BF)
        centred[where(j), :] = stand
    chip = pl.ds(pl.multiple_of((me // 2) * 2 * local, 16), 2 * local)
    stand_ref[...] = centred[chip, :]
    x = normed[...]
    d = dbranch[...]
    branch = jnp.zeros((channels, width), F32)
    dnormed = jnp.zeros((channels, width), F32)
    parts = ((w_in_ref, w_int_ref, w_out_ref, w_outt_ref, b_ref),
             (w_inx_ref, w_intx_ref, w_outx_ref, w_outtx_ref, bx_ref))
    k0, k1 = (0.7978845608028654, 0.044715)
    for part, (w_in, w_int, w_out, w_outt, bias) in enumerate(parts):
        pre = jnp.dot(w_int[...], x, preferred_element_type=F32) + bias[...]
        dact = jnp.dot(w_out[...], d, preferred_element_type=F32)
        square = pre * pre
        th = jnp.tanh(pre * (k0 + (k0 * k1) * square))
        half = 0.5 * pre
        active = (half + half * th).astype(BF)
        slope = 0.5 + 0.5 * th + half * (1.0 - th * th) * (k0 + (3.0 * k0 * k1) * square)
        dpre = dact * slope
        bias_ref[part] += dpre[:, :128] + dpre[:, 128:]
        dhalf = dpre.astype(BF)
        branch += jnp.dot(w_outt[...], active, preferred_element_type=F32)
        dnormed += jnp.dot(w_in[...], dhalf, preferred_element_type=F32)
        acc_ref[2 * part] += lax.dot_general(x, dhalf, NT, preferred_element_type=F32)
        acc_ref[2 * part + 1] += lax.dot_general(d, active, NT, preferred_element_type=F32)
    stand = centred[...]
    centred[...] = branch
    for j in range(blocks):
        branch_ref[j] = centred[where(j), :].astype(BF)
    centred[...] = dnormed
    first = jnp.zeros((1, width), F32)
    for k in range(blocks // 2):
        rows = pl.ds(pl.multiple_of(((me // 2) ^ k) * 2 * local, 16), 2 * local)
        if k == 0:
            dn_own_ref[...] = centred[rows, :]
        else:
            dn_ref[k - 1] = centred[rows, :].astype(BF)
    dbranch_gain = jnp.zeros((1, width), F32)
    for j in range(blocks):
        scaled = centred[where(j), :] * gain_ref[pl.ds(j * local, local), :]
        first = first + jnp.sum(scaled, axis=0, keepdims=True)
        centred[where(j), :] = scaled
    second = jnp.sum(centred[...] * stand, axis=0, keepdims=True)
    q_ref[0] = jnp.concatenate([first, second], axis=0)

    @pl.when(step == pl.num_programs(0) - 1)
    def _():
        for i in range(2):
            own_ref[i] = acc_ref[i]
            send_ref[i] = acc_ref[2 + i].astype(BF)
            db_ref[i] = lax.dot_general(
                jnp.ones((8, 128), F32), bias_ref[i], NT, preferred_element_type=F32, precision=HI
            )


def mlp(me, conv, ct, gain, shift, weights, biases):
    blocks = len(conv)
    rows, width = conv[0].shape
    local = gain.shape[0] // blocks
    steps = rows // local
    channels = blocks * local
    hid = weights[0].shape[1]
    tile = pl.BlockSpec((local, width), lambda i: (i, 0))

    def whole(a):
        return pl.BlockSpec(a.shape, lambda i: (0,) * a.ndim)

    small = [gain, shift, *weights, *biases]
    out_shape = [
        jax.ShapeDtypeStruct((blocks, rows, width), BF),
        jax.ShapeDtypeStruct((max(blocks // 2 - 1, 1), 2 * rows, width), BF),
        jax.ShapeDtypeStruct((2 * rows, width), F32),
        jax.ShapeDtypeStruct((2 * rows, width), F32),
        jax.ShapeDtypeStruct((steps, 1, width), F32),
        jax.ShapeDtypeStruct((steps, 2, width), F32),
        jax.ShapeDtypeStruct((2, channels, hid), F32),
        jax.ShapeDtypeStruct((2, channels, hid), BF),
        jax.ShapeDtypeStruct((2, 8, hid), F32),
    ]
    peers = out_shape[1].shape[0]
    out_specs = [
        pl.BlockSpec((blocks, local, width), lambda i: (0, i, 0)),
        pl.BlockSpec((peers, 2 * local, width), lambda i: (0, i, 0)),
        pl.BlockSpec((2 * local, width), lambda i: (i, 0)),
        pl.BlockSpec((2 * local, width), lambda i: (i, 0)),
        pl.BlockSpec((1, 1, width), lambda i: (i, 0, 0)),
        pl.BlockSpec((1, 2, width), lambda i: (i, 0, 0)),
        pl.BlockSpec((2, channels, hid), lambda i: (0, 0, 0)),
        pl.BlockSpec((2, channels, hid), lambda i: (0, 0, 0)),
        pl.BlockSpec((2, 8, hid), lambda i: (0, 0, 0)),
    ]
    return pl.pallas_call(
        functools.partial(mlp_kernel, blocks),
        grid=(steps,),
        out_shape=out_shape,
        in_specs=[SMEM] + [tile] * (2 * blocks) + [whole(a) for a in small],
        out_specs=out_specs,
        scratch_shapes=[
            pltpu.VMEM((channels, width), BF),
            pltpu.VMEM((channels, width), F32),
            pltpu.VMEM((channels, width), BF),
            pltpu.VMEM((4, channels, hid), F32),
            pltpu.VMEM((2, hid, 128), F32),
        ],
        compiler_params=PARAMS,
        name="mlp",
    )(me, *conv, *ct, *small)


def norm_kernel(peers, core_ref, *refs):
    dn_ref, stand_ref, inv_ref, gain_ref, q_ref = refs[:5]
    got = refs[5 : 5 + peers]
    got_q = refs[5 + peers : 5 + 2 * peers]
    (own_ref, send_ref, edge_own_ref, edge_send_ref, sums_ref, buf) = refs[5 + 2 * peers :]
    core = core_ref[0]
    steps = inv_ref.shape[0]
    both = dn_ref.shape[0] // steps
    local = both // 2
    channels = both * (peers + 1)
    shift_acc = jnp.zeros((both, 128), F32)
    gain_acc = jnp.zeros((both, 128), F32)
    for i in range(steps):
        rows = pl.ds(i * both, both)
        dn = dn_ref[rows, :]
        q = q_ref[i]
        for p in range(peers):
            dn = dn + got[p][0, rows, :].astype(F32)
            q = q + got_q[p][i]
        q = q / channels
        stand = stand_ref[rows, :]
        prod = dn * stand
        shift_acc += dn[:, :128] + dn[:, 128:]
        gain_acc += prod[:, :128] + prod[:, 128:]
        buf[i] = inv_ref[i] * (dn * gain_ref[...] - q[0:1] - stand * q[1:2])
    mine = pl.ds(pl.multiple_of(core * local, 16), local)
    theirs = pl.ds(pl.multiple_of((1 - core) * local, 16), local)
    for i in range(steps):
        own_ref[i] = buf[i, mine, :].astype(BF)
        send_ref[i] = buf[i, theirs, :].astype(BF)
    for i in range(3):
        edge_own_ref[i] = buf[i + core, mine, :].astype(BF)
        edge_send_ref[i] = buf[i + core, theirs, :].astype(BF)
    ones = jnp.ones((8, 128), F32)
    sums_ref[0] = lax.dot_general(ones, shift_acc, NT, preferred_element_type=F32, precision=HI)
    sums_ref[1] = lax.dot_general(ones, gain_acc, NT, preferred_element_type=F32, precision=HI)


def norm_backward(core, dn, stand, inv, gain, q, got, got_q):
    steps, _, width = inv.shape
    both = dn.shape[0] // steps
    local = both // 2
    return pl.pallas_call(
        functools.partial(norm_kernel, len(got)),
        out_shape=[
            jax.ShapeDtypeStruct((steps, local, width), BF),
            jax.ShapeDtypeStruct((steps, local, width), BF),
            jax.ShapeDtypeStruct((3, local, width), BF),
            jax.ShapeDtypeStruct((3, local, width), BF),
            jax.ShapeDtypeStruct((2, 8, both), F32),
        ],
        in_specs=[SMEM] + [VMEM] * (5 + 2 * len(got)),
        out_specs=[VMEM] * 5,
        scratch_shapes=[pltpu.VMEM((steps, both, width), F32)],
        compiler_params=PARAMS,
        name="norm_backward",
    )(core, dn, stand, inv, gain, q, *got, *got_q)


def back_kernel(group, core_ref, own_ref, other_ref, same_ref, cross_ref, image_ref, ct_ref, weight_ref,
                table_ref, dimage_ref, dkernel_ref, taps_ref, rows_ref, corr_ref):
    local, height, width = image_ref.shape
    core = core_ref[0]
    spread_taps(weight_ref, table_ref, taps_ref, height, local)
    half = height // 2
    for part in range(2):
        lanes = slice(part * 128, part * 128 + 128)
        for i in range(half):
            rows_ref[part, pl.ds(pl.multiple_of((core * half + i) * local, 8), local), :] = (
                own_ref[i, :, lanes].astype(F32))
            rows_ref[part, pl.ds(pl.multiple_of(((1 - core) * half + i) * local, 8), local), :] = (
                other_ref[i, :, lanes].astype(F32))
        for i in range(3):
            a = pl.multiple_of((height + 3 * (1 - core) + i) * local, 8)
            b = pl.multiple_of((height + 3 * core + i) * local, 8)
            rows_ref[part, pl.ds(a, local), :] = same_ref[i, :, lanes].astype(F32)
            rows_ref[part, pl.ds(b, local), :] = cross_ref[i, :, lanes].astype(F32)
        rows_ref[part, pl.ds((height + 6) * local, 2 * local), :] = jnp.zeros((2 * local, 128), F32)

    span = group * height
    lane = lax.broadcasted_iota(jnp.int32, (8 * SLOTS, span), 1)
    slot = lax.broadcasted_iota(jnp.int32, (SLOTS, span), 0)
    lane_row = lax.broadcasted_iota(jnp.int32, (SLOTS, span), 1) % height
    row = jnp.where(slot < height, slot, jnp.where(slot < height + 3, slot - height - 3, slot - 3))
    row = jnp.where(slot < height + 6, row, 1000)
    pick = (lax.broadcasted_iota(jnp.int32, (group, span), 0)
            == lax.broadcasted_iota(jnp.int32, (group, span), 1) // height).astype(F32)

    for g in range(local // group):
        right = image_ref[pl.ds(g * group, group)].astype(F32).reshape(span, width).astype(BF)
        corr_ref[...] = jnp.zeros_like(corr_ref)

        def body(i, carry):
            for u in range(8):
                inner = i * 8 + u
                ch = g * group + inner
                tile = jnp.concatenate(
                    [rows_ref[p, pl.ds(ch, SLOTS, stride=local), :] for p in range(2)], axis=1)
                stack = stack_shifts(tile, -1)
                taps = taps_ref[pl.ds(ch, height, stride=local), :].astype(BF)
                value = jnp.dot(taps, stack, preferred_element_type=F32)
                dimage_ref[ch] = (ct_ref[ch].astype(F32) + value).astype(BF)
                corr = lax.dot_general(stack, right, NT, preferred_element_type=F32)
                corr_ref[...] = jnp.where(lane // height == inner, corr, corr_ref[...])
            return carry

        lax.fori_loop(0, group // 8, body, 0)
        lines = []
        for r in range(7):
            mask = row == lane_row - r + 3
            for s in range(7):
                block = corr_ref[pl.ds(s * SLOTS, SLOTS), :]
                lines.append(jnp.sum(jnp.where(mask, block, 0.0), axis=0, keepdims=True))
        lines.append(jnp.zeros((7, span), F32))
        dkernel_ref[pl.ds(g * group, group), :] = lax.dot_general(
            pick, jnp.concatenate(lines, axis=0), NT, preferred_element_type=F32, precision=HI)


def conv_backward(core, own, other, same, cross, image, ct, weight, table):
    local, height, width = image.shape
    group = 32 if local % 32 == 0 else 16
    return pl.pallas_call(
        functools.partial(back_kernel, group),
        out_shape=[
            jax.ShapeDtypeStruct((local, height, width), BF),
            jax.ShapeDtypeStruct((local, 56), F32),
        ],
        in_specs=[SMEM] + [VMEM] * 8,
        out_specs=[VMEM, VMEM],
        scratch_shapes=[
            pltpu.VMEM((height * local, 8 * SLOTS), F32),
            pltpu.VMEM((2, SLOTS * local, 128), F32),
            pltpu.VMEM((8 * SLOTS, group * height), F32),
        ],
        compiler_params=PARAMS,
        name="conv_backward",
    )(core, own, other, same, cross, image, ct, weight, table)


def swap(value, axis, size, k):
    return lax.ppermute(value, axis, [(i, i ^ k) for i in range(size)])


def sum_over_space(value, size):
    if size > 4:
        return lax.psum(value, "space")
    total = value
    for k in range(1, size):
        total = total + swap(value, "space", size, k)
    return total


def scatter_over_space(value, size):
    me = lax.axis_index("space")
    rows = value.shape[1] // size
    half = value.astype(BF)
    if size > 4:
        return lax.psum_scatter(half, "space", scatter_dimension=1, tiled=True).astype(F32)
    total = lax.dynamic_slice_in_dim(value, me * rows, rows, axis=1)
    for k in range(1, size):
        piece = lax.dynamic_slice_in_dim(half, (me ^ k) * rows, rows, axis=1)
        total = total + swap(piece, "space", size, k).astype(F32)
    return total


def per_device(image, dw_weight, ln_gain, ln_shift, w_in, b_in, w_out, layer_scale, cotangent):
    local, height, width = image.shape
    hid = w_in.shape[1]
    n_chan, n_space = lax.axis_size("chan"), lax.axis_size("space")
    half = height // 2
    me = lax.axis_index("chan")
    core = me % 2
    me_s, core_s = (me.astype(jnp.int32).reshape(1), core.astype(jnp.int32).reshape(1))
    up = [(i, i + 1) for i in range(n_space - 1)]
    down = [(i + 1, i) for i in range(n_space - 1)]

    before = lax.ppermute(image[:, height - 3 :], "space", up)
    after = lax.ppermute(image[:, :3], "space", down)
    weight = jnp.pad(dw_weight, ((0, 0), (0, 15)))
    packed = jnp.concatenate([ln_gain, ln_shift, b_in])
    vectors = [packed] + [swap(packed, "chan", n_chan, k) for k in range(1, n_chan)]
    gain = jnp.concatenate([v[:local] for v in vectors])[:, None]
    shift = jnp.concatenate([v[local : 2 * local] for v in vectors])[:, None]
    biases = [vectors[k][2 * local :][:, None] for k in range(2)]
    w_inx = swap(w_in, "chan", n_chan, 1)
    w_outx = swap(w_out, "chan", n_chan, 1)
    weights = [w_in, w_inx, w_in.T, w_inx.T, w_out, w_outx, w_out.T, w_outx.T]

    upstream = cotangent.astype(F32)
    dbranch = (upstream * layer_scale[:, None, None]).astype(BF).transpose(1, 0, 2)
    dbranch = dbranch.reshape(2, half * local, width)
    d_mine = lax.dynamic_index_in_dim(dbranch, core, 0, keepdims=False)
    d_theirs = lax.dynamic_index_in_dim(dbranch, 1 - core, 0, keepdims=False)
    d_all = [d_mine] + [
        swap(d_theirs if k % 2 else d_mine, "chan", n_chan, k) for k in range(1, n_chan)
    ]

    halo = jnp.concatenate([before, after, jnp.zeros((local, 2, width), BF)], axis=1)
    mine, theirs = conv_forward(core_s, image, halo, weight, tap_table(height, False))
    conv = [mine] + [swap(theirs if k % 2 else mine, "chan", n_chan, k) for k in range(1, n_chan)]
    (branch, dn_send, dn, stand, inv, q, dw_own, dw_send, d_b) = mlp(
        me_s, conv, d_all, gain, shift, weights, biases)

    got_q = [swap(q, "chan", n_chan, 2 * k) for k in range(1, n_chan // 2)]
    got = [swap(dn_send[k - 1 : k], "chan", n_chan, 2 * k) for k in range(1, n_chan // 2)]
    dw = dw_own + swap(dw_send, "chan", n_chan, 1).astype(F32)
    dw = scatter_over_space(dw, n_space)

    g_own = gain[:local]
    g_other = gain[local : 2 * local]
    g_pair = jnp.where(core == 0, jnp.concatenate([g_own, g_other]), jnp.concatenate([g_other, g_own]))
    dconv, dconv_send, edge, edge_send, sums = norm_backward(core_s, dn, stand, inv, g_pair, q, got, got_q)
    other = swap(dconv_send, "chan", n_chan, 1)
    same_pairs, cross_pairs = [], []
    for s in range(n_space):
        for c in range(n_chan):
            t = s + 1 if c % 2 else s - 1
            if 0 <= t < n_space:
                same_pairs.append((s * n_chan + c, t * n_chan + c))
                cross_pairs.append((s * n_chan + c, t * n_chan + (c ^ 1)))
    same = lax.ppermute(edge, ("space", "chan"), same_pairs)
    cross = lax.ppermute(edge_send, ("space", "chan"), cross_pairs)

    parts = [branch[0]] + [swap(branch[k], "chan", n_chan, k) for k in range(1, n_chan)]
    b_mine = sum(p.astype(F32) for p in parts[0::2])
    b_theirs = sum(p.astype(F32) for p in parts[1::2])
    total = jnp.where(core == 0, jnp.stack([b_mine, b_theirs]), jnp.stack([b_theirs, b_mine]))
    total = total.reshape(height, local, width).transpose(1, 0, 2)
    output = (image.astype(F32) + layer_scale[:, None, None] * total).astype(BF)
    d_scale = jnp.sum(upstream * total, axis=(1, 2))

    d_image, d_kernel = conv_backward(
        core_s, dconv, other, same, cross, image, cotangent, weight, tap_table(height, True))

    sums = sums[:, 0].reshape(2, 2, local)
    s_mine = lax.dynamic_index_in_dim(sums, core, 1, keepdims=False)
    s_theirs = lax.dynamic_index_in_dim(sums, 1 - core, 1, keepdims=False)
    cross_core = swap(jnp.concatenate([s_theirs.reshape(-1), d_b[1, 0]]), "chan", n_chan, 1)
    vector = jnp.concatenate([s_mine.reshape(-1), d_b[0, 0]]) + cross_core
    vector = jnp.concatenate([vector, d_scale, d_kernel[:, :49].reshape(-1)])
    vector = sum_over_space(vector, n_space) * grad_scale
    d_shift, d_gain = vector[:local], vector[local : 2 * local]
    d_b_in = vector[2 * local : 2 * local + hid]
    d_scale = vector[2 * local + hid : 3 * local + hid]
    d_kernel = vector[3 * local + hid :].reshape(local, 49)
    dw = dw * grad_scale
    return (output, d_image, d_kernel, d_gain, d_shift, dw[0], d_b_in, dw[1].T, d_scale)


def solution(mesh):
    return jax.shard_map(
        per_device,
        mesh=mesh,
        in_specs=(
            P("chan", ("groups", "space"), None),
            P("chan", None),
            P("chan"),
            P("chan"),
            P(None, "chan"),
            P("chan"),
            P("chan", None),
            P("chan"),
            P("chan", ("groups", "space"), None),
        ),
        out_specs=(
            P("chan", ("groups", "space"), None),
            P("chan", ("groups", "space"), None),
            P("chan", "groups"),
            P(("groups", "chan")),
            P(("groups", "chan")),
            P("space", ("groups", "chan")),
            P(("groups", "chan")),
            P(("groups", "chan"), "space"),
            P(("groups", "chan")),
        ),
        check_vma=False,
    )
```

time: 301 us -> 113 us (0.38)
  waiting for transfers between devices: 125 us -> 41.1 us
  other arithmetic: 70.7 us -> 4.22 us
  blocking collectives: 41.8 us -> 0 us
  Pallas kernels: 0 us -> 25.7 us
  starting transfers between devices: 9.25 us -> 29.8 us
  matrix products: 20.2 us -> 0 us
  between operations: 15.3 us -> 1.12 us
  local copies, waits for them, and re-layouts: 17.4 us -> 10.3 us
    reduce_scatter x3 -> x0, waiting for transfers between devices: 47.5 us -> none  [the longest x1 27.4 us: per_device(): lax.psum_scatter(jnp.einsum('ck,kp->cp', rows, dpre_half, preferred_eleme...]
    psum x4 -> x0, blocking collectives: 41.8 us -> none  [the longest x1 19 us: per_device(): lax.psum((d_kernel, d_gain, d_shift, d_scale, d_b_in), 'space')]
    reduce_sum x7 -> x1, other arithmetic: 41.5 us -> 0.23 us  [per_device(): d_scale = jnp.sum(upstream * total, axis=(1, 2))]
    all_gather x2 -> x0, waiting for transfers between devices: 39.2 us -> none  [the longest x1 19.8 us: per_device(): dfull = lax.all_gather(dbranch, 'chan', axis=0, tiled=True)]
    ppermute x4 -> x29, waiting for transfers between devices: 11.7 us -> 41.1 us  [the longest x25 30 us: swap(): return lax.ppermute(value, axis, [(i, i ^ k) for i in range(size)])]
    unnamed x7 -> x0, waiting for transfers between devices: 27 us -> none
    pallas_call x0 -> x4, Pallas kernels: none -> 25.7 us  [the longest x1 11.4 us: mlp(): pl.pallas_call(functools.partial(mlp_kernel, blocks), grid=(steps,), out_...]
    convert_element_type x7 -> x2, other arithmetic: 23.4 us -> 2.39 us  [the longest x1 1.2 us: scatter_over_space(): half = value.astype(BF)]
  transfers between devices with their start and end apart: 10 -> 29, of which waited for: 10 -> 9; matrix products, arithmetic and copies ran while one was open for 8% -> 10% of each run, Pallas kernels for 0% -> 13%
where the time goes in v1:
time: 113 us; the launch traced here: 112 us
  waiting for transfers between devices  41.1 us (36%)
  starting transfers between devices  29.8 us (26%)
  Pallas kernels  25.7 us (23%)
  local copies, waits for them, and re-layouts  10.3 us (9%)
  other arithmetic  4.22 us (4%)
    ppermute x25, waiting for transfers between devices, swap(): return lax.ppermute(value, axis, [(i, i ^ k) for i in range(size)])  30 us
    ppermute x25, starting transfers between devices, swap(): return lax.ppermute(value, axis, [(i, i ^ k) for i in range(size)])  22.5 us
    pallas_call x1, Pallas kernels, mlp(): pl.pallas_call(functools.partial(mlp_kernel, blocks), grid=(steps,), out_...  11.4 us
    pallas_call x1, Pallas kernels, conv_backward(): pl.pallas_call(functools.partial(back_kernel, group), out_shape=[jax.Shap...  9.23 us
    ppermute x1, waiting for transfers between devices, per_device(): same = lax.ppermute(edge, ('space', 'chan'), same_pairs)  4.97 us
    pallas_call x1, Pallas kernels, conv_forward(): pl.pallas_call(conv_kernel, out_shape=[jax.ShapeDtypeStruct((rows, width)...  4.58 us
    ppermute x1, waiting for transfers between devices, per_device(): after = lax.ppermute(image[:, :3], 'space', down)  4.55 us
    ppermute x1, starting transfers between devices, per_device(): before = lax.ppermute(image[:, height - 3:], 'space', up)  4.07 us
  transfers between devices with their start and end apart: 29, of which 9 were waited for; matrix products, arithmetic and copies ran while one was open for 10% of the time, Pallas kernels for 13%

profile of v1, /device:TPU:0, one launch (start us, length us, event | category | flops | bytes accessed | tf_op | source)
XLA Modules:
  0.0 112.2 jit_solution(3922806781345330450)
XLA Ops:
  0.7 0.8 pad_maximum_fusion
  1.5 0.5 collective-permute-start.8
  1.9 2.6 %collective-permute-start.9 = (f32[576]{0:T(1024)S(1)}, f32[576]{0:T(1024)S(1)}, u32[]{:S(2)}, u32[]{:S(2)}) collective-permute-start(f32[576]{0:T(1024)S(1)} %pad_maximum_fusion), channel_id=1, source_target_pairs={{0,2},{1,3},{2,0},{3,1},{4,6},{5,7},{6,4},{7,5},{8,10},{9,11},{10,... | collective-permute-start | bytes 6920 | tf_op jit(solution)/shard_map/ppermute | solution.py:397
  4.6 1.2 %fusion = bf16[96,8,256]{2,0,1:T(8,128)(2,1)S(1)} fusion(f32[96]{0:T(128)} %param.18, bf16[96,8,256]{2,1,0:T(8,128)(2,1)} %ct_ref.1), kind=kLoop, calls=%fused_computation.3 | loop fusion | flops 589824 | bytes 786816 | tf_op jit(solution)/shard_map/convert_element_type | solution.py:446
  5.8 0.8 dynamic-slice_bitcast_fusion
  6.9 4.1 %collective-permute-start = (bf16[96,3,256]{2,1,0:T(4,128)(2,1)S(1)}, bf16[96,3,256]{2,1,0:T(4,128)(2,1)S(1)}, u32[]{:S(2)}, u32[]{:S(2)}) collective-permute-start(bf16[96,3,256]{2,1,0:T(4,128)(2,1)S(1)} %get-tuple-element.79), channel_id=1, source_target_pairs={{0,4},{4,8},{8,12},{1,5},{5,9},{9,13},{2,6},{6,10},{10,14},{3,7},{... | collective-permute-start | bytes 442376 | tf_op jit(solution)/shard_map/ppermute | solution.py:433
  11.2 0.2 copy.54
  11.8 1.3 %collective-permute-start.1 = (bf16[96,3,256]{2,1,0:T(4,128)(2,1)S(1)}, bf16[96,3,256]{2,1,0:T(4,128)(2,1)S(1)}, u32[]{:S(2)}, u32[]{:S(2)}) collective-permute-start(bf16[96,3,256]{2,1,0:T(4,128)(2,1)S(1)} %get-tuple-element.80), channel_id=1, source_target_pairs={{4,0},{8,4},{12,8},{5,1},{9,5},{13,9},{6,2},{10,6},{14,10},{7,3},{... | collective-permute-start | bytes 442376 | tf_op jit(solution)/shard_map/ppermute | solution.py:434
  13.3 0.5 collective-permute-start.12
  13.9 1.6 %collective-permute-done = bf16[96,3,256]{2,1,0:T(4,128)(2,1)S(1)} collective-permute-done((bf16[96,3,256]{2,1,0:T(4,128)(2,1)S(1)}, bf16[96,3,256]{2,1,0:T(4,128)(2,1)S(1)}, u32[]{:S(2)}, u32[]{:S(2)}) %collective-permute-start) | collective-permute-done | bytes 147488 | tf_op jit(solution)/shard_map/ppermute | solution.py:433
  15.4 0.4 collective-permute-start.7
  15.8 4.5 %collective-permute-done.1 = bf16[96,3,256]{2,1,0:T(4,128)(2,1)S(1)} collective-permute-done((bf16[96,3,256]{2,1,0:T(4,128)(2,1)S(1)}, bf16[96,3,256]{2,1,0:T(4,128)(2,1)S(1)}, u32[]{:S(2)}, u32[]{:S(2)}) %collective-permute-start.1) | collective-permute-done | bytes 147488 | tf_op jit(solution)/shard_map/ppermute | solution.py:434
  20.4 1.5 %collective-permute-start.6 = (bf16[384,256]{1,0:T(8,128)(2,1)}, bf16[384,256]{1,0:T(8,128)(2,1)}, u32[]{:S(2)}, u32[]{:S(2)}) collective-permute-start(bf16[384,256]{1,0:T(8,128)(2,1)} %get-tuple-element.78.refs_4_), channel_id=1, source_target_pairs={{0,2},{1,3},{2,0},{3,1},{4,6},{5,7},{6,4},{7,5},{8,10},{9,11},{10,... | collective-permute-start | bytes 589832 | tf_op jit(solution)/shard_map/ppermute | solution.py:397
  21.9 0.2 maximum_maximum_fusion.halo_ref
  22.1 4.6 %conv_forward.1 = (bf16[384,256]{1,0:T(8,128)(2,1)}, bf16[384,256]{1,0:T(8,128)(2,1)}) custom-call(s32[1]{0:T(128)} %bitcast.1.core_ref, bf16[96,8,256]{2,1,0:T(8,128)(2,1)S(1)} %copy-done, bf16[96,8,256]{2,1,0:T(8,128)(2,1)S(1)} %maximum_maximum_fusion.halo_ref, bf16[96,64]{1,0:T(8,128)(2,1)S(1)} %pad.4.weight_ref, bf16[8,64,128]{2,1,0:T(8,128)(2,1)S(1)} %copy-done.11), custom_call_target="tpu_custom_call" | custom-call | tf_op jit(solution)/shard_map/conv_forward/pallas_call | solution.py:97
  26.7 0.7 collective-permute-start.4
  27.4 1.5 %collective-permute-start.3 = (bf16[384,256]{1,0:T(8,128)(2,1)}, bf16[384,256]{1,0:T(8,128)(2,1)}, u32[]{:S(2)}, u32[]{:S(2)}) collective-permute-start(bf16[384,256]{1,0:T(8,128)(2,1)} %get-tuple-element.27.refs_0_), channel_id=1, source_target_pairs={{0,2},{1,3},{2,0},{3,1},{4,6},{5,7},{6,4},{7,5},{8,10},{9,11},{10,... | collective-permute-start | bytes 589832 | tf_op jit(solution)/shard_map/ppermute | solution.py:397
  29.5 0.8 copy.64
  30.2 0.8 copy.65
  31.2 0.2 copy.61.refs_15_
  31.5 7.0 %collective-permute-done.3.refs_2_ = bf16[384,256]{1,0:T(8,128)(2,1)} collective-permute-done((bf16[384,256]{1,0:T(8,128)(2,1)}, bf16[384,256]{1,0:T(8,128)(2,1)}, u32[]{:S(2)}, u32[]{:S(2)}) %collective-permute-start.3) | collective-permute-done | bytes 196640 | tf_op jit(solution)/shard_map/ppermute | solution.py:397
  38.5 0.9 copy-done.9
  39.4 11.4 %mlp.1 = (bf16[4,384,256]{2,1,0:T(8,128)(2,1)S(1)}, bf16[1,768,256]{2,1,0:T(8,128)(2,1)S(1)}, f32[768,256]{1,0:T(8,128)S(1)}, f32[768,256]{1,0:T(8,128)S(1)}, f3...) custom-call(s32[1]{0:T(128)} %bitcast.me_ref, ...), custom_call_target="tpu_custom_call" | custom-call | tf_op jit(solution)/shard_map/mlp/pallas_call | solution.py:239
  50.9 0.6 collective-permute-start.13
  51.5 0.3 copy-done.12
  52.0 1.1 collective-permute-start.16
  53.1 1.0 collective-permute-start.17
  54.1 4.6 %collective-permute-done.13 = bf16[384,256]{1,0:T(8,128)(2,1)S(1)} collective-permute-done((bf16[384,256]{1,0:T(8,128)(2,1)S(1)}, bf16[384,256]{1,0:T(8,128)(2,1)S(1)}, u32[]{:S(2)}, u32[]{:S(2)}) %collective-permute-start.13) | collective-permute-done | bytes 196640 | tf_op jit(solution)/shard_map/ppermute | solution.py:397
  58.8 9.8 %collective-permute-done.15 = bf16[384,256]{1,0:T(8,128)(2,1)S(1)} collective-permute-done((bf16[384,256]{1,0:T(8,128)(2,1)S(1)}, bf16[384,256]{1,0:T(8,128)(2,1)S(1)}, u32[]{:S(2)}, u32[]{:S(2)}) %collective-permute-start.15) | collective-permute-done | bytes 196640 | tf_op jit(solution)/shard_map/ppermute | solution.py:397
  68.8 0.6 norm_backward.1
  69.6 1.3 %collective-permute-start.21 = (f32[576]{0:T(1024)S(1)}, f32[576]{0:T(1024)S(1)}, u32[]{:S(2)}, u32[]{:S(2)}) collective-permute-start(f32[576]{0:T(1024)S(1)} %pad_maximum_fusion.1), channel_id=1, source_target_pairs={{0,1},{1,0},{2,3},{3,2},{4,5},{5,4},{6,7},{7,6},{8,9},{9,8},{10,11... | collective-permute-start | bytes 6920 | tf_op jit(solution)/shard_map/ppermute | solution.py:397
  70.9 0.2 fusion.1
  71.2 1.0 copy.66
  72.3 1.3 %collective-permute-start.19 = (bf16[3,96,256]{2,1,0:T(8,128)(2,1)S(1)}, bf16[3,96,256]{2,1,0:T(8,128)(2,1)S(1)}, u32[]{:S(2)}, u32[]{:S(2)}) collective-permute-start(bf16[3,96,256]{2,1,0:T(8,128)(2,1)S(1)} %get-tuple-element.37), channel_id=1, source_target_pairs={{1,5},{3,7},{4,0},{5,9},{6,2},{7,11},{8,4},{9,13},{10,6},{11,15},{... | collective-permute-start | bytes 442376 | tf_op jit(solution)/shard_map/ppermute | solution.py:477
  73.6 0.7 collective-permute-start.20
  74.4 5.0 %collective-permute-done.19.same_ref = bf16[3,96,256]{2,1,0:T(8,128)(2,1)S(1)} collective-permute-done((bf16[3,96,256]{2,1,0:T(8,128)(2,1)S(1)}, bf16[3,96,256]{2,1,0:T(8,128)(2,1)S(1)}, u32[]{:S(2)}, u32[]{:S(2)}) %collective-permute-start.19) | collective-permute-done | bytes 147488 | tf_op jit(solution)/shard_map/ppermute | solution.py:477
  79.4 9.2 %conv_backward.1 = (bf16[96,8,256]{2,1,0:T(8,128)(2,1)}, f32[96,56]{1,0:T(8,128)S(1)}) custom-call(s32[1]{0:T(128)} %bitcast.1.core_ref, bf16[4,96,256]{2,1,0:T(8,128)(2,1)S(1)} %get-tuple-element.35.own_ref, bf16[4,96,256]{2,1,0:T(8,128)(2,1)S(1)} %collective-permute-done.18.other_ref, bf16[3,96,256]{2,1,0:T(8,128)(2,1)S(1)} %collective-permute-done.19.same_ref, ...), custom_call_target="tpu_custom_call" | custom-call | tf_op jit(solution)/shard_map/conv_backward/pallas_call | solution.py:378
  88.9 3.4 %collective-permute-start.22 = (f32[5376]{0:T(1024)S(1)}, f32[5376]{0:T(1024)S(1)}, u32[]{:S(2)}, u32[]{:S(2)}) collective-permute-start(f32[5376]{0:T(1024)S(1)} %concatenate.57), channel_id=1, source_target_pairs={{0,4},{4,0},{8,12},{12,8},{1,5},{5,1},{9,13},{13,9},{2,6},{6,2},{1... | collective-permute-start | bytes 64520 | tf_op jit(solution)/shard_map/ppermute | solution.py:397
  92.3 2.6 %collective-permute-start.23 = (f32[5376]{0:T(1024)S(1)}, f32[5376]{0:T(1024)S(1)}, u32[]{:S(2)}, u32[]{:S(2)}) collective-permute-start(f32[5376]{0:T(1024)S(1)} %concatenate.57), channel_id=1, source_target_pairs={{0,8},{4,12},{8,0},{12,4},{1,9},{5,13},{9,1},{13,5},{2,10},{6,14},... | collective-permute-start | bytes 64520 | tf_op jit(solution)/shard_map/ppermute | solution.py:397
  94.9 1.2 %fusion.5 = (bf16[2,384,384]{2,1,0:T(8,128)(2,1)S(1)}, f32[2,384,384]{2,1,0:T(8,128)S(1)}) fusion(f32[2,384,384]{2,1,0:T(8,128)S(1)} %copy-done.5, bf16[2,384,384]{2,1,0:T(8,128)(2,1)} %collective-permute-done.25), kind=kLoop, calls=%fused_computation.39 | loop fusion | flops 884736 | bytes 3538944 | tf_op jit(solution)/shard_map/convert_element_type | solution.py:412
  96.2 1.0 collective-permute-start.26
  97.1 3.5 %collective-permute-start.27 = (bf16[2,96,384]{2,1,0:T(8,128)(2,1)S(1)}, bf16[2,96,384]{2,1,0:T(8,128)(2,1)S(1)}, u32[]{:S(2)}, u32[]{:S(2)}) collective-permute-start(bf16[2,96,384]{2,1,0:T(8,128)(2,1)S(1)} %get-tuple-element.76), channel_id=1, source_target_pairs={{0,8},{4,12},{8,0},{12,4},{1,9},{5,13},{9,1},{13,5},{2,10},{6,14},... | collective-permute-start | bytes 442376 | tf_op jit(solution)/shard_map/ppermute | solution.py:397
  100.8 0.6 slice.104
  101.7 0.7 copy.67
  102.3 0.6 fusion.7
  102.9 2.6 %collective-permute-done.26 = bf16[2,96,384]{2,1,0:T(8,128)(2,1)S(1)} collective-permute-done((bf16[2,96,384]{2,1,0:T(8,128)(2,1)S(1)}, bf16[2,96,384]{2,1,0:T(8,128)(2,1)S(1)}, u32[]{:S(2)}, u32[]{:S(2)}) %collective-permute-start.26) | collective-permute-done | bytes 147488 | tf_op jit(solution)/shard_map/ppermute | solution.py:397
  105.5 5.8 %collective-permute-done.27 = bf16[2,96,384]{2,1,0:T(8,128)(2,1)S(1)} collective-permute-done((bf16[2,96,384]{2,1,0:T(8,128)(2,1)S(1)}, bf16[2,96,384]{2,1,0:T(8,128)(2,1)S(1)}, u32[]{:S(2)}, u32[]{:S(2)}) %collective-permute-start.27) | collective-permute-done | bytes 147488 | tf_op jit(solution)/shard_map/ppermute | solution.py:397
  111.4 0.7 slice_bitcast_fusion.3
  (104 shorter events, 3.8 us)
Async XLA Ops:
  0.6 6.1 %copy-start = (bf16[96,8,256]{2,1,0:T(8,128)(2,1)S(1)}, bf16[96,8,256]{2,1,0:T(8,128)(2,1)}, u32[]{:S(2)}) copy-start(bf16[96,8,256]{2,1,0:T(8,128)(2,1)} %image_ref.3) | copy-start | bytes 1179652
  1.5 11.8 %collective-permute-start.8 = (f32[576]{0:T(1024)S(1)}, f32[576]{0:T(1024)S(1)}, u32[]{:S(2)}, u32[]{:S(2)}) collective-permute-start(f32[576]{0:T(1024)S(1)} %pad_maximum_fusion), channel_id=1, source_target_pairs={{0,1},{1,0},{2,3},{3,2},{4,5},{5,4},{6,7},{7,6},{8,9},{9,8},{10,11... | collective-permute-start | bytes 6920 | tf_op jit(solution)/shard_map/ppermute | solution.py:397
  1.9 9.9 %collective-permute-start.9 = (f32[576]{0:T(1024)S(1)}, f32[576]{0:T(1024)S(1)}, u32[]{:S(2)}, u32[]{:S(2)}) collective-permute-start(f32[576]{0:T(1024)S(1)} %pad_maximum_fusion), channel_id=1, source_target_pairs={{0,2},{1,3},{2,0},{3,1},{4,6},{5,7},{6,4},{7,5},{8,10},{9,11},{10,... | collective-permute-start | bytes 6920 | tf_op jit(solution)/shard_map/ppermute | solution.py:397
  4.5 8.7 %collective-permute-start.10 = (f32[576]{0:T(1024)S(1)}, f32[576]{0:T(1024)S(1)}, u32[]{:S(2)}, u32[]{:S(2)}) collective-permute-start(f32[576]{0:T(1024)S(1)} %pad_maximum_fusion), channel_id=1, source_target_pairs={{0,3},{1,2},{2,1},{3,0},{4,7},{5,6},{6,5},{7,4},{8,11},{9,10},{10,... | collective-permute-start | bytes 6920 | tf_op jit(solution)/shard_map/ppermute | solution.py:397
  4.6 6.4 %copy-start.15 = (f32[384]{0:T(512)S(1)}, f32[384]{0:T(512)}, u32[]{:S(2)}) copy-start(f32[384]{0:T(512)} %param.16) | copy-start | bytes 4612
  4.6 6.5 %copy-start.14 = (bf16[96,49]{0,1:T(8,128)(2,1)S(1)}, bf16[96,49]{0,1:T(8,128)(2,1)}, u32[]{:S(2)}) copy-start(bf16[96,49]{0,1:T(8,128)(2,1)} %param.12) | copy-start | bytes 28228
  4.6 6.6 %copy-start.2 = (bf16[384,384]{1,0:T(8,128)(2,1)S(1)}, bf16[384,384]{1,0:T(8,128)(2,1)}, u32[]{:S(2)}) copy-start(bf16[384,384]{1,0:T(8,128)(2,1)} %refs_10_.1) | copy-start | bytes 884740
  5.8 5.7 %copy-start.3 = (bf16[384,384]{1,0:T(8,128)(2,1)S(1)}, bf16[384,384]{1,0:T(8,128)(2,1)}, u32[]{:S(2)}) copy-start(bf16[384,384]{1,0:T(8,128)(2,1)} %refs_14_.1) | copy-start | bytes 884740
  6.6 20.1 %collective-permute-start.5 = (bf16[384,256]{1,0:T(8,128)(2,1)}, bf16[384,256]{1,0:T(8,128)(2,1)S(1)}, u32[]{:S(2)}, u32[]{:S(2)}) collective-permute-start(bf16[384,256]{1,0:T(8,128)(2,1)} %get-tuple-element.77), channel_id=1, source_target_pairs={{0,1},{1,0},{2,3},{3,2},{4,5},{5,4},{6,7},{7,6},{8,9},{9,8},{10,11... | collective-permute-start | bytes 589832 | tf_op jit(solution)/shard_map/ppermute | solution.py:397
  6.9 15.3 %copy-start.11 = (bf16[8,64,128]{2,1,0:T(8,128)(2,1)S(1)}, bf16[8,64,128]{2,1,0:T(8,128)(2,1)}, u32[]{:S(2)}) copy-start(bf16[8,64,128]{2,1,0:T(8,128)(2,1)} %constant.53.clone.table_ref) | copy-start | bytes 393220
  6.9 8.5 %collective-permute-start = (bf16[96,3,256]{2,1,0:T(4,128)(2,1)S(1)}, bf16[96,3,256]{2,1,0:T(4,128)(2,1)S(1)}, u32[]{:S(2)}, u32[]{:S(2)}) collective-permute-start(bf16[96,3,256]{2,1,0:T(4,128)(2,1)S(1)} %get-tuple-element.79), channel_id=1, source_target_pairs={{0,4},{4,8},{8,12},{1,5},{5,9},{9,13},{2,6},{6,10},{10,14},{3,7},{... | collective-permute-start | bytes 442376 | tf_op jit(solution)/shard_map/ppermute | solution.py:433
  11.5 17.4 %copy-start.16 = (f32[96]{0:T(128)S(1)}, f32[96]{0:T(128)}, u32[]{:S(2)}) copy-start(f32[96]{0:T(128)} %param.13) | copy-start | bytes 1156
  11.5 17.4 %copy-start.17 = (f32[96]{0:T(128)S(1)}, f32[96]{0:T(128)}, u32[]{:S(2)}) copy-start(f32[96]{0:T(128)} %param.14) | copy-start | bytes 1156
  11.7 17.7 %copy-start.6 = (bf16[96,64]{1,0:T(8,128)(2,1)}, bf16[96,64]{1,0:T(8,128)(2,1)S(1)}, u32[]{:S(2)}) copy-start(bf16[96,64]{1,0:T(8,128)(2,1)S(1)} %pad.4.weight_ref) | copy-start | bytes 36868
  11.8 8.6 %collective-permute-start.1 = (bf16[96,3,256]{2,1,0:T(4,128)(2,1)S(1)}, bf16[96,3,256]{2,1,0:T(4,128)(2,1)S(1)}, u32[]{:S(2)}, u32[]{:S(2)}) collective-permute-start(bf16[96,3,256]{2,1,0:T(4,128)(2,1)S(1)} %get-tuple-element.80), channel_id=1, source_target_pairs={{4,0},{8,4},{12,8},{5,1},{9,5},{13,9},{6,2},{10,6},{14,10},{7,3},{... | collective-permute-start | bytes 442376 | tf_op jit(solution)/shard_map/ppermute | solution.py:434
  13.2 13.5 %collective-permute-start.11 = (bf16[384,384]{0,1:T(8,128)(2,1)S(1)}, bf16[384,384]{0,1:T(8,128)(2,1)S(1)}, u32[]{:S(2)}, u32[]{:S(2)}) collective-permute-start(bf16[384,384]{0,1:T(8,128)(2,1)S(1)} %copy.54), channel_id=1, source_target_pairs={{0,1},{1,0},{2,3},{3,2},{4,5},{5,4},{6,7},{7,6},{8,9},{9,8},{10,11... | collective-permute-start | bytes 884744 | tf_op jit(solution)/shard_map/ppermute | solution.py:397
  13.3 14.1 %collective-permute-start.12 = (bf16[384,384]{0,1:T(8,128)(2,1)S(1)}, bf16[384,384]{0,1:T(8,128)(2,1)S(1)}, u32[]{:S(2)}, u32[]{:S(2)}) collective-permute-start(bf16[384,384]{0,1:T(8,128)(2,1)S(1)} %copy.56), channel_id=1, source_target_pairs={{0,1},{1,0},{2,3},{3,2},{4,5},{5,4},{6,7},{7,6},{8,9},{9,8},{10,11... | collective-permute-start | bytes 884744 | tf_op jit(solution)/shard_map/ppermute | solution.py:397
  15.4 16.1 %collective-permute-start.7 = (bf16[384,256]{1,0:T(8,128)(2,1)}, bf16[384,256]{1,0:T(8,128)(2,1)}, u32[]{:S(2)}, u32[]{:S(2)}) collective-permute-start(bf16[384,256]{1,0:T(8,128)(2,1)} %get-tuple-element.77), channel_id=1, source_target_pairs={{0,3},{1,2},{2,1},{3,0},{4,7},{5,6},{6,5},{7,4},{8,11},{9,10},{10,... | collective-permute-start | bytes 589832 | tf_op jit(solution)/shard_map/ppermute | solution.py:397
  20.4 11.1 %collective-permute-start.6 = (bf16[384,256]{1,0:T(8,128)(2,1)}, bf16[384,256]{1,0:T(8,128)(2,1)}, u32[]{:S(2)}, u32[]{:S(2)}) collective-permute-start(bf16[384,256]{1,0:T(8,128)(2,1)} %get-tuple-element.78.refs_4_), channel_id=1, source_target_pairs={{0,2},{1,3},{2,0},{3,1},{4,6},{5,7},{6,4},{7,5},{8,10},{9,11},{10,... | collective-permute-start | bytes 589832 | tf_op jit(solution)/shard_map/ppermute | solution.py:397
  26.7 3.5 %copy-start.8 = (bf16[384,256]{1,0:T(8,128)(2,1)}, bf16[384,256]{1,0:T(8,128)(2,1)S(1)}, u32[]{:S(2)}) copy-start(bf16[384,256]{1,0:T(8,128)(2,1)S(1)} %collective-permute-done.5.refs_5_) | copy-start | bytes 589828
  26.7 4.8 %collective-permute-start.2 = (bf16[384,256]{1,0:T(8,128)(2,1)}, bf16[384,256]{1,0:T(8,128)(2,1)}, u32[]{:S(2)}, u32[]{:S(2)}) collective-permute-start(bf16[384,256]{1,0:T(8,128)(2,1)} %get-tuple-element.28), channel_id=1, source_target_pairs={{0,1},{1,0},{2,3},{3,2},{4,5},{5,4},{6,7},{7,6},{8,9},{9,8},{10,11... | collective-permute-start | bytes 589832 | tf_op jit(solution)/shard_map/ppermute | solution.py:397
  26.7 11.8 %collective-permute-start.4 = (bf16[384,256]{1,0:T(8,128)(2,1)}, bf16[384,256]{1,0:T(8,128)(2,1)}, u32[]{:S(2)}, u32[]{:S(2)}) collective-permute-start(bf16[384,256]{1,0:T(8,128)(2,1)} %get-tuple-element.28), channel_id=1, source_target_pairs={{0,3},{1,2},{2,1},{3,0},{4,7},{5,6},{6,5},{7,4},{8,11},{9,10},{10,... | collective-permute-start | bytes 589832 | tf_op jit(solution)/shard_map/ppermute | solution.py:397
  27.4 11.1 %collective-permute-start.3 = (bf16[384,256]{1,0:T(8,128)(2,1)}, bf16[384,256]{1,0:T(8,128)(2,1)}, u32[]{:S(2)}, u32[]{:S(2)}) collective-permute-start(bf16[384,256]{1,0:T(8,128)(2,1)} %get-tuple-element.27.refs_0_), channel_id=1, source_target_pairs={{0,2},{1,3},{2,0},{3,1},{4,6},{5,7},{6,4},{7,5},{8,10},{9,11},{10,... | collective-permute-start | bytes 589832 | tf_op jit(solution)/shard_map/ppermute | solution.py:397
  38.5 0.9 copy-start.9
  50.8 17.8 %copy-start.4 = (f32[2,384,384]{2,1,0:T(8,128)}, f32[2,384,384]{2,1,0:T(8,128)S(1)}, u32[]{:S(2)}) copy-start(f32[2,384,384]{2,1,0:T(8,128)S(1)} %get-tuple-element.43) | copy-start | bytes 3538948
  50.8 1.0 copy-start.12
  50.8 1.1 %copy-start.13 = (f32[192,1]{1,0:T(8,128)S(1)}, f32[192,1]{1,0:T(8,128)}, u32[]{:S(2)}) copy-start(f32[192,1]{1,0:T(8,128)} %copy.65) | copy-start | bytes 2308
  50.9 7.9 %collective-permute-start.13 = (bf16[384,256]{1,0:T(8,128)(2,1)S(1)}, bf16[384,256]{1,0:T(8,128)(2,1)S(1)}, u32[]{:S(2)}, u32[]{:S(2)}) collective-permute-start(bf16[384,256]{1,0:T(8,128)(2,1)S(1)} %get-tuple-element.71), channel_id=1, source_target_pairs={{0,2},{1,3},{2,0},{3,1},{4,6},{5,7},{6,4},{7,5},{8,10},{9,11},{10,... | collective-permute-start | bytes 589832 | tf_op jit(solution)/shard_map/ppermute | solution.py:397
  51.9 42.9 %collective-permute-start.25 = (bf16[2,384,384]{2,1,0:T(8,128)(2,1)}, bf16[2,384,384]{2,1,0:T(8,128)(2,1)}, u32[]{:S(2)}, u32[]{:S(2)}) collective-permute-start(bf16[2,384,384]{2,1,0:T(8,128)(2,1)} %get-tuple-element.44), channel_id=1, source_target_pairs={{0,1},{1,0},{2,3},{3,2},{4,5},{5,4},{6,7},{7,6},{8,9},{9,8},{10,11... | collective-permute-start | bytes 1769480 | tf_op jit(solution)/shard_map/ppermute | solution.py:397
  52.0 16.7 %collective-permute-start.16 = (bf16[1,768,256]{2,1,0:T(8,128)(2,1)S(1)}, bf16[1,768,256]{2,1,0:T(8,128)(2,1)S(1)}, u32[]{:S(2)}, u32[]{:S(2)}) collective-permute-start(bf16[1,768,256]{2,1,0:T(8,128)(2,1)S(1)} %get-tuple-element.34), channel_id=1, source_target_pairs={{0,2},{1,3},{2,0},{3,1},{4,6},{5,7},{6,4},{7,5},{8,10},{9,11},{10,... | collective-permute-start | bytes 1179656 | tf_op jit(solution)/shard_map/ppermute | solution.py:397
  53.1 15.6 %collective-permute-start.17 = (f32[4,2,256]{2,1,0:T(2,128)S(1)}, f32[4,2,256]{2,1,0:T(2,128)S(1)}, u32[]{:S(2)}, u32[]{:S(2)}) collective-permute-start(f32[4,2,256]{2,1,0:T(2,128)S(1)} %get-tuple-element.33.refs_4_), channel_id=1, source_target_pairs={{0,2},{1,3},{2,0},{3,1},{4,6},{5,7},{6,4},{7,5},{8,10},{9,11},{10,... | collective-permute-start | bytes 24584 | tf_op jit(solution)/shard_map/ppermute | solution.py:397
  54.1 4.7 %collective-permute-start.14 = (bf16[384,256]{1,0:T(8,128)(2,1)S(1)}, bf16[384,256]{1,0:T(8,128)(2,1)S(1)}, u32[]{:S(2)}, u32[]{:S(2)}) collective-permute-start(bf16[384,256]{1,0:T(8,128)(2,1)S(1)} %get-tuple-element.73), channel_id=1, source_target_pairs={{0,1},{1,0},{2,3},{3,2},{4,5},{5,4},{6,7},{7,6},{8,9},{9,8},{10,11... | collective-permute-start | bytes 589832 | tf_op jit(solution)/shard_map/ppermute | solution.py:397
  58.8 9.8 %collective-permute-start.15 = (bf16[384,256]{1,0:T(8,128)(2,1)S(1)}, bf16[384,256]{1,0:T(8,128)(2,1)S(1)}, u32[]{:S(2)}, u32[]{:S(2)}) collective-permute-start(bf16[384,256]{1,0:T(8,128)(2,1)S(1)} %get-tuple-element.72), channel_id=1, source_target_pairs={{0,3},{1,2},{2,1},{3,0},{4,7},{5,6},{6,5},{7,4},{8,11},{9,10},{10,... | collective-permute-start | bytes 589832 | tf_op jit(solution)/shard_map/ppermute | solution.py:397
  68.7 2.2 %copy-start.1 = (bf16[96,8,256]{2,1,0:T(8,128)(2,1)S(1)}, bf16[96,8,256]{2,1,0:T(8,128)(2,1)}, u32[]{:S(2)}) copy-start(bf16[96,8,256]{2,1,0:T(8,128)(2,1)} %ct_ref.1) | copy-start | bytes 1179652
  68.7 2.2 %copy-start.18 = (f32[96]{0:T(128)S(1)}, f32[96]{0:T(128)}, u32[]{:S(2)}) copy-start(f32[96]{0:T(128)} %param.18) | copy-start | bytes 1156
  69.6 4.7 %collective-permute-start.21 = (f32[576]{0:T(1024)S(1)}, f32[576]{0:T(1024)S(1)}, u32[]{:S(2)}, u32[]{:S(2)}) collective-permute-start(f32[576]{0:T(1024)S(1)} %pad_maximum_fusion.1), channel_id=1, source_target_pairs={{0,1},{1,0},{2,3},{3,2},{4,5},{5,4},{6,7},{7,6},{8,9},{9,8},{10,11... | collective-permute-start | bytes 6920 | tf_op jit(solution)/shard_map/ppermute | solution.py:397
  70.9 8.4 %copy-start.7 = (bf16[96,64]{1,0:T(8,128)(2,1)S(1)}, bf16[96,64]{1,0:T(8,128)(2,1)}, u32[]{:S(2)}) copy-start(bf16[96,64]{1,0:T(8,128)(2,1)} %copy-done.6) | copy-start | bytes 36868
  70.9 8.4 %copy-start.10 = (bf16[8,64,128]{2,1,0:T(8,128)(2,1)S(1)}, bf16[8,64,128]{2,1,0:T(8,128)(2,1)}, u32[]{:S(2)}) copy-start(bf16[8,64,128]{2,1,0:T(8,128)(2,1)} %constant.54.clone.table_ref) | copy-start | bytes 393220
  71.2 23.7 %copy-start.5 = (f32[2,384,384]{2,1,0:T(8,128)S(1)}, f32[2,384,384]{2,1,0:T(8,128)}, u32[]{:S(2)}) copy-start(f32[2,384,384]{2,1,0:T(8,128)} %copy-done.4) | copy-start | bytes 3538948
  72.2 7.1 %collective-permute-start.18 = (bf16[4,96,256]{2,1,0:T(8,128)(2,1)S(1)}, bf16[4,96,256]{2,1,0:T(8,128)(2,1)S(1)}, u32[]{:S(2)}, u32[]{:S(2)}) collective-permute-start(bf16[4,96,256]{2,1,0:T(8,128)(2,1)S(1)} %get-tuple-element.36), channel_id=1, source_target_pairs={{0,1},{1,0},{2,3},{3,2},{4,5},{5,4},{6,7},{7,6},{8,9},{9,8},{10,11... | collective-permute-start | bytes 589832 | tf_op jit(solution)/shard_map/ppermute | solution.py:397
  72.3 7.0 %collective-permute-start.19 = (bf16[3,96,256]{2,1,0:T(8,128)(2,1)S(1)}, bf16[3,96,256]{2,1,0:T(8,128)(2,1)S(1)}, u32[]{:S(2)}, u32[]{:S(2)}) collective-permute-start(bf16[3,96,256]{2,1,0:T(8,128)(2,1)S(1)} %get-tuple-element.37), channel_id=1, source_target_pairs={{1,5},{3,7},{4,0},{5,9},{6,2},{7,11},{8,4},{9,13},{10,6},{11,15},{... | collective-permute-start | bytes 442376 | tf_op jit(solution)/shard_map/ppermute | solution.py:477
  73.6 5.7 %collective-permute-start.20 = (bf16[3,96,256]{2,1,0:T(8,128)(2,1)S(1)}, bf16[3,96,256]{2,1,0:T(8,128)(2,1)S(1)}, u32[]{:S(2)}, u32[]{:S(2)}) collective-permute-start(bf16[3,96,256]{2,1,0:T(8,128)(2,1)S(1)} %get-tuple-element.38), channel_id=1, source_target_pairs={{1,4},{3,6},{4,1},{5,8},{6,3},{7,10},{8,5},{9,12},{10,7},{11,14},{... | collective-permute-start | bytes 442376 | tf_op jit(solution)/shard_map/ppermute | solution.py:478
  88.9 11.8 %collective-permute-start.22 = (f32[5376]{0:T(1024)S(1)}, f32[5376]{0:T(1024)S(1)}, u32[]{:S(2)}, u32[]{:S(2)}) collective-permute-start(f32[5376]{0:T(1024)S(1)} %concatenate.57), channel_id=1, source_target_pairs={{0,4},{4,0},{8,12},{12,8},{1,5},{5,1},{9,13},{13,9},{2,6},{6,2},{1... | collective-permute-start | bytes 64520 | tf_op jit(solution)/shard_map/ppermute | solution.py:397
  92.3 8.4 %collective-permute-start.23 = (f32[5376]{0:T(1024)S(1)}, f32[5376]{0:T(1024)S(1)}, u32[]{:S(2)}, u32[]{:S(2)}) collective-permute-start(f32[5376]{0:T(1024)S(1)} %concatenate.57), channel_id=1, source_target_pairs={{0,8},{4,12},{8,0},{12,4},{1,9},{5,13},{9,1},{13,5},{2,10},{6,14},... | collective-permute-start | bytes 64520 | tf_op jit(solution)/shard_map/ppermute | solution.py:397
  94.9 5.9 %collective-permute-start.24 = (f32[5376]{0:T(1024)S(1)}, f32[5376]{0:T(1024)S(1)}, u32[]{:S(2)}, u32[]{:S(2)}) collective-permute-start(f32[5376]{0:T(1024)S(1)} %concatenate.57), channel_id=1, source_target_pairs={{0,12},{4,8},{8,4},{12,0},{1,13},{5,9},{9,5},{13,1},{2,14},{6,10},... | collective-permute-start | bytes 64520 | tf_op jit(solution)/shard_map/ppermute | solution.py:397
  96.2 9.4 %collective-permute-start.26 = (bf16[2,96,384]{2,1,0:T(8,128)(2,1)S(1)}, bf16[2,96,384]{2,1,0:T(8,128)(2,1)S(1)}, u32[]{:S(2)}, u32[]{:S(2)}) collective-permute-start(bf16[2,96,384]{2,1,0:T(8,128)(2,1)S(1)} %get-tuple-element.74), channel_id=1, source_target_pairs={{0,4},{4,0},{8,12},{12,8},{1,5},{5,1},{9,13},{13,9},{2,6},{6,2},{1... | collective-permute-start | bytes 442376 | tf_op jit(solution)/shard_map/ppermute | solution.py:397
  97.1 14.2 %collective-permute-start.27 = (bf16[2,96,384]{2,1,0:T(8,128)(2,1)S(1)}, bf16[2,96,384]{2,1,0:T(8,128)(2,1)S(1)}, u32[]{:S(2)}, u32[]{:S(2)}) collective-permute-start(bf16[2,96,384]{2,1,0:T(8,128)(2,1)S(1)} %get-tuple-element.76), channel_id=1, source_target_pairs={{0,8},{4,12},{8,0},{12,4},{1,9},{5,13},{9,1},{13,5},{2,10},{6,14},... | collective-permute-start | bytes 442376 | tf_op jit(solution)/shard_map/ppermute | solution.py:397
  100.6 10.7 %collective-permute-start.28 = (bf16[2,96,384]{2,1,0:T(8,128)(2,1)S(1)}, bf16[2,96,384]{2,1,0:T(8,128)(2,1)S(1)}, u32[]{:S(2)}, u32[]{:S(2)}) collective-permute-start(bf16[2,96,384]{2,1,0:T(8,128)(2,1)S(1)} %get-tuple-element.75), channel_id=1, source_target_pairs={{0,12},{4,8},{8,4},{12,0},{1,13},{5,9},{9,5},{13,1},{2,14},{6,10},... | collective-permute-start | bytes 442376 | tf_op jit(solution)/shard_map/ppermute | solution.py:397

commit v2 on v1

v2 whole, which is shorter than its diff:
```python
import functools

import jax
import jax.numpy as jnp
from jax import lax
from jax.experimental import pallas as pl
from jax.experimental.pallas import tpu as pltpu
from jax.sharding import PartitionSpec as P

BF = jnp.bfloat16
F32 = jnp.float32
grad_scale = 1.0 / 128.0
SLOTS = 16
VMEM = pl.BlockSpec(memory_space=pltpu.VMEM)
SMEM = pl.BlockSpec(memory_space=pltpu.SMEM)


def cost(microseconds):
    return pl.CostEstimate(flops=int(microseconds * 1.1e9), bytes_accessed=0, transcendentals=0)


def grant(mib):
    return pltpu.CompilerParams(vmem_limit_bytes=mib << 20)


HI = lax.Precision.HIGHEST
NT = (((1,), (1,)), ((), ()))


def column(row):
    return jnp.broadcast_to(row, (8, row.shape[1])).T[:, :1]


def shift_halves(a, b, by):
    if by == 0:
        return a, b
    lane = lax.broadcasted_iota(jnp.int32, a.shape, 1)
    k = (-by) % 128
    ra, rb = pltpu.roll(a, k, 1), pltpu.roll(b, k, 1)
    if by > 0:
        inner = lane < 128 - by
        return jnp.where(inner, ra, rb), jnp.where(inner, rb, 0.0)
    inner = lane >= -by
    return jnp.where(inner, ra, 0.0), jnp.where(inner, rb, ra)


def taps_kernel(flip, height, weight_ref, out_ref, rows_ref):
    local = out_ref.shape[0] // (7 * height)
    count = 7 * height
    tap = lax.broadcasted_iota(jnp.int32, (64, 128), 0)
    slot = lax.broadcasted_iota(jnp.int32, (64, 128), 1) % SLOTS
    row = jnp.where(slot < height + 3, slot, slot - SLOTS)
    weight = weight_ref[...].astype(F32).T[:local].astype(BF)
    for h in range(height):
        r = h + 3 - row if flip else row - h + 3
        base = jnp.where((r >= 0) & (r < 7) & (row >= -3), 7 * r, -100)
        for s in range(7):
            table = (tap == base + s).astype(F32).astype(BF)
            rows_ref[pl.ds((s * height + h) * local, local), :] = jnp.dot(
                weight, table, preferred_element_type=F32)
    lane = lax.broadcasted_iota(jnp.int32, (count, 128), 1) // SLOTS

    def body(g, carry):
        for u in range(0, 8, 2):
            pair = [
                jnp.where(lane == u + v, rows_ref[pl.ds(g * 8 + u + v, count, stride=local), :], 0.0)
                for v in range(2)
            ]
            start = pl.multiple_of((g * 8 + u) * count, 16)
            out_ref[pl.ds(start, 2 * count), :] = jnp.concatenate(pair, axis=0).astype(BF)
        return carry

    lax.fori_loop(0, local // 8, body, 0)


def make_taps(weight, local, height, flip):
    count = 7 * height
    return pl.pallas_call(
        functools.partial(taps_kernel, flip, height),
        out_shape=jax.ShapeDtypeStruct((local * count, 128), BF),
        in_specs=[VMEM],
        out_specs=VMEM,
        scratch_shapes=[pltpu.VMEM((count * local, 128), F32)],
        compiler_params=grant(6),
        cost_estimate=cost(2.4),
        name="taps_back" if flip else "taps_forward",
    )(weight)


def vector_of(lines, count):
    lines = lines.astype(F32)
    return [
        lines[r : r + 1] + lines[count + r : count + r + 1] + lines[2 * count + r : 2 * count + r + 1]
        for r in range(count)
    ]


def edge_kernel(ids_ref, image_ref, edge_a_ref, edge_b_ref, rows_ref):
    local, height, width = image_ref.shape
    odd = ids_ref[1] & 1

    def body(g, carry):
        for u in range(8):
            tile = image_ref[g * 8 + u].astype(F32)
            for part in range(2):
                rows_ref[part, pl.ds(g * 8 + u, height, stride=local), :] = tile[:, part * 128 : part * 128 + 128]
        return carry

    lax.fori_loop(0, local // 8, body, 0)
    top, bottom = (0, (height - 3) * local)
    for part in range(2):
        lanes = slice(part * 128, part * 128 + 128)
        to_a = pl.multiple_of(jnp.where(odd == 0, bottom, top), 16)
        to_b = pl.multiple_of(jnp.where(odd == 0, top, bottom), 16)
        edge_a_ref[:, lanes] = rows_ref[part, pl.ds(to_a, 3 * local), :].astype(BF)
        edge_b_ref[:, lanes] = rows_ref[part, pl.ds(to_b, 3 * local), :].astype(BF)


def edges(ids, image):
    local, height, width = image.shape
    return pl.pallas_call(
        edge_kernel,
        out_shape=[jax.ShapeDtypeStruct((3 * local, width), BF)] * 2,
        in_specs=[SMEM, VMEM],
        out_specs=[VMEM, VMEM],
        scratch_shapes=[pltpu.VMEM((2, height * local, 128), F32)],
        compiler_params=grant(3),
        cost_estimate=cost(1.2),
        name="edges",
    )(ids, image)


def pack_kernel(ids_ref, ct_ref, vector_ref, own_ref, send_ref, rows_ref, col_ref):
    local, height, width = ct_ref.shape
    core = ids_ref[0] & 1
    vector = vector_ref[...]
    count = vector.shape[1] // width
    col_ref[...] = column(vector)
    scale = col_ref[pl.ds(vector.shape[1] - 128, local), :]
    high = vector.astype(BF).astype(F32)
    middle = (vector - high).astype(BF).astype(F32)
    low = vector - high - middle
    lines = [part[:, r * width : r * width + width] for part in (high, middle, low) for r in range(count)]
    lines = jnp.concatenate(lines + [jnp.zeros((16 - 3 * count, width), F32)], axis=0).astype(BF)
    own_ref[pl.ds(height // 2 * local, 16), :] = lines
    send_ref[pl.ds(height // 2 * local, 16), :] = lines

    def body(g, carry):
        for u in range(8):
            tile = ct_ref[g * 8 + u].astype(F32)
            for part in range(2):
                rows_ref[part, pl.ds(g * 8 + u, height, stride=local), :] = tile[:, part * 128 : part * 128 + 128]
        return carry

    lax.fori_loop(0, local // 8, body, 0)
    for i in range(height // 2):
        rows = pl.ds(i * local, local)
        mine = pl.multiple_of((core * (height // 2) + i) * local, 16)
        theirs = pl.multiple_of(((1 - core) * (height // 2) + i) * local, 16)
        for part in range(2):
            lanes = slice(part * 128, part * 128 + 128)
            own_ref[rows, lanes] = (rows_ref[part, pl.ds(mine, local), :] * scale).astype(BF)
            send_ref[rows, lanes] = (rows_ref[part, pl.ds(theirs, local), :] * scale).astype(BF)


def pack(ids, ct, vector):
    local, height, width = ct.shape
    return pl.pallas_call(
        pack_kernel,
        out_shape=[jax.ShapeDtypeStruct((height // 2 * local + 16, width), BF)] * 2,
        in_specs=[SMEM, VMEM, VMEM],
        out_specs=[VMEM, VMEM],
        scratch_shapes=[
            pltpu.VMEM((2, height * local, 128), F32),
            pltpu.VMEM((vector.shape[1], 1), F32),
        ],
        compiler_params=grant(4),
        cost_estimate=cost(1.4),
        name="pack",
    )(ids, ct, vector)


def turn_kernel(*refs):
    for source, out in zip(refs[:4], refs[4:]):
        out[...] = source[...].T


def turn(*weights):
    return pl.pallas_call(
        turn_kernel,
        out_shape=[jax.ShapeDtypeStruct(w.shape[::-1], BF) for w in weights],
        in_specs=[VMEM] * 4,
        out_specs=[VMEM] * 4,
        compiler_params=grant(5),
        cost_estimate=cost(0.4),
        name="turn",
    )(*weights)


def merge_kernel(ids_ref, own_ref, got_ref, mine_ref, *rest):
    outs, buf = rest[:-1], rest[-1]
    rows = mine_ref.shape[1]
    me = ids_ref[1]
    for p in range(2):
        buf[...] = own_ref[p].astype(F32) + got_ref[p].astype(F32)
        mine_ref[p] = buf[pl.ds(pl.multiple_of(me * rows, 8), rows), :]
        for k, out in enumerate(outs):
            out[p] = buf[pl.ds(pl.multiple_of((me ^ (k + 1)) * rows, 8), rows), :].astype(BF)


def merge(ids, own, got, size):
    rows, hid = own.shape[1] // size, own.shape[2]
    return pl.pallas_call(
        merge_kernel,
        out_shape=[jax.ShapeDtypeStruct((2, rows, hid), F32)]
        + [jax.ShapeDtypeStruct((2, rows, hid), BF)] * (size - 1),
        in_specs=[SMEM, VMEM, VMEM],
        out_specs=[VMEM] * size,
        scratch_shapes=[pltpu.VMEM(own.shape[1:], F32)],
        compiler_params=grant(5),
        cost_estimate=cost(1),
        name="merge",
    )(ids, own, got)


def shift_sum(products, height, sign):
    left = products[3 * height : 4 * height, :128]
    right = products[3 * height : 4 * height, 128:]
    for s in (0, 1, 2, 4, 5, 6):
        block = products[s * height : (s + 1) * height]
        a, b = shift_halves(block[:, :128], block[:, 128:], sign * (s - 3))
        left, right = left + a, right + b
    return left, right


def conv_kernel(ids_ref, image_ref, got_a_ref, got_b_ref, taps_ref, own_ref, send_ref, image16_ref, acc_ref, rim_ref):
    local, height, width = image_ref.shape
    rows = own_ref.shape[0]
    count = 7 * height
    core, odd = ids_ref[0] & 1, ids_ref[1] & 1
    for part in range(2):
        lanes = slice(part * 128, part * 128 + 128)
        to_a = pl.multiple_of(5 * odd * local, 16)
        to_b = pl.multiple_of(5 * (1 - odd) * local, 16)
        rim_ref[part, pl.ds(to_a, 3 * local), :] = got_a_ref[:, lanes].astype(F32)
        rim_ref[part, pl.ds(to_b, 3 * local), :] = got_b_ref[:, lanes].astype(F32)
        rim_ref[part, pl.ds(3 * local, 2 * local), :] = jnp.zeros((2 * local, 128), F32)

    def body(g, carry):
        for u in range(8):
            ch = g * 8 + u
            pair = [rim_ref[p, pl.ds(ch, SLOTS - height, stride=local), :] for p in range(2)]
            tile = jnp.concatenate([image_ref[ch].astype(F32), jnp.concatenate(pair, axis=1)], axis=0)
            image16_ref[ch] = tile.astype(BF)
        right = image16_ref[pl.ds(g * 8, 8)].reshape(8 * SLOTS, width)
        taps = taps_ref[pl.ds(pl.multiple_of(g * 8 * count, 16), 8 * count), :]
        products = jnp.dot(taps, right, preferred_element_type=F32)
        for u in range(8):
            pair = shift_sum(products[u * count : (u + 1) * count], height, 1)
            for half in range(2):
                acc_ref[half, pl.ds(g * 8 + u, height, stride=local), :] = pair[half]
        return carry

    lax.fori_loop(0, local // 8, body, 0)
    for half in range(2):
        lanes = slice(half * 128, half * 128 + 128)
        mine = pl.multiple_of(core * rows, 16)
        theirs = pl.multiple_of((1 - core) * rows, 16)
        own_ref[:, lanes] = acc_ref[half, pl.ds(mine, rows), :].astype(BF)
        send_ref[:, lanes] = acc_ref[half, pl.ds(theirs, rows), :].astype(BF)


def conv_forward(ids, image, got_a, got_b, taps):
    local, height, width = image.shape
    rows = height // 2 * local
    return pl.pallas_call(
        conv_kernel,
        out_shape=[jax.ShapeDtypeStruct((rows, width), BF)] * 2
        + [jax.ShapeDtypeStruct((local, SLOTS, width), BF)],
        in_specs=[SMEM] + [VMEM] * 4,
        out_specs=[VMEM] * 3,
        scratch_shapes=[
            pltpu.VMEM((2, height * local, 128), F32),
            pltpu.VMEM((2, (SLOTS - height) * local, 128), F32),
        ],
        compiler_params=grant(6),
        cost_estimate=cost(5),
        name="conv_forward",
    )(ids, image, got_a, got_b, taps)


def mlp_kernel(blocks, me_ref, *refs):
    conv_refs = refs[:blocks]
    ct_refs = refs[blocks : 2 * blocks]
    vec_refs = refs[2 * blocks : 3 * blocks]
    (w_in_ref, w_inx_ref, w_int_ref, w_intx_ref, w_out_ref, w_outx_ref,
     w_outt_ref, w_outtx_ref) = refs[3 * blocks : 3 * blocks + 8]
    (branch_ref, dn_ref, dn_own_ref, stand_ref, inv_ref, q_ref, dw_ref, dwx_ref, small_ref, normed, centred, dbranch, acc_ref, bias_ref, col_ref) = refs[3 * blocks + 8 :]
    step = pl.program_id(0)
    me = me_ref[0]
    local = conv_refs[0].shape[0]
    width = conv_refs[0].shape[1]
    channels = blocks * local
    hid = w_in_ref.shape[1]

    @pl.when(step == 0)
    def _():
        acc_ref[...] = jnp.zeros_like(acc_ref)
        bias_ref[...] = jnp.zeros_like(bias_ref)
        for j in range(blocks):
            for r, line in enumerate(vector_of(vec_refs[j][...], col_ref.shape[1] // width)):
                col_ref[j, pl.ds(r * width, width), :] = column(line)

    def where(j):
        return pl.ds(pl.multiple_of((me ^ j) * local, 16), local)

    total = jnp.zeros((1, width), F32)
    for j in range(blocks):
        value = conv_refs[j][...].astype(F32)
        centred[where(j), :] = value
        total = total + jnp.sum(value, axis=0, keepdims=True)
        dbranch[where(j), :] = ct_refs[j][...]
    average = total / channels
    value = centred[...] - average
    variance = jnp.sum(value * value, axis=0, keepdims=True) / channels
    inv_std = lax.rsqrt(variance + 1e-06)
    inv_ref[0] = inv_std
    for j in range(blocks):
        stand = (centred[where(j), :] - average) * inv_std
        gain, shift = col_ref[j, pl.ds(0, local), :], col_ref[j, pl.ds(local, local), :]
        normed[where(j), :] = (stand * gain + shift).astype(BF)
        centred[where(j), :] = stand
    chip = pl.ds(pl.multiple_of((me // 2) * 2 * local, 16), 2 * local)
    stand_ref[...] = centred[chip, :]
    x = normed[...]
    d = dbranch[...]
    branch = jnp.zeros((channels, width), F32)
    dnormed = jnp.zeros((channels, width), F32)
    parts = ((w_in_ref, w_int_ref, w_out_ref, w_outt_ref),
             (w_inx_ref, w_intx_ref, w_outx_ref, w_outtx_ref))
    k0, k1 = (0.7978845608028654, 0.044715)
    for part, (w_in, w_int, w_out, w_outt) in enumerate(parts):
        bias = col_ref[part, pl.ds(2 * local, hid), :]
        pre = jnp.dot(w_int[...], x, preferred_element_type=F32) + bias
        dact = jnp.dot(w_out[...], d, preferred_element_type=F32)
        square = pre * pre
        th = jnp.tanh(pre * (k0 + (k0 * k1) * square))
        half = 0.5 * pre
        active = (half + half * th).astype(BF)
        slope = 0.5 + 0.5 * th + half * (1.0 - th * th) * (k0 + (3.0 * k0 * k1) * square)
        dpre = dact * slope
        bias_ref[part] += dpre[:, :128] + dpre[:, 128:]
        dhalf = dpre.astype(BF)
        branch += jnp.dot(w_outt[...], active, preferred_element_type=F32)
        dnormed += jnp.dot(w_in[...], dhalf, preferred_element_type=F32)
        acc_ref[2 * part] += lax.dot_general(x, dhalf, NT, preferred_element_type=F32)
        acc_ref[2 * part + 1] += lax.dot_general(d, active, NT, preferred_element_type=F32)
    stand = centred[...]
    centred[...] = branch
    for j in range(blocks):
        branch_ref[j] = centred[where(j), :].astype(BF)
    centred[...] = dnormed
    first = jnp.zeros((1, width), F32)
    for k in range(blocks // 2):
        rows = pl.ds(pl.multiple_of(((me // 2) ^ k) * 2 * local, 16), 2 * local)
        if k == 0:
            dn_own_ref[...] = centred[rows, :]
        else:
            dn_ref[k - 1, pl.ds(0, 2 * local), :] = centred[rows, :].astype(BF)
    for j in range(blocks):
        scaled = centred[where(j), :] * col_ref[j, pl.ds(0, local), :]
        first = first + jnp.sum(scaled, axis=0, keepdims=True)
        centred[where(j), :] = scaled
    second = jnp.sum(centred[...] * stand, axis=0, keepdims=True)
    q = jnp.concatenate([first, second], axis=0)
    q_ref[0] = q
    high = q.astype(BF)
    low = (q - high.astype(F32)).astype(BF)
    pad = jnp.zeros((12, width), F32)
    extra = jnp.concatenate([high.astype(F32), low.astype(F32), pad], axis=0).astype(BF)
    for k in range(1, blocks // 2):
        dn_ref[k - 1, pl.ds(2 * local, 16), :] = extra

    @pl.when(step == pl.num_programs(0) - 1)
    def _():
        ones = jnp.ones((8, 128), F32)
        for k in range(2):
            dw_ref[k] = acc_ref[k].astype(BF)
            dwx_ref[k] = acc_ref[2 + k].astype(BF)
        for j in range(blocks):
            prod = acc_ref[1, where(j), :] * w_outt_ref[where(j), :].astype(F32)
            prod = prod + acc_ref[3, where(j), :] * w_outtx_ref[where(j), :].astype(F32)
            if hid % 128:
                fold = jnp.pad(jnp.sum(prod, axis=1, keepdims=True), ((0, 0), (0, 127)))
            else:
                fold = sum(prod[:, i : i + 128] for i in range(128, hid, 128)) + prod[:, :128]
            sources = [fold] + [bias_ref[j, pl.ds(r * local, local), :] for r in range(hid // local if j < 2 else 0)]
            lines = [
                lax.dot_general(ones, a, NT, preferred_element_type=F32, precision=HI)[:1] for a in sources
            ]
            lines.append(jnp.zeros((8 - len(lines), local), F32))
            small_ref[j] = jnp.concatenate(lines, axis=0)


def mlp(me, conv, ct, lines, weights):
    blocks = len(conv)
    rows, width = conv[0].shape
    channels, hid = weights[0].shape
    local = channels // blocks
    steps = rows // local
    tile = pl.BlockSpec((local, width), lambda i: (i, 0))

    def whole(a):
        return pl.BlockSpec(a.shape, lambda i: (0,) * a.ndim)

    small = [*weights]
    last = pl.BlockSpec((16, width), lambda i: (rows // 16, 0))
    peers = max(blocks // 2 - 1, 1)
    out_shape = [
        jax.ShapeDtypeStruct((blocks, rows, width), BF),
        jax.ShapeDtypeStruct((peers, steps * (2 * local + 16), width), BF),
        jax.ShapeDtypeStruct((2 * rows, width), F32),
        jax.ShapeDtypeStruct((2 * rows, width), F32),
        jax.ShapeDtypeStruct((steps, 1, width), F32),
        jax.ShapeDtypeStruct((steps, 2, width), F32),
        *[jax.ShapeDtypeStruct((2, channels, hid), BF)] * 2,
        jax.ShapeDtypeStruct((blocks, 8, local), F32),
    ]
    out_specs = [
        pl.BlockSpec((blocks, local, width), lambda i: (0, i, 0)),
        pl.BlockSpec((peers, 2 * local + 16, width), lambda i: (0, i, 0)),
        pl.BlockSpec((2 * local, width), lambda i: (i, 0)),
        pl.BlockSpec((2 * local, width), lambda i: (i, 0)),
        pl.BlockSpec((1, 1, width), lambda i: (i, 0, 0)),
        pl.BlockSpec((1, 2, width), lambda i: (i, 0, 0)),
        *[pl.BlockSpec((2, channels, hid), lambda i: (0, 0, 0))] * 2,
        pl.BlockSpec((blocks, 8, local), lambda i: (0, 0, 0)),
    ]
    return pl.pallas_call(
        functools.partial(mlp_kernel, blocks),
        grid=(steps,),
        out_shape=out_shape,
        in_specs=[SMEM] + [tile] * (2 * blocks) + [last] * blocks + [whole(a) for a in small],
        out_specs=out_specs,
        scratch_shapes=[
            pltpu.VMEM((channels, width), BF),
            pltpu.VMEM((channels, width), F32),
            pltpu.VMEM((channels, width), BF),
            pltpu.VMEM((4, channels, hid), F32),
            pltpu.VMEM((2, hid, 128), F32),
            pltpu.VMEM((blocks, lines * width, 1), F32),
        ],
        compiler_params=grant(22),
        cost_estimate=cost(11),
        name="mlp",
    )(me, *conv, *ct, *ct, *small)


def norm_kernel(peers, count, core_ref, *refs):
    dn_ref, stand_ref, inv_ref, vec_ref, vecx_ref, q_ref, scale_ref, small_ref = refs[:8]
    got = refs[8 : 8 + peers]
    got_small = refs[8 + peers : 9 + 3 * peers]
    (own_ref, send_ref, edge_own_ref, edge_send_ref, sums_ref, sums_send_ref, buf, gain_ref, fold_ref) = refs[9 + 3 * peers :]
    core = core_ref[0] & 1
    steps = inv_ref.shape[0]
    both = dn_ref.shape[0] // steps
    local = both // 2
    channels = both * (peers + 1)
    mine = pl.ds(pl.multiple_of(core * local, 16), local)
    theirs = pl.ds(pl.multiple_of((1 - core) * local, 16), local)
    last = pl.ds(vec_ref.shape[0] - 16, 16)
    gain_ref[mine, :] = column(vector_of(vec_ref[last, :], count)[0])[:local]
    gain_ref[theirs, :] = column(vector_of(vecx_ref[last, :], count)[0])[:local]
    shift_acc = jnp.zeros((both, 128), F32)
    gain_acc = jnp.zeros((both, 128), F32)
    for i in range(steps):
        rows = pl.ds(i * both, both)
        dn = dn_ref[rows, :]
        q = q_ref[i]
        for p in range(peers):
            start = i * (both + 16)
            dn = dn + got[p][0, pl.ds(start, both), :].astype(F32)
            extra = got[p][0, pl.ds(start + both, 16), :].astype(F32)
            q = q + (extra[0:2] + extra[2:4])
        q = q / channels
        stand = stand_ref[rows, :]
        prod = dn * stand
        shift_acc += dn[:, :128] + dn[:, 128:]
        gain_acc += prod[:, :128] + prod[:, 128:]
        buf[i] = inv_ref[i] * (dn * gain_ref[...] - q[0:1] - stand * q[1:2])
    for i in range(steps):
        own_ref[i] = buf[i, mine, :].astype(BF)
        send_ref[i] = buf[i, theirs, :].astype(BF)
    for i in range(3):
        edge_own_ref[i] = buf[i + core, mine, :].astype(BF)
        edge_send_ref[i] = buf[i + core, theirs, :].astype(BF)
    ones = jnp.ones((8, 128), F32)
    fold_ref[0], fold_ref[1] = shift_acc, gain_acc
    small = small_ref[0]
    for got_ref in got_small:
        small = small + got_ref[...]
    start = scale_ref.shape[1] - 128
    lines = [small[:1] / scale_ref[:, start : start + local], small[1:5]]
    for rows, out, rest in (
        (mine, sums_ref, lines), (theirs, sums_send_ref, [jnp.zeros((5, local), F32)])):
        pair = [
            lax.dot_general(ones, fold_ref[k, rows, :], NT, preferred_element_type=F32, precision=HI)[:1]
            for k in range(2)
        ]
        out[...] = jnp.concatenate(pair + rest + [jnp.zeros((1, local), F32)], axis=0)


def norm_backward(core, count, dn, stand, inv, vector, vector_x, q, scale, small, got, got_small):
    steps, _, width = inv.shape
    both = dn.shape[0] // steps
    local = both // 2
    return pl.pallas_call(
        functools.partial(norm_kernel, len(got), count),
        out_shape=[
            jax.ShapeDtypeStruct((steps, local, width), BF),
            jax.ShapeDtypeStruct((steps, local, width), BF),
            jax.ShapeDtypeStruct((3, local, width), BF),
            jax.ShapeDtypeStruct((3, local, width), BF),
            jax.ShapeDtypeStruct((8, local), F32),
            jax.ShapeDtypeStruct((8, local), F32),
        ],
        in_specs=[SMEM] + [VMEM] * (8 + len(got) + len(got_small)),
        out_specs=[VMEM] * 6,
        scratch_shapes=[
            pltpu.VMEM((steps, both, width), F32),
            pltpu.VMEM((both, 1), F32),
            pltpu.VMEM((2, both, 128), F32),
        ],
        compiler_params=grant(5),
        cost_estimate=cost(1.3),
        name="norm_backward",
    )(core, dn, stand, inv, vector, vector_x, q, scale, small, *got, *got_small)


def fill_tile(rows_ref, own_ref, other_ref, core, local):
    half = own_ref.shape[0]
    for part in range(2):
        lanes = slice(part * 128, part * 128 + 128)
        for i in range(half):
            rows_ref[part, pl.ds(pl.multiple_of((core * half + i) * local, 8), local), :] = (
                own_ref[i, :, lanes].astype(F32))
            rows_ref[part, pl.ds(pl.multiple_of(((1 - core) * half + i) * local, 8), local), :] = (
                other_ref[i, :, lanes].astype(F32))


def kernel_grad_kernel(core_ref, own_ref, other_ref, image_ref, sums_ref, sums_got_ref, dkernel_ref, rows_ref,
                       corr_ref, line_ref):
    local, _, width = image_ref.shape
    height = 2 * own_ref.shape[0]
    count = 7 * height
    span = 16 * SLOTS
    fill_tile(rows_ref, own_ref, other_ref, core_ref[0] & 1, local)
    lane = lax.broadcasted_iota(jnp.int32, (count, span), 1) // SLOTS
    inner_slot = lax.broadcasted_iota(jnp.int32, (7, 128), 1) % SLOTS

    def body(g, carry):
        images = image_ref[pl.ds(g * 16, 16)].reshape(span, width)
        corr = jnp.zeros((count, span), F32)
        for inner in range(16):
            a = rows_ref[0, pl.ds(g * 16 + inner, height, stride=local), :]
            b = rows_ref[1, pl.ds(g * 16 + inner, height, stride=local), :]
            stack = jnp.concatenate(
                [jnp.concatenate(shift_halves(a, b, 3 - s), axis=1) for s in range(7)], axis=0)
            value = lax.dot_general(stack.astype(BF), images, NT, preferred_element_type=F32)
            corr = jnp.where(lane == inner, value, corr)
        for part in range(2):
            lanes = slice(part * 128, part * 128 + 128)
            corr_ref[part] = corr[:, lanes]
            line = corr_ref[part, pl.ds(0, 7, stride=height), :]
            for h in range(1, height):
                value = corr_ref[part, pl.ds(h, 7, stride=height), :]
                line = line + jnp.where(
                    inner_slot < SLOTS - h, pltpu.roll(value, 128 - h, 1), pltpu.roll(value, SLOTS - h, 1))
            line_ref[part, g, pl.ds(0, 7), :] = line
        return carry

    lax.fori_loop(0, local // 16, body, 0)
    slot = lax.broadcasted_iota(jnp.int32, (7, span), 1) % SLOTS
    total = jnp.zeros(dkernel_ref.shape, F32)
    for g in range(local // 16):
        lines = jnp.concatenate([line_ref[p, g, pl.ds(0, 7), :] for p in range(2)], axis=1)
        spread = [jnp.where(slot == (r - 3) % SLOTS, lines, 0.0) for r in range(7)] + [jnp.zeros((7, span), F32)]
        pick = (lax.broadcasted_iota(jnp.int32, (local, span), 0) - g * 16
                == lax.broadcasted_iota(jnp.int32, (local, span), 1) // SLOTS).astype(F32)
        total = total + lax.dot_general(
            jnp.concatenate(spread, axis=0), pick, NT, preferred_element_type=F32, precision=HI)
    dkernel_ref[...] = total * grad_scale
    sums = (sums_ref[...] + sums_got_ref[...]) * grad_scale
    dkernel_ref[pl.ds(49, 7), :] = sums[:7]


def kernel_grad(core, own, other, image16, sums, sums_got):
    local = image16.shape[0]
    height = 2 * own.shape[0]
    return pl.pallas_call(
        kernel_grad_kernel,
        out_shape=jax.ShapeDtypeStruct((56, local), F32),
        in_specs=[SMEM] + [VMEM] * 5,
        out_specs=VMEM,
        scratch_shapes=[
            pltpu.VMEM((2, height * local, 128), F32),
            pltpu.VMEM((2, 7 * height, 128), F32),
            pltpu.VMEM((2, local // 16, 8, 128), F32),
        ],
        compiler_params=grant(5),
        cost_estimate=cost(4),
        name="kernel_grad",
    )(core, own, other, image16, sums, sums_got)


def image_grad_kernel(core_ref, own_ref, other_ref, same_ref, cross_ref, ct_ref, taps_ref, out_ref, rows_ref):
    local, height, width = ct_ref.shape
    core = core_ref[0] & 1
    count = 7 * height
    fill_tile(rows_ref, own_ref, other_ref, core, local)
    for part in range(2):
        lanes = slice(part * 128, part * 128 + 128)
        for i in range(3):
            a = pl.multiple_of((height + 5 * core + i) * local, 8)
            b = pl.multiple_of((height + 5 * (1 - core) + i) * local, 8)
            rows_ref[part, pl.ds(a, local), :] = same_ref[i, :, lanes].astype(F32)
            rows_ref[part, pl.ds(b, local), :] = cross_ref[i, :, lanes].astype(F32)
        rows_ref[part, pl.ds((height + 3) * local, 2 * local), :] = jnp.zeros((2 * local, 128), F32)

    def body(g, carry):
        tiles = []
        for u in range(8):
            pair = [rows_ref[p, pl.ds(g * 8 + u, SLOTS, stride=local), :] for p in range(2)]
            tiles.append(jnp.concatenate(pair, axis=1))
        right = jnp.concatenate(tiles, axis=0).astype(BF)
        start = pl.multiple_of(g * 8 * count, 16)
        products = jnp.dot(taps_ref[pl.ds(start, 8 * count), :], right, preferred_element_type=F32)
        for u in range(8):
            ch = g * 8 + u
            left_right = shift_sum(products[u * count : (u + 1) * count], height, -1)
            out_ref[ch] = (ct_ref[ch].astype(F32) + jnp.concatenate(left_right, axis=1)).astype(BF)
        return carry

    lax.fori_loop(0, local // 8, body, 0)


def image_grad(core, own, other, same, cross, ct, taps):
    local, height, width = ct.shape
    return pl.pallas_call(
        image_grad_kernel,
        out_shape=jax.ShapeDtypeStruct((local, height, width), BF),
        in_specs=[SMEM] + [VMEM] * 6,
        out_specs=VMEM,
        scratch_shapes=[pltpu.VMEM((2, SLOTS * local, 128), F32)],
        compiler_params=grant(6),
        cost_estimate=cost(5),
        name="image_grad",
    )(core, own, other, same, cross, ct, taps)


def finish_kernel(blocks, core_ref, image_ref, vector_ref, sums_ref, sums_got_ref, *refs):
    part_refs = refs[:blocks]
    out_ref, dkernel_ref, shift_ref, gain_ref, scale_ref, bias_ref, rows_ref, col_ref = refs[blocks:]
    sums = sums_ref[...] + sums_got_ref[...]
    dkernel_ref[...] = sums[:49]
    shift_ref[...], gain_ref[...], scale_ref[...] = sums[49:50], sums[50:51], sums[51:52]
    bias_ref[...] = jnp.concatenate([sums[52 + i : 53 + i] for i in range(4)], axis=1)
    local, height, width = image_ref.shape
    half = height // 2
    core = core_ref[0] & 1
    col_ref[...] = column(vector_ref[...])
    scale = col_ref[pl.ds(vector_ref.shape[1] - 128, local), :]
    for which in range(2):
        place = core if which == 0 else 1 - core
        for i in range(half):
            rows = pl.ds(i * local, local)
            total = part_refs[which][rows, :].astype(F32)
            for k in range(which + 2, blocks, 2):
                total = total + part_refs[k][rows, :].astype(F32)
            total = total * scale
            start = pl.multiple_of((place * half + i) * local, 8)
            for part in range(2):
                rows_ref[part, pl.ds(start, local), :] = total[:, part * 128 : part * 128 + 128]

    def body(g, carry):
        for u in range(8):
            ch = g * 8 + u
            pair = [rows_ref[p, pl.ds(ch, height, stride=local), :] for p in range(2)]
            out_ref[ch] = (image_ref[ch].astype(F32) + jnp.concatenate(pair, axis=1)).astype(BF)
        return carry

    lax.fori_loop(0, local // 8, body, 0)


def finish(core, image, vector, sums, sums_got, parts):
    local, height, width = image.shape
    return pl.pallas_call(
        functools.partial(finish_kernel, len(parts)),
        out_shape=[
            jax.ShapeDtypeStruct((local, height, width), BF),
            jax.ShapeDtypeStruct((49, local), F32),
            *[jax.ShapeDtypeStruct((1, local), F32)] * 3,
            jax.ShapeDtypeStruct((1, 4 * local), F32),
        ],
        in_specs=[SMEM] + [VMEM] * (4 + len(parts)),
        out_specs=[VMEM] * 6,
        scratch_shapes=[
            pltpu.VMEM((2, height * local, 128), F32),
            pltpu.VMEM((vector.shape[1], 1), F32),
        ],
        compiler_params=grant(5),
        cost_estimate=cost(2),
        name="finish",
    )(core, image, vector, sums, sums_got, *parts)


def swap(value, axis, size, k):
    return lax.ppermute(value, axis, [(i, i ^ k) for i in range(size)])


def after(value, *gates):
    return lax.optimization_barrier((value, *gates))[0]


def sum_over_space(value, size):
    k = 1
    while 2 * k < size:
        value = value + swap(value, "space", size, k)
        k *= 2
    return value, swap(value, "space", size, k)


def scatter_over_space(ids, own, got, size):
    if size > 4:
        total = (own.astype(F32) + got.astype(F32)).astype(BF)
        return lax.psum_scatter(total, "space", scatter_dimension=1, tiled=True).astype(F32), total
    mine, *others = merge(ids, own, got, size)
    moved = [swap(p, "space", size, k + 1) for k, p in enumerate(others)]
    return mine + sum(m.astype(F32) for m in moved), mine


def per_device(image, dw_weight, ln_gain, ln_shift, w_in, b_in, w_out, layer_scale, cotangent):
    local, height, width = image.shape
    hid = w_in.shape[1]
    n_chan, n_space = lax.axis_size("chan"), lax.axis_size("space")
    ids = jnp.stack([lax.axis_index("chan"), lax.axis_index("space")]).astype(jnp.int32)

    used = 2 * local + hid + 128
    count = -(-used // width)
    packed = jnp.pad(jnp.concatenate([ln_gain, ln_shift, b_in]), (0, count * width - used))
    packed = jnp.concatenate([packed, jnp.pad(layer_scale, (0, 128 - local))])[None]
    d_mine, d_theirs = pack(ids, cotangent, packed)
    d_all = [d_mine] + [
        swap(d_theirs if k % 2 else d_mine, "chan", n_chan, k) for k in range(1, n_chan)
    ]
    pairs_a = [(s, s ^ 1) for s in range(n_space) if s ^ 1 < n_space]
    pairs_b = [(s, t) for s in range(n_space) for t in [s + 1 if s % 2 else s - 1] if 0 <= t < n_space]
    edge_a, edge_b = edges(ids, after(image, d_mine))
    got_a = lax.ppermute(edge_a, "space", pairs_a)
    got_b = lax.ppermute(edge_b, "space", pairs_b)
    dw_weight, w_in, w_out = lax.optimization_barrier((dw_weight, w_in, w_out, edge_a))[:3]
    w_inx = swap(w_in, "chan", n_chan, 1)
    w_outx = swap(w_out, "chan", n_chan, 1)
    weight = jnp.pad(dw_weight.T, ((0, 15), (0, -local % 128)))
    taps = make_taps(weight, local, height, False)
    taps, d_all = lax.optimization_barrier((taps, d_all))

    mine, theirs, image16 = conv_forward(ids, image, got_a, got_b, taps)
    conv = [mine] + [swap(theirs if k % 2 else mine, "chan", n_chan, k) for k in range(1, n_chan)]
    w_in, w_inx, w_out, w_outx, weight = lax.optimization_barrier((w_in, w_inx, w_out, w_outx, weight, mine))[:5]
    w_int, w_intx, w_outt, w_outtx = turn(w_in, w_inx, w_out, w_outx)
    taps_back = make_taps(weight, local, height, True)
    weights = [w_in, w_inx, w_int, w_intx, w_out, w_outx, w_outt, w_outtx]
    conv[0] = after(conv[0], taps_back)
    branch, dn_send, dn, stand, inv, q, dw, dw_send, small = mlp(ids, conv, d_all, count, weights)

    got = [swap(dn_send[k - 1 : k], "chan", n_chan, 2 * k) for k in range(1, n_chan // 2)]
    dw, gate = scatter_over_space(ids, dw, swap(dw_send, "chan", n_chan, 1), n_space)
    dw = dw * grad_scale
    inv = after(inv, gate)
    got_small = [swap(small[k], "chan", n_chan, k) for k in range(1, n_chan)]

    dconv, dconv_send, edge, edge_send, sums, sums_send = norm_backward(
        ids, count, dn, stand, inv, d_all[0], d_all[1], q, packed, small, got, got_small)
    same_pairs, cross_pairs = [], []
    for s in range(n_space):
        for c in range(n_chan):
            t = s + 1 if c % 2 else s - 1
            if 0 <= t < n_space:
                same_pairs.append((s * n_chan + c, t * n_chan + c))
                cross_pairs.append((s * n_chan + c, t * n_chan + (c ^ 1)))
    same = lax.ppermute(edge, ("space", "chan"), same_pairs)
    cross = lax.ppermute(edge_send, ("space", "chan"), cross_pairs)
    other = swap(dconv_send, "chan", n_chan, 1)
    sums_got = swap(sums_send, "chan", n_chan, 1)
    branch = after(branch, other)
    parts = [branch[0]] + [swap(branch[k], "chan", n_chan, k) for k in range(1, n_chan)]

    sums, sums_got = sum_over_space(kernel_grad(ids, dconv, other, image16, sums, sums_got), n_space)
    d_image = image_grad(ids, dconv, other, same, cross, cotangent, taps_back)
    output, d_kernel, d_shift, d_gain, d_scale, d_b_in = finish(ids, image, packed, sums, sums_got, parts)
    return (output, d_image, d_kernel.T, d_gain[0], d_shift[0], dw[0], d_b_in[0], dw[1].T, d_scale[0])


def solution(mesh):
    return jax.shard_map(
        per_device,
        mesh=mesh,
        in_specs=(
            P("chan", ("groups", "space"), None),
            P("chan", None),
            P("chan"),
            P("chan"),
            P(None, "chan"),
            P("chan"),
            P("chan", None),
            P("chan"),
            P("chan", ("groups", "space"), None),
        ),
        out_specs=(
            P("chan", ("groups", "space"), None),
            P("chan", ("groups", "space"), None),
            P("chan", "groups"),
            P(("groups", "chan")),
            P(("groups", "chan")),
            P("space", ("groups", "chan")),
            P(("groups", "chan")),
            P(("groups", "chan"), "space"),
            P(("groups", "chan")),
        ),
        check_vma=False,
    )
```

time: 113 us -> 94.1 us (0.83)
  waiting for transfers between devices: 41.1 us -> 16.3 us
  Pallas kernels: 25.7 us -> 40.9 us
  local copies, waits for them, and re-layouts: 10.3 us -> 1.82 us
  other arithmetic: 4.22 us -> 2.19 us
  starting transfers between devices: 29.8 us -> 31.8 us
    pallas_call x2 -> x10, Pallas kernels: 9.78 us -> 24.6 us  [the longest x1 6.55 us: kernel_grad(): pl.pallas_call(kernel_grad_kernel, out_shape=jax.ShapeDtypeStruct((56, lo...]
    ppermute x25 -> x23, waiting for transfers between devices: 30 us -> 16 us  [swap(): return lax.ppermute(value, axis, [(i, i ^ k) for i in range(size)])]
    ppermute x2, waiting for transfers between devices: 6.1 us -> 0.36 us  [the longest x1 0.36 us: per_device(): got_a = lax.ppermute(edge_a, 'space', pairs_a)]
    ppermute x1, waiting for transfers between devices: 4.97 us -> 0.01 us  [per_device(): same = lax.ppermute(edge, ('space', 'chan'), same_pairs)]
    unnamed x43 -> x12, local copies, waits for them, and re-layouts: 3.69 us -> 1.02 us
    convert_element_type x2 -> x0, other arithmetic: 2.39 us -> none  [the longest x1 1.2 us: scatter_over_space(): half = value.astype(BF)]
    ppermute x25 -> x23, starting transfers between devices: 22.5 us -> 24.3 us  [swap(): return lax.ppermute(value, axis, [(i, i ^ k) for i in range(size)])]
    concatenate x5 -> x0, local copies, waits for them, and re-layouts: 1.77 us -> none  [the longest x2 0.85 us: per_device(): jnp.concatenate([g_own, g_other])]
  transfers between devices with their start and end apart: 29 -> 27, of which waited for: 9 -> 10; matrix products, arithmetic and copies ran while one was open for 10% -> 1% of each run, Pallas kernels for 13% -> 28%
where the time goes in v2:
time: 94.1 us; the launch traced here: 93.9 us
  Pallas kernels  40.9 us (43%)
  starting transfers between devices  31.8 us (34%)
  waiting for transfers between devices  16.3 us (17%)
  other arithmetic  2.19 us (2%)
  local copies, waits for them, and re-layouts  1.82 us (2%)
    ppermute x23, starting transfers between devices, swap(): return lax.ppermute(value, axis, [(i, i ^ k) for i in range(size)])  24.3 us
    ppermute x23, waiting for transfers between devices, swap(): return lax.ppermute(value, axis, [(i, i ^ k) for i in range(size)])  16 us
    pallas_call x1, Pallas kernels, mlp(): pl.pallas_call(functools.partial(mlp_kernel, blocks), grid=(steps,), out_...  11.2 us
    pallas_call x1, Pallas kernels, kernel_grad(): pl.pallas_call(kernel_grad_kernel, out_shape=jax.ShapeDtypeStruct((56, lo...  6.55 us
    pallas_call x1, Pallas kernels, image_grad(): pl.pallas_call(image_grad_kernel, out_shape=jax.ShapeDtypeStruct((local,...  5.88 us
    pallas_call x1, Pallas kernels, conv_forward(): pl.pallas_call(conv_kernel, out_shape=[jax.ShapeDtypeStruct((rows, width)...  5.08 us
    ppermute x1, starting transfers between devices, per_device(): got_a = lax.ppermute(edge_a, 'space', pairs_a)  4.94 us
    pallas_call x2, Pallas kernels, make_taps(): pl.pallas_call(functools.partial(taps_kernel, flip, height), out_shape=ja...  4.91 us
  transfers between devices with their start and end apart: 27, of which 10 were waited for; matrix products, arithmetic and copies ran while one was open for 1% of the time, Pallas kernels for 28%

profile of v2, /device:TPU:0, one launch (start us, length us, event | category | flops | bytes accessed | tf_op | source)
XLA Modules:
  0.0 93.9 jit_solution(11139751977458180874)
XLA Ops:
  0.6 0.8 select_maximum_fusion.1
  1.4 0.7 select_maximum_fusion
  2.2 1.0 %copy-done = bf16[96,8,256]{2,1,0:T(8,128)(2,1)S(1)} copy-done((bf16[96,8,256]{2,1,0:T(8,128)(2,1)S(1)}, bf16[96,8,256]{2,1,0:T(8,128)(2,1)}, u32[]{:S(2)}) %copy-start) | copy-done | bytes 393240
  3.2 1.4 %pack.1 = (bf16[400,256]{1,0:T(8,128)(2,1)S(1)}, bf16[400,256]{1,0:T(8,128)(2,1)S(1)}) custom-call(s32[2]{0:T(128)S(1)} %pad_add_fusion.ids_ref.me_ref.core_ref, bf16[96,8,256]{2,1,0:T(8,128)(2,1)S(1)} %copy-done, f32[1,768]{1,0:T(1,128)S(1)} %broadcast_in_dim.3.vector_ref.refs_6_), custom_call_target="tpu_custom_call" | custom-call | flops 1540000000 | tf_op jit(solution)/shard_map/pack/pallas_call | solution.py:168
  4.6 2.4 %collective-permute-start.4 = (bf16[400,256]{1,0:T(8,128)(2,1)S(1)}, bf16[400,256]{1,0:T(8,128)(2,1)S(1)}, u32[]{:S(2)}, u32[]{:S(2)}) collective-permute-start(bf16[400,256]{1,0:T(8,128)(2,1)S(1)} %get-tuple-element.67), channel_id=1, source_target_pairs={{0,3},{1,2},{2,1},{3,0},{4,7},{5,6},{6,5},{7,4},{8,11},{9,10},{10,... | collective-permute-start | bytes 614408 | tf_op jit(solution)/shard_map/ppermute | solution.py:718
  7.0 0.7 collective-permute-start.2
  7.8 1.2 %edges.1 = (bf16[288,256]{1,0:T(8,128)(2,1)S(1)}, bf16[288,256]{1,0:T(8,128)(2,1)S(1)}) custom-call(s32[2]{0:T(128)S(1)} %pad_add_fusion.ids_ref.me_ref.core_ref, bf16[96,8,256]{2,1,0:T(8,128)(2,1)S(1)} %copy-done.2), custom_call_target="tpu_custom_call" | custom-call | flops 1320000000 | tf_op jit(solution)/shard_map/edges/pallas_call | solution.py:121
  9.0 0.7 collective-permute-start.1
  9.7 4.9 %collective-permute-start = (bf16[288,256]{1,0:T(8,128)(2,1)S(1)}, bf16[288,256]{1,0:T(8,128)(2,1)S(1)}, u32[]{:S(2)}, u32[]{:S(2)}) collective-permute-start(bf16[288,256]{1,0:T(8,128)(2,1)S(1)} %get-tuple-element.64), channel_id=1, source_target_pairs={{0,4},{4,0},{8,12},{12,8},{1,5},{5,1},{9,13},{13,9},{2,6},{6,2},{1... | collective-permute-start | bytes 442376 | tf_op jit(solution)/shard_map/ppermute | solution.py:759
  14.6 2.4 %taps_forward.1.taps_ref = bf16[5376,128]{1,0:T(8,128)(2,1)S(1)} custom-call(bf16[64,128]{1,0:T(8,128)(2,1)S(1)} %pad.14.weight_ref), custom_call_target="tpu_custom_call" | custom-call | flops 2640000000 | tf_op jit(solution)/shard_map/taps_forward/pallas_call | solution.py:78
  17.2 0.5 collective-permute-start.6
  17.7 0.4 collective-permute-done.got_a_ref
  18.1 5.1 %conv_forward.1 = (bf16[384,256]{1,0:T(8,128)(2,1)S(1)}, bf16[384,256]{1,0:T(8,128)(2,1)S(1)}, bf16[96,16,256]{2,1,0:T(8,128)(2,1)S(1)}) custom-call(s32[2]{0:T(128)S(1)} %pad_add_fusion.ids_ref.me_ref.core_ref, bf16[96,8,256]{2,1,0:T(8,128)(2,1)S(1)} %copy-done.2, bf16[288,256]{1,0:T(8,128)(2,1)S(1)} %collective-permute-done.got_a_ref, ...), custom_call_target="tpu_custom_call" | custom-call | flops 5500000256 | tf_op jit(solution)/shard_map/conv_forward/pallas_call | solution.py:276
  23.2 1.1 %collective-permute-start.9 = (bf16[384,256]{1,0:T(8,128)(2,1)S(1)}, bf16[384,256]{1,0:T(8,128)(2,1)S(1)}, u32[]{:S(2)}, u32[]{:S(2)}) collective-permute-start(bf16[384,256]{1,0:T(8,128)(2,1)S(1)} %get-tuple-element.74), channel_id=1, source_target_pairs={{0,3},{1,2},{2,1},{3,0},{4,7},{5,6},{6,5},{7,4},{8,11},{9,10},{10,... | collective-permute-start | bytes 589832 | tf_op jit(solution)/shard_map/ppermute | solution.py:718
  24.2 0.6 collective-permute-start.7
  24.8 0.5 collective-permute-start.8
  25.4 2.5 %taps_back.1.taps_ref = bf16[5376,128]{1,0:T(8,128)(2,1)S(1)} custom-call(bf16[64,128]{1,0:T(8,128)(2,1)S(1)} %pad.14.weight_ref), custom_call_target="tpu_custom_call" | custom-call | flops 2640000000 | tf_op jit(solution)/shard_map/taps_back/pallas_call | solution.py:78
  27.8 0.4 turn.1
  28.2 2.2 %collective-permute-done.9.refs_3_ = bf16[384,256]{1,0:T(8,128)(2,1)S(1)} collective-permute-done((bf16[384,256]{1,0:T(8,128)(2,1)S(1)}, bf16[384,256]{1,0:T(8,128)(2,1)S(1)}, u32[]{:S(2)}, u32[]{:S(2)}) %collective-permute-start.9) | collective-permute-done | bytes 196640 | tf_op jit(solution)/shard_map/ppermute | solution.py:718
  30.4 4.3 %collective-permute-done.8.refs_2_ = bf16[384,256]{1,0:T(8,128)(2,1)S(1)} collective-permute-done((bf16[384,256]{1,0:T(8,128)(2,1)S(1)}, bf16[384,256]{1,0:T(8,128)(2,1)S(1)}, u32[]{:S(2)}, u32[]{:S(2)}) %collective-permute-start.8) | collective-permute-done | bytes 196640 | tf_op jit(solution)/shard_map/ppermute | solution.py:718
  34.6 11.2 %mlp.1 = (bf16[4,384,256]{2,1,0:T(8,128)(2,1)S(1)}, bf16[1,832,256]{2,1,0:T(8,128)(2,1)S(1)}, f32[768,256]{1,0:T(8,128)S(1)}, f32[768,256]{1,0:T(8,128)S(1)}, f3...) custom-call(s32[2]{0:T(128)S(1)} %pad_add_fusion.ids_ref.me_ref.core, ...), custom_call_target="tpu_custom_call" | custom-call | flops 12099999744 | tf_op jit(solution)/shard_map/mlp/pallas_call | solution.py:439
  46.0 1.5 %collective-permute-start.11 = (bf16[1,832,256]{2,1,0:T(8,128)(2,1)S(1)}, bf16[1,832,256]{2,1,0:T(8,128)(2,1)S(1)}, u32[]{:S(2)}, u32[]{:S(2)}) collective-permute-start(bf16[1,832,256]{2,1,0:T(8,128)(2,1)S(1)} %get-tuple-element.96), channel_id=1, source_target_pairs={{0,2},{1,3},{2,0},{3,1},{4,6},{5,7},{6,4},{7,5},{8,10},{9,11},{10,... | collective-permute-start | bytes 1277960 | tf_op jit(solution)/shard_map/ppermute | solution.py:718
  47.5 0.4 collective-permute-done.10.got_ref
  47.9 0.8 merge.1
  48.7 1.8 %collective-permute-start.24 = (bf16[2,96,384]{2,1,0:T(8,128)(2,1)S(1)}, bf16[2,96,384]{2,1,0:T(8,128)(2,1)S(1)}, u32[]{:S(2)}, u32[]{:S(2)}) collective-permute-start(bf16[2,96,384]{2,1,0:T(8,128)(2,1)S(1)} %get-tuple-element.110), channel_id=1, source_target_pairs={{0,4},{4,0},{8,12},{12,8},{1,5},{5,1},{9,13},{13,9},{2,6},{6,2},{1... | collective-permute-start | bytes 442376 | tf_op jit(solution)/shard_map/ppermute | solution.py:718
  50.5 2.2 %collective-permute-start.25 = (bf16[2,96,384]{2,1,0:T(8,128)(2,1)S(1)}, bf16[2,96,384]{2,1,0:T(8,128)(2,1)S(1)}, u32[]{:S(2)}, u32[]{:S(2)}) collective-permute-start(bf16[2,96,384]{2,1,0:T(8,128)(2,1)S(1)} %get-tuple-element.111), channel_id=1, source_target_pairs={{0,8},{4,12},{8,0},{12,4},{1,9},{5,13},{9,1},{13,5},{2,10},{6,14},... | collective-permute-start | bytes 442376 | tf_op jit(solution)/shard_map/ppermute | solution.py:718
  52.8 0.4 collective-permute-start.26
  53.2 0.4 collective-permute-start.14
  53.6 4.2 %collective-permute-done.14.refs_11_ = f32[8,96]{1,0:T(8,128)S(1)} collective-permute-done((f32[8,96]{1,0:T(8,128)S(1)}, f32[8,96]{1,0:T(8,128)S(1)}, u32[]{:S(2)}, u32[]{:S(2)}) %collective-permute-start.14) | collective-permute-done | bytes 3104 | tf_op jit(solution)/shard_map/ppermute | solution.py:718
  57.8 1.5 %collective-permute-start.13 = (f32[8,96]{1,0:T(8,128)S(1)}, f32[8,96]{1,0:T(8,128)S(1)}, u32[]{:S(2)}, u32[]{:S(2)}) collective-permute-start(f32[8,96]{1,0:T(8,128)S(1)} %get-tuple-element.122), channel_id=1, source_target_pairs={{0,2},{1,3},{2,0},{3,1},{4,6},{5,7},{6,4},{7,5},{8,10},{9,11},{10,... | collective-permute-start | bytes 9224 | tf_op jit(solution)/shard_map/ppermute | solution.py:718
  59.3 2.1 %collective-permute-done.13.refs_10_ = f32[8,96]{1,0:T(8,128)S(1)} collective-permute-done((f32[8,96]{1,0:T(8,128)S(1)}, f32[8,96]{1,0:T(8,128)S(1)}, u32[]{:S(2)}, u32[]{:S(2)}) %collective-permute-start.13) | collective-permute-done | bytes 3104 | tf_op jit(solution)/shard_map/ppermute | solution.py:718
  61.4 1.2 %collective-permute-done.12.refs_9_ = f32[8,96]{1,0:T(8,128)S(1)} collective-permute-done((f32[8,96]{1,0:T(8,128)S(1)}, f32[8,96]{1,0:T(8,128)S(1)}, u32[]{:S(2)}, u32[]{:S(2)}) %collective-permute-start.12) | collective-permute-done | bytes 3104 | tf_op jit(solution)/shard_map/ppermute | solution.py:718
  62.6 1.3 %norm_backward.1 = (bf16[4,96,256]{2,1,0:T(8,128)(2,1)S(1)}, bf16[4,96,256]{2,1,0:T(8,128)(2,1)S(1)}, bf16[3,96,256]{2,1,0:T(8,128)(2,1)S(1)}, bf16[3,96,256]{2,...) custom-call(s32[2]{0:T(128)S(1)} %pad_add_fusion.ids_ref.me_ref.core_ref, ...), custom_call_target="tpu_custom_call" | custom-call | flops 1430000000 | tf_op jit(solution)/shard_map/norm_backward/pallas_call | solution.py:517
  64.0 1.3 %collective-permute-start.22 = (bf16[3,96,256]{2,1,0:T(8,128)(2,1)S(1)}, bf16[3,96,256]{2,1,0:T(8,128)(2,1)S(1)}, u32[]{:S(2)}, u32[]{:S(2)}) collective-permute-start(bf16[3,96,256]{2,1,0:T(8,128)(2,1)S(1)} %get-tuple-element.105), channel_id=1, source_target_pairs={{1,5},{3,7},{4,0},{5,9},{6,2},{7,11},{8,4},{9,13},{10,6},{11,15},{... | collective-permute-start | bytes 442376 | tf_op jit(solution)/shard_map/ppermute | solution.py:792
  65.3 0.7 collective-permute-start.23
  66.0 4.1 %collective-permute-start.15 = (bf16[4,96,256]{2,1,0:T(8,128)(2,1)S(1)}, bf16[4,96,256]{2,1,0:T(8,128)(2,1)S(1)}, u32[]{:S(2)}, u32[]{:S(2)}) collective-permute-start(bf16[4,96,256]{2,1,0:T(8,128)(2,1)S(1)} %get-tuple-element.98), channel_id=1, source_target_pairs={{0,1},{1,0},{2,3},{3,2},{4,5},{5,4},{6,7},{7,6},{8,9},{9,8},{10,11... | collective-permute-start | bytes 589832 | tf_op jit(solution)/shard_map/ppermute | solution.py:718
  70.2 0.7 slice_bitcast_fusion.4
  70.9 0.3 collective-permute-done.15.other_ref
  71.2 6.5 %kernel_grad.1 = f32[56,96]{1,0:T(8,128)S(1)} custom-call(s32[2]{0:T(128)S(1)} %pad_add_fusion.ids_ref.me_ref.core_ref, bf16[4,96,256]{2,1,0:T(8,128)(2,1)S(1)} %get-tuple-element.97.own_ref, bf16[4,96,256]{2,1,0:T(8,128)(2,1)S(1)} %collective-permute-done.15.other_ref, bf16[96,16,256]{2,1,0:T(8,128)(2,1)S(1)} %get-tuple-element.99.image_ref, ...), custom_call_target="tpu_custom_call" | custom-call | flops 4400000000 | tf_op jit(solution)/shard_map/kernel_grad/pallas_call | solution.py:600
  77.7 1.8 %collective-permute-start.17 = (f32[56,96]{1,0:T(8,128)S(1)}, f32[56,96]{1,0:T(8,128)S(1)}, u32[]{:S(2)}, u32[]{:S(2)}) collective-permute-start(f32[56,96]{1,0:T(8,128)S(1)} %kernel_grad.1), channel_id=1, source_target_pairs={{0,4},{4,0},{8,12},{12,8},{1,5},{5,1},{9,13},{13,9},{2,6},{6,2},{1... | collective-permute-start | bytes 64520 | tf_op jit(solution)/shard_map/ppermute | solution.py:718
  79.6 1.1 %collective-permute-start.21 = (bf16[384,256]{1,0:T(8,128)(2,1)S(1)}, bf16[384,256]{1,0:T(8,128)(2,1)S(1)}, u32[]{:S(2)}, u32[]{:S(2)}) collective-permute-start(bf16[384,256]{1,0:T(8,128)(2,1)S(1)} %get-tuple-element.115), channel_id=1, source_target_pairs={{0,3},{1,2},{2,1},{3,0},{4,7},{5,6},{6,5},{7,4},{8,11},{9,10},{10,... | collective-permute-start | bytes 589832 | tf_op jit(solution)/shard_map/ppermute | solution.py:718
  80.7 0.7 collective-permute-start.20
  81.4 0.3 collective-permute-done.17
  81.7 2.5 %collective-permute-start.18 = (f32[56,96]{1,0:T(8,128)S(1)}, f32[56,96]{1,0:T(8,128)S(1)}, u32[]{:S(2)}, u32[]{:S(2)}) collective-permute-start(f32[56,96]{1,0:T(8,128)S(1)} %add.18.sums_ref), channel_id=1, source_target_pairs={{0,8},{4,12},{8,0},{12,4},{1,9},{5,13},{9,1},{13,5},{2,10},{6,14},... | collective-permute-start | bytes 64520 | tf_op jit(solution)/shard_map/ppermute | solution.py:718
  84.2 5.9 %image_grad.1 = bf16[96,8,256]{2,1,0:T(8,128)(2,1)} custom-call(s32[2]{0:T(128)S(1)} %pad_add_fusion.ids_ref.me_ref.core_ref, bf16[4,96,256]{2,1,0:T(8,128)(2,1)S(1)} %get-tuple-element.97.own_ref, bf16[4,96,256]{2,1,0:T(8,128)(2,1)S(1)} %collective-permute-done.15.other_ref, bf16[3,96,256]{2,1,0:T(8,128)(2,1)S(1)} %collective-permute-done.22.same_ref, ...), custom_call_target="tpu_custom_call" | custom-call | flops 5500000256 | tf_op jit(solution)/shard_map/image_grad/pallas_call | solution.py:649
  90.1 1.0 %collective-permute-done.20.refs_2_ = bf16[384,256]{1,0:T(8,128)(2,1)S(1)} collective-permute-done((bf16[384,256]{1,0:T(8,128)(2,1)S(1)}, bf16[384,256]{1,0:T(8,128)(2,1)S(1)}, u32[]{:S(2)}, u32[]{:S(2)}) %collective-permute-start.20) | collective-permute-done | bytes 196640 | tf_op jit(solution)/shard_map/ppermute | solution.py:718
  91.1 2.2 %finish.1 = (bf16[96,8,256]{2,1,0:T(8,128)(2,1)}, f32[49,96]{1,0:T(8,128)}, f32[1,96]{1,0:T(1,128)}, f32[1,96]{1,0:T(1,128)}, f32[1,96]{1,0:T(1,128)}, /*index=5*/f32[1,384]{1,0:T(1,128)S(1)}) custom-call(s32[2]{0:T(128)S(1)} %pad_add_fusion.ids_ref.me_ref.core_ref, bf16[96,8,256]{2,1,0:T(8,128)(2,1)S(1)} %copy-done.2, ...), custom_call_target="tpu_custom_call" | custom-call | flops 2200000000 | tf_op jit(solution)/shard_map/finish/pallas_call | solution.py:697
  93.3 0.6 reduce
  (41 shorter events, 0.7 us)
Async XLA Ops:
  2.2 1.0 %copy-start = (bf16[96,8,256]{2,1,0:T(8,128)(2,1)S(1)}, bf16[96,8,256]{2,1,0:T(8,128)(2,1)}, u32[]{:S(2)}) copy-start(bf16[96,8,256]{2,1,0:T(8,128)(2,1)} %ct_ref.3) | copy-start | bytes 1179652
  3.2 4.6 %copy-start.2 = (bf16[96,8,256]{2,1,0:T(8,128)(2,1)S(1)}, bf16[96,8,256]{2,1,0:T(8,128)(2,1)}, u32[]{:S(2)}) copy-start(bf16[96,8,256]{2,1,0:T(8,128)(2,1)} %image_ref.4) | copy-start | bytes 1179652
  4.6 12.5 %collective-permute-start.4 = (bf16[400,256]{1,0:T(8,128)(2,1)S(1)}, bf16[400,256]{1,0:T(8,128)(2,1)S(1)}, u32[]{:S(2)}, u32[]{:S(2)}) collective-permute-start(bf16[400,256]{1,0:T(8,128)(2,1)S(1)} %get-tuple-element.67), channel_id=1, source_target_pairs={{0,3},{1,2},{2,1},{3,0},{4,7},{5,6},{6,5},{7,4},{8,11},{9,10},{10,... | collective-permute-start | bytes 614408 | tf_op jit(solution)/shard_map/ppermute | solution.py:718
  7.0 10.2 %collective-permute-start.2 = (bf16[400,256]{1,0:T(8,128)(2,1)S(1)}, bf16[400,256]{1,0:T(8,128)(2,1)S(1)}, u32[]{:S(2)}, u32[]{:S(2)}) collective-permute-start(bf16[400,256]{1,0:T(8,128)(2,1)S(1)} %get-tuple-element.67), channel_id=1, source_target_pairs={{0,1},{1,0},{2,3},{3,2},{4,5},{5,4},{6,7},{7,6},{8,9},{9,8},{10,11... | collective-permute-start | bytes 614408 | tf_op jit(solution)/shard_map/ppermute | solution.py:718
  7.7 6.9 %copy-start.5 = (bf16[96,49]{0,1:T(8,128)(2,1)S(1)}, bf16[96,49]{0,1:T(8,128)(2,1)}, u32[]{:S(2)}) copy-start(bf16[96,49]{0,1:T(8,128)(2,1)} %param.10) | copy-start | bytes 28228
  7.7 10.0 %collective-permute-start.3 = (bf16[400,256]{1,0:T(8,128)(2,1)S(1)}, bf16[400,256]{1,0:T(8,128)(2,1)S(1)}, u32[]{:S(2)}, u32[]{:S(2)}) collective-permute-start(bf16[400,256]{1,0:T(8,128)(2,1)S(1)} %get-tuple-element.75.refs_4_.refs_8_.refs_3_), channel_id=1, source_target_pairs={{0,2},{1,3},{2,0},{3,1},{4,6},{5,7},{6,4},{7,5},{8,10},{9,11},{10,... | collective-permute-start | bytes 614408 | tf_op jit(solution)/shard_map/ppermute | solution.py:718
  9.0 8.7 %collective-permute-start.1 = (bf16[288,256]{1,0:T(8,128)(2,1)S(1)}, bf16[288,256]{1,0:T(8,128)(2,1)S(1)}, u32[]{:S(2)}, u32[]{:S(2)}) collective-permute-start(bf16[288,256]{1,0:T(8,128)(2,1)S(1)} %get-tuple-element.65), channel_id=1, source_target_pairs={{4,8},{8,4},{5,9},{9,5},{6,10},{10,6},{7,11},{11,7},{20,24},{24,20... | collective-permute-start | bytes 442376 | tf_op jit(solution)/shard_map/ppermute | solution.py:760
  9.7 8.4 %collective-permute-start = (bf16[288,256]{1,0:T(8,128)(2,1)S(1)}, bf16[288,256]{1,0:T(8,128)(2,1)S(1)}, u32[]{:S(2)}, u32[]{:S(2)}) collective-permute-start(bf16[288,256]{1,0:T(8,128)(2,1)S(1)} %get-tuple-element.64), channel_id=1, source_target_pairs={{0,4},{4,0},{8,12},{12,8},{1,5},{5,1},{9,13},{13,9},{2,6},{6,2},{1... | collective-permute-start | bytes 442376 | tf_op jit(solution)/shard_map/ppermute | solution.py:759
  14.6 2.5 %copy-start.3 = (bf16[384,384]{1,0:T(8,128)(2,1)S(1)}, bf16[384,384]{1,0:T(8,128)(2,1)}, u32[]{:S(2)}) copy-start(bf16[384,384]{1,0:T(8,128)(2,1)} %refs_12_) | copy-start | bytes 884740
  14.6 2.6 %copy-start.4 = (bf16[384,384]{1,0:T(8,128)(2,1)S(1)}, bf16[384,384]{1,0:T(8,128)(2,1)}, u32[]{:S(2)}) copy-start(bf16[384,384]{1,0:T(8,128)(2,1)} %refs_16_) | copy-start | bytes 884740
  17.1 8.2 %collective-permute-start.5 = (bf16[384,384]{1,0:T(8,128)(2,1)S(1)}, bf16[384,384]{1,0:T(8,128)(2,1)S(1)}, u32[]{:S(2)}, u32[]{:S(2)}) collective-permute-start(bf16[384,384]{1,0:T(8,128)(2,1)S(1)} %copy-done.3), channel_id=1, source_target_pairs={{0,1},{1,0},{2,3},{3,2},{4,5},{5,4},{6,7},{7,6},{8,9},{9,8},{10,11... | collective-permute-start | bytes 884744 | tf_op jit(solution)/shard_map/ppermute | solution.py:718
  17.2 8.2 %collective-permute-start.6 = (bf16[384,384]{1,0:T(8,128)(2,1)S(1)}, bf16[384,384]{1,0:T(8,128)(2,1)S(1)}, u32[]{:S(2)}, u32[]{:S(2)}) collective-permute-start(bf16[384,384]{1,0:T(8,128)(2,1)S(1)} %copy-done.4), channel_id=1, source_target_pairs={{0,1},{1,0},{2,3},{3,2},{4,5},{5,4},{6,7},{7,6},{8,9},{9,8},{10,11... | collective-permute-start | bytes 884744 | tf_op jit(solution)/shard_map/ppermute | solution.py:718
  23.2 7.2 %collective-permute-start.9 = (bf16[384,256]{1,0:T(8,128)(2,1)S(1)}, bf16[384,256]{1,0:T(8,128)(2,1)S(1)}, u32[]{:S(2)}, u32[]{:S(2)}) collective-permute-start(bf16[384,256]{1,0:T(8,128)(2,1)S(1)} %get-tuple-element.74), channel_id=1, source_target_pairs={{0,3},{1,2},{2,1},{3,0},{4,7},{5,6},{6,5},{7,4},{8,11},{9,10},{10,... | collective-permute-start | bytes 589832 | tf_op jit(solution)/shard_map/ppermute | solution.py:718
  24.2 6.1 %collective-permute-start.7 = (bf16[384,256]{1,0:T(8,128)(2,1)S(1)}, bf16[384,256]{1,0:T(8,128)(2,1)S(1)}, u32[]{:S(2)}, u32[]{:S(2)}) collective-permute-start(bf16[384,256]{1,0:T(8,128)(2,1)S(1)} %get-tuple-element.74), channel_id=1, source_target_pairs={{0,1},{1,0},{2,3},{3,2},{4,5},{5,4},{6,7},{7,6},{8,9},{9,8},{10,11... | collective-permute-start | bytes 589832 | tf_op jit(solution)/shard_map/ppermute | solution.py:718
  24.8 9.8 %collective-permute-start.8 = (bf16[384,256]{1,0:T(8,128)(2,1)S(1)}, bf16[384,256]{1,0:T(8,128)(2,1)S(1)}, u32[]{:S(2)}, u32[]{:S(2)}) collective-permute-start(bf16[384,256]{1,0:T(8,128)(2,1)S(1)} %get-tuple-element.73.refs_0_), channel_id=1, source_target_pairs={{0,2},{1,3},{2,0},{3,1},{4,6},{5,7},{6,4},{7,5},{8,10},{9,11},{10,... | collective-permute-start | bytes 589832 | tf_op jit(solution)/shard_map/ppermute | solution.py:718
  45.9 2.1 %collective-permute-start.10 = (bf16[2,384,384]{2,1,0:T(8,128)(2,1)S(1)}, bf16[2,384,384]{2,1,0:T(8,128)(2,1)S(1)}, u32[]{:S(2)}, u32[]{:S(2)}) collective-permute-start(bf16[2,384,384]{2,1,0:T(8,128)(2,1)S(1)} %get-tuple-element.91), channel_id=1, source_target_pairs={{0,1},{1,0},{2,3},{3,2},{4,5},{5,4},{6,7},{7,6},{8,9},{9,8},{10,11... | collective-permute-start | bytes 1769480 | tf_op jit(solution)/shard_map/ppermute | solution.py:718
  46.0 16.6 %collective-permute-start.11 = (bf16[1,832,256]{2,1,0:T(8,128)(2,1)S(1)}, bf16[1,832,256]{2,1,0:T(8,128)(2,1)S(1)}, u32[]{:S(2)}, u32[]{:S(2)}) collective-permute-start(bf16[1,832,256]{2,1,0:T(8,128)(2,1)S(1)} %get-tuple-element.96), channel_id=1, source_target_pairs={{0,2},{1,3},{2,0},{3,1},{4,6},{5,7},{6,4},{7,5},{8,10},{9,11},{10,... | collective-permute-start | bytes 1277960 | tf_op jit(solution)/shard_map/ppermute | solution.py:718
  48.7 16.6 %collective-permute-start.24 = (bf16[2,96,384]{2,1,0:T(8,128)(2,1)S(1)}, bf16[2,96,384]{2,1,0:T(8,128)(2,1)S(1)}, u32[]{:S(2)}, u32[]{:S(2)}) collective-permute-start(bf16[2,96,384]{2,1,0:T(8,128)(2,1)S(1)} %get-tuple-element.110), channel_id=1, source_target_pairs={{0,4},{4,0},{8,12},{12,8},{1,5},{5,1},{9,13},{13,9},{2,6},{6,2},{1... | collective-permute-start | bytes 442376 | tf_op jit(solution)/shard_map/ppermute | solution.py:718
  50.5 15.5 %collective-permute-start.25 = (bf16[2,96,384]{2,1,0:T(8,128)(2,1)S(1)}, bf16[2,96,384]{2,1,0:T(8,128)(2,1)S(1)}, u32[]{:S(2)}, u32[]{:S(2)}) collective-permute-start(bf16[2,96,384]{2,1,0:T(8,128)(2,1)S(1)} %get-tuple-element.111), channel_id=1, source_target_pairs={{0,8},{4,12},{8,0},{12,4},{1,9},{5,13},{9,1},{13,5},{2,10},{6,14},... | collective-permute-start | bytes 442376 | tf_op jit(solution)/shard_map/ppermute | solution.py:718
  52.8 17.3 %collective-permute-start.26 = (bf16[2,96,384]{2,1,0:T(8,128)(2,1)S(1)}, bf16[2,96,384]{2,1,0:T(8,128)(2,1)S(1)}, u32[]{:S(2)}, u32[]{:S(2)}) collective-permute-start(bf16[2,96,384]{2,1,0:T(8,128)(2,1)S(1)} %get-tuple-element.112), channel_id=1, source_target_pairs={{0,12},{4,8},{8,4},{12,0},{1,13},{5,9},{9,5},{13,1},{2,14},{6,10},... | collective-permute-start | bytes 442376 | tf_op jit(solution)/shard_map/ppermute | solution.py:718
  53.2 4.6 %collective-permute-start.14 = (f32[8,96]{1,0:T(8,128)S(1)}, f32[8,96]{1,0:T(8,128)S(1)}, u32[]{:S(2)}, u32[]{:S(2)}) collective-permute-start(f32[8,96]{1,0:T(8,128)S(1)} %get-tuple-element.121), channel_id=1, source_target_pairs={{0,3},{1,2},{2,1},{3,0},{4,7},{5,6},{6,5},{7,4},{8,11},{9,10},{10,... | collective-permute-start | bytes 9224 | tf_op jit(solution)/shard_map/ppermute | solution.py:718
  57.8 3.6 %collective-permute-start.13 = (f32[8,96]{1,0:T(8,128)S(1)}, f32[8,96]{1,0:T(8,128)S(1)}, u32[]{:S(2)}, u32[]{:S(2)}) collective-permute-start(f32[8,96]{1,0:T(8,128)S(1)} %get-tuple-element.122), channel_id=1, source_target_pairs={{0,2},{1,3},{2,0},{3,1},{4,6},{5,7},{6,4},{7,5},{8,10},{9,11},{10,... | collective-permute-start | bytes 9224 | tf_op jit(solution)/shard_map/ppermute | solution.py:718
  61.4 1.2 %collective-permute-start.12 = (f32[8,96]{1,0:T(8,128)S(1)}, f32[8,96]{1,0:T(8,128)S(1)}, u32[]{:S(2)}, u32[]{:S(2)}) collective-permute-start(f32[8,96]{1,0:T(8,128)S(1)} %get-tuple-element.123), channel_id=1, source_target_pairs={{0,1},{1,0},{2,3},{3,2},{4,5},{5,4},{6,7},{7,6},{8,9},{9,8},{10,11... | collective-permute-start | bytes 9224 | tf_op jit(solution)/shard_map/ppermute | solution.py:718
  63.8 7.3 %collective-permute-start.16 = (f32[8,96]{1,0:T(8,128)S(1)}, f32[8,96]{1,0:T(8,128)S(1)}, u32[]{:S(2)}, u32[]{:S(2)}) collective-permute-start(f32[8,96]{1,0:T(8,128)S(1)} %get-tuple-element.101), channel_id=1, source_target_pairs={{0,1},{1,0},{2,3},{3,2},{4,5},{5,4},{6,7},{7,6},{8,9},{9,8},{10,11... | collective-permute-start | bytes 9224 | tf_op jit(solution)/shard_map/ppermute | solution.py:718
  64.0 17.7 %collective-permute-start.22 = (bf16[3,96,256]{2,1,0:T(8,128)(2,1)S(1)}, bf16[3,96,256]{2,1,0:T(8,128)(2,1)S(1)}, u32[]{:S(2)}, u32[]{:S(2)}) collective-permute-start(bf16[3,96,256]{2,1,0:T(8,128)(2,1)S(1)} %get-tuple-element.105), channel_id=1, source_target_pairs={{1,5},{3,7},{4,0},{5,9},{6,2},{7,11},{8,4},{9,13},{10,6},{11,15},{... | collective-permute-start | bytes 442376 | tf_op jit(solution)/shard_map/ppermute | solution.py:792
  65.3 18.9 %collective-permute-start.23 = (bf16[3,96,256]{2,1,0:T(8,128)(2,1)S(1)}, bf16[3,96,256]{2,1,0:T(8,128)(2,1)S(1)}, u32[]{:S(2)}, u32[]{:S(2)}) collective-permute-start(bf16[3,96,256]{2,1,0:T(8,128)(2,1)S(1)} %get-tuple-element.106), channel_id=1, source_target_pairs={{1,4},{3,6},{4,1},{5,8},{6,3},{7,10},{8,5},{9,12},{10,7},{11,14},{... | collective-permute-start | bytes 442376 | tf_op jit(solution)/shard_map/ppermute | solution.py:793
  66.0 5.1 %collective-permute-start.15 = (bf16[4,96,256]{2,1,0:T(8,128)(2,1)S(1)}, bf16[4,96,256]{2,1,0:T(8,128)(2,1)S(1)}, u32[]{:S(2)}, u32[]{:S(2)}) collective-permute-start(bf16[4,96,256]{2,1,0:T(8,128)(2,1)S(1)} %get-tuple-element.98), channel_id=1, source_target_pairs={{0,1},{1,0},{2,3},{3,2},{4,5},{5,4},{6,7},{7,6},{8,9},{9,8},{10,11... | collective-permute-start | bytes 589832 | tf_op jit(solution)/shard_map/ppermute | solution.py:718
  77.7 6.5 %copy-start.1 = (bf16[96,8,256]{2,1,0:T(8,128)(2,1)S(1)}, bf16[96,8,256]{2,1,0:T(8,128)(2,1)}, u32[]{:S(2)}) copy-start(bf16[96,8,256]{2,1,0:T(8,128)(2,1)} %ct_ref.3) | copy-start | bytes 1179652
  77.7 4.0 %collective-permute-start.17 = (f32[56,96]{1,0:T(8,128)S(1)}, f32[56,96]{1,0:T(8,128)S(1)}, u32[]{:S(2)}, u32[]{:S(2)}) collective-permute-start(f32[56,96]{1,0:T(8,128)S(1)} %kernel_grad.1), channel_id=1, source_target_pairs={{0,4},{4,0},{8,12},{12,8},{1,5},{5,1},{9,13},{13,9},{2,6},{6,2},{1... | collective-permute-start | bytes 64520 | tf_op jit(solution)/shard_map/ppermute | solution.py:718
  79.6 10.5 %collective-permute-start.21 = (bf16[384,256]{1,0:T(8,128)(2,1)S(1)}, bf16[384,256]{1,0:T(8,128)(2,1)S(1)}, u32[]{:S(2)}, u32[]{:S(2)}) collective-permute-start(bf16[384,256]{1,0:T(8,128)(2,1)S(1)} %get-tuple-element.115), channel_id=1, source_target_pairs={{0,3},{1,2},{2,1},{3,0},{4,7},{5,6},{6,5},{7,4},{8,11},{9,10},{10,... | collective-permute-start | bytes 589832 | tf_op jit(solution)/shard_map/ppermute | solution.py:718
  80.7 10.4 %collective-permute-start.20 = (bf16[384,256]{1,0:T(8,128)(2,1)S(1)}, bf16[384,256]{1,0:T(8,128)(2,1)S(1)}, u32[]{:S(2)}, u32[]{:S(2)}) collective-permute-start(bf16[384,256]{1,0:T(8,128)(2,1)S(1)} %get-tuple-element.116), channel_id=1, source_target_pairs={{0,2},{1,3},{2,0},{3,1},{4,6},{5,7},{6,4},{7,5},{8,10},{9,11},{10,... | collective-permute-start | bytes 589832 | tf_op jit(solution)/shard_map/ppermute | solution.py:718
  81.7 9.4 %collective-permute-start.19 = (bf16[384,256]{1,0:T(8,128)(2,1)S(1)}, bf16[384,256]{1,0:T(8,128)(2,1)S(1)}, u32[]{:S(2)}, u32[]{:S(2)}) collective-permute-start(bf16[384,256]{1,0:T(8,128)(2,1)S(1)} %get-tuple-element.117), channel_id=1, source_target_pairs={{0,1},{1,0},{2,3},{3,2},{4,5},{5,4},{6,7},{7,6},{8,9},{9,8},{10,11... | collective-permute-start | bytes 589832 | tf_op jit(solution)/shard_map/ppermute | solution.py:718
  81.7 8.4 %collective-permute-start.18 = (f32[56,96]{1,0:T(8,128)S(1)}, f32[56,96]{1,0:T(8,128)S(1)}, u32[]{:S(2)}, u32[]{:S(2)}) collective-permute-start(f32[56,96]{1,0:T(8,128)S(1)} %add.18.sums_ref), channel_id=1, source_target_pairs={{0,8},{4,12},{8,0},{12,4},{1,9},{5,13},{9,1},{13,5},{2,10},{6,14},... | collective-permute-start | bytes 64520 | tf_op jit(solution)/shard_map/ppermute | solution.py:718

commit v3 on v2

--- a/solution.py
+++ b/solution.py
@@ -70,7 +70,7 @@
             out_ref[pl.ds(start, 2 * count), :] = jnp.concatenate(pair, axis=0).astype(BF)
         return carry
 
-    lax.fori_loop(0, local // 8, body, 0)
+    lax.fori_loop(0, local // 8, body, 0, unroll=6)
 
 
 def make_taps(weight, local, height, flip):
@@ -106,7 +106,7 @@
                 rows_ref[part, pl.ds(g * 8 + u, height, stride=local), :] = tile[:, part * 128 : part * 128 + 128]
         return carry
 
-    lax.fori_loop(0, local // 8, body, 0)
+    lax.fori_loop(0, local // 8, body, 0, unroll=6)
     top, bottom = (0, (height - 3) * local)
     for part in range(2):
         lanes = slice(part * 128, part * 128 + 128)
@@ -152,7 +152,7 @@
                 rows_ref[part, pl.ds(g * 8 + u, height, stride=local), :] = tile[:, part * 128 : part * 128 + 128]
         return carry
 
-    lax.fori_loop(0, local // 8, body, 0)
+    lax.fori_loop(0, local // 8, body, 0, unroll=6)
     for i in range(height // 2):
         rows = pl.ds(i * local, local)
         mine = pl.multiple_of((core * (height // 2) + i) * local, 16)
@@ -261,7 +261,7 @@
                 acc_ref[half, pl.ds(g * 8 + u, height, stride=local), :] = pair[half]
         return carry
 
-    lax.fori_loop(0, local // 8, body, 0)
+    lax.fori_loop(0, local // 8, body, 0, unroll=6)
     for half in range(2):
         lanes = slice(half * 128, half * 128 + 128)
         mine = pl.multiple_of(core * rows, 16)
@@ -289,178 +289,172 @@
     )(ids, image, got_a, got_b, taps)
 
 
-def mlp_kernel(blocks, me_ref, *refs):
+def mlp_kernel(blocks, count, me_ref, *refs):
     conv_refs = refs[:blocks]
     ct_refs = refs[blocks : 2 * blocks]
-    vec_refs = refs[2 * blocks : 3 * blocks]
     (w_in_ref, w_inx_ref, w_int_ref, w_intx_ref, w_out_ref, w_outx_ref,
-     w_outt_ref, w_outtx_ref) = refs[3 * blocks : 3 * blocks + 8]
-    (branch_ref, dn_ref, dn_own_ref, stand_ref, inv_ref, q_ref, dw_ref, dwx_ref, small_ref, normed, centred, dbranch, acc_ref, bias_ref, col_ref) = refs[3 * blocks + 8 :]
-    step = pl.program_id(0)
+     w_outt_ref, w_outtx_ref) = refs[2 * blocks : 2 * blocks + 8]
+    (branch_ref, dn_ref, dn_own_ref, stand_ref, inv_ref, q_ref, dw_ref, dwx_ref, small_ref,
+     normed, dbranch, active, dhalf, centred, fold_ref, rounded, bias_ref, gain_ref, shift_ref,
+     b_ref) = refs[2 * blocks + 8 :]
     me = me_ref[0]
-    local = conv_refs[0].shape[0]
-    width = conv_refs[0].shape[1]
-    channels = blocks * local
+    steps, _, width = inv_ref.shape
     hid = w_in_ref.shape[1]
-
-    @pl.when(step == 0)
-    def _():
-        acc_ref[...] = jnp.zeros_like(acc_ref)
-        bias_ref[...] = jnp.zeros_like(bias_ref)
-        for j in range(blocks):
-            for r, line in enumerate(vector_of(vec_refs[j][...], col_ref.shape[1] // width)):
-                col_ref[j, pl.ds(r * width, width), :] = column(line)
+    channels = w_in_ref.shape[0]
+    local = channels // blocks
 
     def where(j):
         return pl.ds(pl.multiple_of((me ^ j) * local, 16), local)
 
-    total = jnp.zeros((1, width), F32)
+    def chip(k):
+        return pl.ds(pl.multiple_of(((me // 2) ^ k) * 2 * local, 16), 2 * local)
+
+    def wide(value):
+        return jnp.concatenate([value, value], axis=1)
+
     for j in range(blocks):
-        value = conv_refs[j][...].astype(F32)
-        centred[where(j), :] = value
-        total = total + jnp.sum(value, axis=0, keepdims=True)
-        dbranch[where(j), :] = ct_refs[j][...]
-    average = total / channels
-    value = centred[...] - average
-    variance = jnp.sum(value * value, axis=0, keepdims=True) / channels
-    inv_std = lax.rsqrt(variance + 1e-06)
-    inv_ref[0] = inv_std
-    for j in range(blocks):
-        stand = (centred[where(j), :] - average) * inv_std
-        gain, shift = col_ref[j, pl.ds(0, local), :], col_ref[j, pl.ds(local, local), :]
-        normed[where(j), :] = (stand * gain + shift).astype(BF)
-        centred[where(j), :] = stand
-    chip = pl.ds(pl.multiple_of((me // 2) * 2 * local, 16), 2 * local)
-    stand_ref[...] = centred[chip, :]
-    x = normed[...]
-    d = dbranch[...]
-    branch = jnp.zeros((channels, width), F32)
-    dnormed = jnp.zeros((channels, width), F32)
+        lines = vector_of(ct_refs[j][pl.ds(steps * local, 16), :], count)
+        cols = jnp.concatenate([column(line) for line in lines], axis=0)
+        gain_ref[where(j), :] = jnp.broadcast_to(cols[:local], (local, 128))
+        shift_ref[where(j), :] = jnp.broadcast_to(cols[local : 2 * local], (local, 128))
+        if j < 2:
+            b_ref[j] = jnp.broadcast_to(cols[2 * local : 2 * local + hid], (hid, 128))
+
+    k0, k1 = (0.7978845608028654, 0.044715)
     parts = ((w_in_ref, w_int_ref, w_out_ref, w_outt_ref),
              (w_inx_ref, w_intx_ref, w_outx_ref, w_outtx_ref))
-    k0, k1 = (0.7978845608028654, 0.044715)
-    for part, (w_in, w_int, w_out, w_outt) in enumerate(parts):
-        bias = col_ref[part, pl.ds(2 * local, hid), :]
-        pre = jnp.dot(w_int[...], x, preferred_element_type=F32) + bias
-        dact = jnp.dot(w_out[...], d, preferred_element_type=F32)
-        square = pre * pre
-        th = jnp.tanh(pre * (k0 + (k0 * k1) * square))
-        half = 0.5 * pre
-        active = (half + half * th).astype(BF)
-        slope = 0.5 + 0.5 * th + half * (1.0 - th * th) * (k0 + (3.0 * k0 * k1) * square)
-        dpre = dact * slope
-        bias_ref[part] += dpre[:, :128] + dpre[:, 128:]
-        dhalf = dpre.astype(BF)
-        branch += jnp.dot(w_outt[...], active, preferred_element_type=F32)
-        dnormed += jnp.dot(w_in[...], dhalf, preferred_element_type=F32)
-        acc_ref[2 * part] += lax.dot_general(x, dhalf, NT, preferred_element_type=F32)
-        acc_ref[2 * part + 1] += lax.dot_general(d, active, NT, preferred_element_type=F32)
-    stand = centred[...]
-    centred[...] = branch
-    for j in range(blocks):
-        branch_ref[j] = centred[where(j), :].astype(BF)
-    centred[...] = dnormed
-    first = jnp.zeros((1, width), F32)
+    for i in range(steps):
+        rows = pl.ds(i * local, local)
+        pixels = slice(i * width, i * width + width)
+        for j in range(blocks):
+            rounded[where(j), :] = conv_refs[j][rows, :]
+            dbranch[where(j), pixels] = ct_refs[j][rows, :]
+        value = rounded[...].astype(F32)
+        average = jnp.sum(value, axis=0, keepdims=True) / channels
+        value = value - average
+        variance = jnp.sum(value * value, axis=0, keepdims=True) / channels
+        inv_std = lax.rsqrt(variance + 1e-06)
+        inv_ref[i] = inv_std
+        stand = value * inv_std
+        centred[...] = stand
+        normed[:, pixels] = (stand * wide(gain_ref[...]) + wide(shift_ref[...])).astype(BF)
+        stand_ref[pl.ds(i * 2 * local, 2 * local), :] = centred[chip(0), :]
+        x = normed[:, pixels]
+        d = dbranch[:, pixels]
+        branch, dnormed = None, None
+        for part, (w_in, w_int, w_out, w_outt) in enumerate(parts):
+            pre = jnp.dot(w_int[...], x, preferred_element_type=F32) + wide(b_ref[part])
+            dact = jnp.dot(w_out[...], d, preferred_element_type=F32)
+            square = pre * pre
+            th = jnp.tanh(pre * (k0 + (k0 * k1) * square))
+            half = 0.5 * pre
+            active[part, :, pixels] = (half + half * th).astype(BF)
+            slope = 0.5 + 0.5 * th + half * (1.0 - th * th) * (k0 + (3.0 * k0 * k1) * square)
+            dpre = dact * slope
+            bias = dpre[:, :128] + dpre[:, 128:]
+            bias_ref[part] = bias if i == 0 else bias_ref[part] + bias
+            dhalf[part, :, pixels] = dpre.astype(BF)
+            b_part = jnp.dot(w_outt[...], active[part, :, pixels], preferred_element_type=F32)
+            d_part = jnp.dot(w_in[...], dhalf[part, :, pixels], preferred_element_type=F32)
+            branch = b_part if part == 0 else branch + b_part
+            dnormed = d_part if part == 0 else dnormed + d_part
+        rounded[...] = branch.astype(BF)
+        for j in range(blocks):
+            branch_ref[j, rows, :] = rounded[where(j), :]
+        scaled = dnormed * wide(gain_ref[...])
+        first = jnp.sum(scaled, axis=0, keepdims=True)
+        second = jnp.sum(scaled * centred[...], axis=0, keepdims=True)
+        centred[...] = dnormed
+        dn_own_ref[pl.ds(i * 2 * local, 2 * local), :] = centred[chip(0), :]
+        q = jnp.concatenate([first, second], axis=0)
+        q_ref[i] = q
+        high = q.astype(BF).astype(F32)
+        start = i * (2 * local + 16)
+        extra = jnp.concatenate([high, q - high, jnp.zeros((12, width), F32)], axis=0).astype(BF)
+        for k in range(1, blocks // 2):
+            dn_ref[k - 1, pl.ds(start, 2 * local), :] = centred[chip(k), :].astype(BF)
+            dn_ref[k - 1, pl.ds(start + 2 * local, 16), :] = extra
+
+    ones = jnp.ones((8, 128), F32)
+
+    def lane_sums(value):
+        return lax.dot_general(ones, value, NT, preferred_element_type=F32, precision=HI)[:1]
+
+    prod = None
+    for part, out in ((0, dw_ref), (1, dwx_ref)):
+        out[0] = lax.dot_general(normed[...], dhalf[part], NT, preferred_element_type=F32).astype(BF)
+        d_out = lax.dot_general(dbranch[...], active[part], NT, preferred_element_type=F32)
+        out[1] = d_out.astype(BF)
+        term = d_out * parts[part][3][...].astype(F32)
+        prod = term if part == 0 else prod + term
+    if hid % 128:
+        fold_ref[...] = jnp.concatenate(
+            [jnp.sum(prod, axis=1, keepdims=True), jnp.zeros((channels, 127), F32)], axis=1)
+    else:
+        fold_ref[...] = sum(prod[:, i : i + 128] for i in range(128, hid, 128)) + prod[:, :128]
+    pad = jnp.zeros((1, width - 2 * local), F32)
     for k in range(blocks // 2):
-        rows = pl.ds(pl.multiple_of(((me // 2) ^ k) * 2 * local, 16), 2 * local)
+        line = jnp.concatenate([lane_sums(fold_ref[chip(k), :]), pad], axis=1)
         if k == 0:
-            dn_own_ref[...] = centred[rows, :]
+            scale_line = line
         else:
-            dn_ref[k - 1, pl.ds(0, 2 * local), :] = centred[rows, :].astype(BF)
-    for j in range(blocks):
-        scaled = centred[where(j), :] * col_ref[j, pl.ds(0, local), :]
-        first = first + jnp.sum(scaled, axis=0, keepdims=True)
-        centred[where(j), :] = scaled
-    second = jnp.sum(centred[...] * stand, axis=0, keepdims=True)
-    q = jnp.concatenate([first, second], axis=0)
-    q_ref[0] = q
-    high = q.astype(BF)
-    low = (q - high.astype(F32)).astype(BF)
-    pad = jnp.zeros((12, width), F32)
-    extra = jnp.concatenate([high.astype(F32), low.astype(F32), pad], axis=0).astype(BF)
-    for k in range(1, blocks // 2):
-        dn_ref[k - 1, pl.ds(2 * local, 16), :] = extra
-
-    @pl.when(step == pl.num_programs(0) - 1)
-    def _():
-        ones = jnp.ones((8, 128), F32)
-        for k in range(2):
-            dw_ref[k] = acc_ref[k].astype(BF)
-            dwx_ref[k] = acc_ref[2 + k].astype(BF)
-        for j in range(blocks):
-            prod = acc_ref[1, where(j), :] * w_outt_ref[where(j), :].astype(F32)
-            prod = prod + acc_ref[3, where(j), :] * w_outtx_ref[where(j), :].astype(F32)
-            if hid % 128:
-                fold = jnp.pad(jnp.sum(prod, axis=1, keepdims=True), ((0, 0), (0, 127)))
-            else:
-                fold = sum(prod[:, i : i + 128] for i in range(128, hid, 128)) + prod[:, :128]
-            sources = [fold] + [bias_ref[j, pl.ds(r * local, local), :] for r in range(hid // local if j < 2 else 0)]
-            lines = [
-                lax.dot_general(ones, a, NT, preferred_element_type=F32, precision=HI)[:1] for a in sources
-            ]
-            lines.append(jnp.zeros((8 - len(lines), local), F32))
-            small_ref[j] = jnp.concatenate(lines, axis=0)
-
-
-def mlp(me, conv, ct, lines, weights):
+            high = line.astype(BF).astype(F32)
+            middle = (line - high).astype(BF).astype(F32)
+            q = q_ref[steps - 1]
+            q_high = q.astype(BF).astype(F32)
+            extra = [q_high, q - q_high, high, middle, line - high - middle, jnp.zeros((9, width), F32)]
+            dn_ref[k - 1, pl.ds(dn_ref.shape[1] - 16, 16), :] = jnp.concatenate(extra, axis=0).astype(BF)
+    small_ref[0] = jnp.concatenate([scale_line, jnp.zeros((7, width), F32)], axis=0)
+    for part in range(2):
+        lines = [lane_sums(bias_ref[part, pl.ds(r * local, local), :]) for r in range(hid // local)]
+        lines = jnp.concatenate(lines + [jnp.zeros((8 - len(lines), local), F32)], axis=0)
+        small_ref[1 + part] = jnp.concatenate([lines, jnp.zeros((8, width - local), F32)], axis=1)
+
+
+def mlp(me, conv, ct, count, weights):
     blocks = len(conv)
     rows, width = conv[0].shape
     channels, hid = weights[0].shape
     local = channels // blocks
     steps = rows // local
-    tile = pl.BlockSpec((local, width), lambda i: (i, 0))
-
-    def whole(a):
-        return pl.BlockSpec(a.shape, lambda i: (0,) * a.ndim)
-
-    small = [*weights]
-    last = pl.BlockSpec((16, width), lambda i: (rows // 16, 0))
     peers = max(blocks // 2 - 1, 1)
-    out_shape = [
-        jax.ShapeDtypeStruct((blocks, rows, width), BF),
-        jax.ShapeDtypeStruct((peers, steps * (2 * local + 16), width), BF),
-        jax.ShapeDtypeStruct((2 * rows, width), F32),
-        jax.ShapeDtypeStruct((2 * rows, width), F32),
-        jax.ShapeDtypeStruct((steps, 1, width), F32),
-        jax.ShapeDtypeStruct((steps, 2, width), F32),
-        *[jax.ShapeDtypeStruct((2, channels, hid), BF)] * 2,
-        jax.ShapeDtypeStruct((blocks, 8, local), F32),
-    ]
-    out_specs = [
-        pl.BlockSpec((blocks, local, width), lambda i: (0, i, 0)),
-        pl.BlockSpec((peers, 2 * local + 16, width), lambda i: (0, i, 0)),
-        pl.BlockSpec((2 * local, width), lambda i: (i, 0)),
-        pl.BlockSpec((2 * local, width), lambda i: (i, 0)),
-        pl.BlockSpec((1, 1, width), lambda i: (i, 0, 0)),
-        pl.BlockSpec((1, 2, width), lambda i: (i, 0, 0)),
-        *[pl.BlockSpec((2, channels, hid), lambda i: (0, 0, 0))] * 2,
-        pl.BlockSpec((blocks, 8, local), lambda i: (0, 0, 0)),
-    ]
-    return pl.pallas_call(
-        functools.partial(mlp_kernel, blocks),
-        grid=(steps,),
-        out_shape=out_shape,
-        in_specs=[SMEM] + [tile] * (2 * blocks) + [last] * blocks + [whole(a) for a in small],
-        out_specs=out_specs,
+    return pl.pallas_call(
+        functools.partial(mlp_kernel, blocks, count),
+        out_shape=[
+            jax.ShapeDtypeStruct((blocks, rows, width), BF),
+            jax.ShapeDtypeStruct((peers, steps * (2 * local + 16), width), BF),
+            jax.ShapeDtypeStruct((2 * rows, width), F32),
+            jax.ShapeDtypeStruct((2 * rows, width), F32),
+            jax.ShapeDtypeStruct((steps, 1, width), F32),
+            jax.ShapeDtypeStruct((steps, 2, width), F32),
+            *[jax.ShapeDtypeStruct((2, channels, hid), BF)] * 2,
+            jax.ShapeDtypeStruct((3, 8, width), F32),
+        ],
+        in_specs=[SMEM] + [VMEM] * (2 * blocks + 8),
+        out_specs=[VMEM] * 9,
         scratch_shapes=[
+            pltpu.VMEM((channels, rows // local * width), BF),
+            pltpu.VMEM((channels, rows // local * width), BF),
+            pltpu.VMEM((2, hid, rows // local * width), BF),
+            pltpu.VMEM((2, hid, rows // local * width), BF),
+            pltpu.VMEM((channels, width), F32),
+            pltpu.VMEM((channels, 128), F32),
             pltpu.VMEM((channels, width), BF),
-            pltpu.VMEM((channels, width), F32),
-            pltpu.VMEM((channels, width), BF),
-            pltpu.VMEM((4, channels, hid), F32),
             pltpu.VMEM((2, hid, 128), F32),
-            pltpu.VMEM((blocks, lines * width, 1), F32),
+            pltpu.VMEM((channels, 128), F32),
+            pltpu.VMEM((channels, 128), F32),
+            pltpu.VMEM((2, hid, 128), F32),
         ],
         compiler_params=grant(22),
-        cost_estimate=cost(11),
+        cost_estimate=cost(8),
         name="mlp",
-    )(me, *conv, *ct, *ct, *small)
+    )(me, *conv, *ct, *weights)
 
 
 def norm_kernel(peers, count, core_ref, *refs):
-    dn_ref, stand_ref, inv_ref, vec_ref, vecx_ref, q_ref, scale_ref, small_ref = refs[:8]
-    got = refs[8 : 8 + peers]
-    got_small = refs[8 + peers : 9 + 3 * peers]
-    (own_ref, send_ref, edge_own_ref, edge_send_ref, sums_ref, sums_send_ref, buf, gain_ref, fold_ref) = refs[9 + 3 * peers :]
+    dn_ref, stand_ref, inv_ref, vec_ref, vecx_ref, q_ref, small_ref = refs[:7]
+    got = refs[7 : 7 + peers]
+    (own_ref, send_ref, edge_own_ref, edge_send_ref, sums_ref, buf, gain_ref, fold_ref) = refs[7 + peers :]
     core = core_ref[0] & 1
     steps = inv_ref.shape[0]
     both = dn_ref.shape[0] // steps
@@ -490,27 +484,38 @@
         buf[i] = inv_ref[i] * (dn * gain_ref[...] - q[0:1] - stand * q[1:2])
     for i in range(steps):
         own_ref[i] = buf[i, mine, :].astype(BF)
-        send_ref[i] = buf[i, theirs, :].astype(BF)
+        send_ref[pl.ds(i * local, local), :] = buf[i, theirs, :].astype(BF)
     for i in range(3):
         edge_own_ref[i] = buf[i + core, mine, :].astype(BF)
         edge_send_ref[i] = buf[i + core, theirs, :].astype(BF)
     ones = jnp.ones((8, 128), F32)
     fold_ref[0], fold_ref[1] = shift_acc, gain_acc
-    small = small_ref[0]
-    for got_ref in got_small:
-        small = small + got_ref[...]
-    start = scale_ref.shape[1] - 128
-    lines = [small[:1] / scale_ref[:, start : start + local], small[1:5]]
-    for rows, out, rest in (
-        (mine, sums_ref, lines), (theirs, sums_send_ref, [jnp.zeros((5, local), F32)])):
+    line = small_ref[0, pl.ds(0, 1), :]
+    for p in range(peers):
+        extra = got[p][0, pl.ds(got[p].shape[1] - 16, 16), :].astype(F32)
+        line = line + (extra[4:5] + extra[5:6] + extra[6:7])
+    low, high = line[:, :local], line[:, local : 2 * local]
+    scale_mine = jnp.where(core == 0, low, high)
+    scale_theirs = jnp.where(core == 0, high, low)
+    for rows, scale, which in ((mine, scale_mine, 1), (theirs, scale_theirs, 2)):
         pair = [
             lax.dot_general(ones, fold_ref[k, rows, :], NT, preferred_element_type=F32, precision=HI)[:1]
             for k in range(2)
         ]
-        out[...] = jnp.concatenate(pair + rest + [jnp.zeros((1, local), F32)], axis=0)
-
-
-def norm_backward(core, count, dn, stand, inv, vector, vector_x, q, scale, small, got, got_small):
+        bias = small_ref[which, pl.ds(0, 4), pl.ds(0, local)]
+        sums = jnp.concatenate(pair + [scale, bias, jnp.zeros((1, local), F32)], axis=0)
+        if which == 1:
+            sums_ref[...] = sums
+        else:
+            high = sums.astype(BF).astype(F32)
+            middle = (sums - high).astype(BF).astype(F32)
+            lines = jnp.concatenate([high, middle, sums - high - middle, jnp.zeros((8, local), F32)], axis=0)
+            width = send_ref.shape[1]
+            lines = jnp.concatenate([lines, jnp.zeros((32, width - local), F32)], axis=1)
+            send_ref[pl.ds(steps * local, 32), :] = lines.astype(BF)
+
+
+def norm_backward(core, count, dn, stand, inv, vector, vector_x, q, small, got):
     steps, _, width = inv.shape
     both = dn.shape[0] // steps
     local = both // 2
@@ -518,14 +523,13 @@
         functools.partial(norm_kernel, len(got), count),
         out_shape=[
             jax.ShapeDtypeStruct((steps, local, width), BF),
-            jax.ShapeDtypeStruct((steps, local, width), BF),
+            jax.ShapeDtypeStruct((steps * local + 32, width), BF),
             jax.ShapeDtypeStruct((3, local, width), BF),
             jax.ShapeDtypeStruct((3, local, width), BF),
             jax.ShapeDtypeStruct((8, local), F32),
-            jax.ShapeDtypeStruct((8, local), F32),
         ],
-        in_specs=[SMEM] + [VMEM] * (8 + len(got) + len(got_small)),
-        out_specs=[VMEM] * 6,
+        in_specs=[SMEM] + [VMEM] * (7 + len(got)),
+        out_specs=[VMEM] * 5,
         scratch_shapes=[
             pltpu.VMEM((steps, both, width), F32),
             pltpu.VMEM((both, 1), F32),
@@ -534,7 +538,7 @@
         compiler_params=grant(5),
         cost_estimate=cost(1.3),
         name="norm_backward",
-    )(core, dn, stand, inv, vector, vector_x, q, scale, small, *got, *got_small)
+    )(core, dn, stand, inv, vector, vector_x, q, small, *got)
 
 
 def fill_tile(rows_ref, own_ref, other_ref, core, local):
@@ -545,10 +549,10 @@
             rows_ref[part, pl.ds(pl.multiple_of((core * half + i) * local, 8), local), :] = (
                 own_ref[i, :, lanes].astype(F32))
             rows_ref[part, pl.ds(pl.multiple_of(((1 - core) * half + i) * local, 8), local), :] = (
-                other_ref[i, :, lanes].astype(F32))
-
-
-def kernel_grad_kernel(core_ref, own_ref, other_ref, image_ref, sums_ref, sums_got_ref, dkernel_ref, rows_ref,
+                other_ref[pl.ds(i * local, local), lanes].astype(F32))
+
+
+def kernel_grad_kernel(core_ref, own_ref, other_ref, image_ref, vector_ref, sums_ref, dkernel_ref, rows_ref,
                        corr_ref, line_ref):
     local, _, width = image_ref.shape
     height = 2 * own_ref.shape[0]
@@ -561,13 +565,16 @@
     def body(g, carry):
         images = image_ref[pl.ds(g * 16, 16)].reshape(span, width)
         corr = jnp.zeros((count, span), F32)
-        for inner in range(16):
-            a = rows_ref[0, pl.ds(g * 16 + inner, height, stride=local), :]
-            b = rows_ref[1, pl.ds(g * 16 + inner, height, stride=local), :]
-            stack = jnp.concatenate(
-                [jnp.concatenate(shift_halves(a, b, 3 - s), axis=1) for s in range(7)], axis=0)
-            value = lax.dot_general(stack.astype(BF), images, NT, preferred_element_type=F32)
-            corr = jnp.where(lane == inner, value, corr)
+        for first in range(0, 16, 8):
+            stacks = []
+            for inner in range(first, first + 8):
+                a = rows_ref[0, pl.ds(g * 16 + inner, height, stride=local), :]
+                b = rows_ref[1, pl.ds(g * 16 + inner, height, stride=local), :]
+                stacks += [jnp.concatenate(shift_halves(a, b, 3 - s), axis=1) for s in range(7)]
+            stack = jnp.concatenate(stacks, axis=0).astype(BF)
+            value = lax.dot_general(stack, images, NT, preferred_element_type=F32)
+            for inner in range(8):
+                corr = jnp.where(lane == first + inner, value[inner * count : (inner + 1) * count], corr)
         for part in range(2):
             lanes = slice(part * 128, part * 128 + 128)
             corr_ref[part] = corr[:, lanes]
@@ -579,7 +586,7 @@
             line_ref[part, g, pl.ds(0, 7), :] = line
         return carry
 
-    lax.fori_loop(0, local // 16, body, 0)
+    lax.fori_loop(0, local // 16, body, 0, unroll=3)
     slot = lax.broadcasted_iota(jnp.int32, (7, span), 1) % SLOTS
     total = jnp.zeros(dkernel_ref.shape, F32)
     for g in range(local // 16):
@@ -590,11 +597,14 @@
         total = total + lax.dot_general(
             jnp.concatenate(spread, axis=0), pick, NT, preferred_element_type=F32, precision=HI)
     dkernel_ref[...] = total * grad_scale
-    sums = (sums_ref[...] + sums_got_ref[...]) * grad_scale
-    dkernel_ref[pl.ds(49, 7), :] = sums[:7]
-
-
-def kernel_grad(core, own, other, image16, sums, sums_got):
+    lines = other_ref[pl.ds(height // 2 * local, 32), pl.ds(0, local)].astype(F32)
+    sums = (sums_ref[...] + (lines[:8] + lines[8:16] + lines[16:24])) * grad_scale
+    start = vector_ref.shape[1] - 128
+    scale_line = sums[2:3] / vector_ref[:, start : start + local]
+    dkernel_ref[pl.ds(49, 7), :] = jnp.concatenate([sums[:2], scale_line, sums[3:7]], axis=0)
+
+
+def kernel_grad(core, own, other, image16, vector, sums):
     local = image16.shape[0]
     height = 2 * own.shape[0]
     return pl.pallas_call(
@@ -610,7 +620,7 @@
         compiler_params=grant(5),
         cost_estimate=cost(4),
         name="kernel_grad",
-    )(core, own, other, image16, sums, sums_got)
+    )(core, own, other, image16, vector, sums)
 
 
 def image_grad_kernel(core_ref, own_ref, other_ref, same_ref, cross_ref, ct_ref, taps_ref, out_ref, rows_ref):
@@ -641,7 +651,7 @@
             out_ref[ch] = (ct_ref[ch].astype(F32) + jnp.concatenate(left_right, axis=1)).astype(BF)
         return carry
 
-    lax.fori_loop(0, local // 8, body, 0)
+    lax.fori_loop(0, local // 8, body, 0, unroll=6)
 
 
 def image_grad(core, own, other, same, cross, ct, taps):
@@ -664,7 +674,10 @@
     sums = sums_ref[...] + sums_got_ref[...]
     dkernel_ref[...] = sums[:49]
     shift_ref[...], gain_ref[...], scale_ref[...] = sums[49:50], sums[50:51], sums[51:52]
-    bias_ref[...] = jnp.concatenate([sums[52 + i : 53 + i] for i in range(4)], axis=1)
+    bias = jnp.concatenate([sums[52 + i : 53 + i] for i in range(4)], axis=1)
+    lanes = bias_ref.shape[1]
+    bias_ref[...] = jnp.concatenate(
+        [bias[:, i * lanes : (i + 1) * lanes] for i in range(bias_ref.shape[0])], axis=0)
     local, height, width = image_ref.shape
     half = height // 2
     core = core_ref[0] & 1
@@ -689,7 +702,7 @@
             out_ref[ch] = (image_ref[ch].astype(F32) + jnp.concatenate(pair, axis=1)).astype(BF)
         return carry
 
-    lax.fori_loop(0, local // 8, body, 0)
+    lax.fori_loop(0, local // 8, body, 0, unroll=6)
 
 
 def finish(core, image, vector, sums, sums_got, parts):
@@ -700,7 +713,7 @@
             jax.ShapeDtypeStruct((local, height, width), BF),
             jax.ShapeDtypeStruct((49, local), F32),
             *[jax.ShapeDtypeStruct((1, local), F32)] * 3,
-            jax.ShapeDtypeStruct((1, 4 * local), F32),
+            jax.ShapeDtypeStruct((local // 32, 128) if local % 32 == 0 else (1, 4 * local), F32),
         ],
         in_specs=[SMEM] + [VMEM] * (4 + len(parts)),
         out_specs=[VMEM] * 6,
@@ -733,10 +746,9 @@
 def scatter_over_space(ids, own, got, size):
     if size > 4:
         total = (own.astype(F32) + got.astype(F32)).astype(BF)
-        return lax.psum_scatter(total, "space", scatter_dimension=1, tiled=True).astype(F32), total
+        return [lax.psum_scatter(total, "space", scatter_dimension=1, tiled=True)], total
     mine, *others = merge(ids, own, got, size)
-    moved = [swap(p, "space", size, k + 1) for k, p in enumerate(others)]
-    return mine + sum(m.astype(F32) for m in moved), mine
+    return [mine] + [swap(p, "space", size, k + 1) for k, p in enumerate(others)], mine
 
 
 def per_device(image, dw_weight, ln_gain, ln_shift, w_in, b_in, w_out, layer_scale, cotangent):
@@ -747,8 +759,8 @@
 
     used = 2 * local + hid + 128
     count = -(-used // width)
-    packed = jnp.pad(jnp.concatenate([ln_gain, ln_shift, b_in]), (0, count * width - used))
-    packed = jnp.concatenate([packed, jnp.pad(layer_scale, (0, 128 - local))])[None]
+    parts = [ln_gain, ln_shift, b_in, jnp.zeros(count * width - used, F32), layer_scale, jnp.zeros(128 - local, F32)]
+    packed = jnp.concatenate([v for v in parts if v.size])[None]
     d_mine, d_theirs = pack(ids, cotangent, packed)
     d_all = [d_mine] + [
         swap(d_theirs if k % 2 else d_mine, "chan", n_chan, k) for k in range(1, n_chan)
@@ -776,12 +788,10 @@
 
     got = [swap(dn_send[k - 1 : k], "chan", n_chan, 2 * k) for k in range(1, n_chan // 2)]
     dw, gate = scatter_over_space(ids, dw, swap(dw_send, "chan", n_chan, 1), n_space)
-    dw = dw * grad_scale
     inv = after(inv, gate)
-    got_small = [swap(small[k], "chan", n_chan, k) for k in range(1, n_chan)]
-
-    dconv, dconv_send, edge, edge_send, sums, sums_send = norm_backward(
-        ids, count, dn, stand, inv, d_all[0], d_all[1], q, packed, small, got, got_small)
+
+    dconv, dconv_send, edge, edge_send, sums = norm_backward(
+        ids, count, dn, stand, inv, d_all[0], d_all[1], q, small, got)
     same_pairs, cross_pairs = [], []
     for s in range(n_space):
         for c in range(n_chan):
@@ -792,14 +802,16 @@
     same = lax.ppermute(edge, ("space", "chan"), same_pairs)
     cross = lax.ppermute(edge_send, ("space", "chan"), cross_pairs)
     other = swap(dconv_send, "chan", n_chan, 1)
-    sums_got = swap(sums_send, "chan", n_chan, 1)
+    dw = sum(term.astype(F32) for term in dw) * grad_scale
     branch = after(branch, other)
     parts = [branch[0]] + [swap(branch[k], "chan", n_chan, k) for k in range(1, n_chan)]
 
-    sums, sums_got = sum_over_space(kernel_grad(ids, dconv, other, image16, sums, sums_got), n_space)
+    sums = kernel_grad(ids, dconv, other, image16, packed, sums)
+    sums, sums_got = sum_over_space(sums, n_space)
     d_image = image_grad(ids, dconv, other, same, cross, cotangent, taps_back)
     output, d_kernel, d_shift, d_gain, d_scale, d_b_in = finish(ids, image, packed, sums, sums_got, parts)
-    return (output, d_image, d_kernel.T, d_gain[0], d_shift[0], dw[0], d_b_in[0], dw[1].T, d_scale[0])
+    flat = [v.reshape(-1) for v in (d_gain, d_shift, d_b_in, d_scale)]
+    return (output, d_image, d_kernel.T, *flat[:2], dw[0], flat[2], dw[1].T, flat[3])
 
 
 def solution(mesh):

time: 94.1 us -> 80.7 us (0.86)
  Pallas kernels: 40.9 us -> 30.7 us
  other arithmetic: 2.19 us -> 0.15 us
  starting transfers between devices: 31.8 us -> 30.3 us
    pallas_call x1, Pallas kernels: 6.55 us -> 3.01 us  [kernel_grad(): pl.pallas_call(kernel_grad_kernel, out_shape=jax.ShapeDtypeStruct((56, lo...]
    pallas_call x1, Pallas kernels: 5.88 us -> 3.5 us  [image_grad(): pl.pallas_call(image_grad_kernel, out_shape=jax.ShapeDtypeStruct((local,...]
    pallas_call x1, Pallas kernels: 5.08 us -> 2.88 us  [conv_forward(): pl.pallas_call(conv_kernel, out_shape=[jax.ShapeDtypeStruct((rows, width)...]
    pallas_call x1, Pallas kernels: 11.2 us -> 9.48 us  [mlp(): pl.pallas_call(functools.partial(mlp_kernel, blocks, count), out_shape=[j...]
    ppermute x23 -> x19, starting transfers between devices: 24.3 us -> 22.7 us  [swap(): return lax.ppermute(value, axis, [(i, i ^ k) for i in range(size)])]
    concatenate x2 -> x0, other arithmetic: 1.44 us -> none  [the longest x1 0.78 us: per_device(): jnp.concatenate([ln_gain, ln_shift, b_in])]
    ppermute x23 -> x19, waiting for transfers between devices: 16 us -> 15.3 us  [swap(): return lax.ppermute(value, axis, [(i, i ^ k) for i in range(size)])]
  transfers between devices with their start and end apart: 27 -> 23, of which waited for: 10 -> 8; matrix products, arithmetic and copies ran while one was open for 1% -> 1% of each run, Pallas kernels for 28% -> 22%
where the time goes in v3:
time: 80.7 us; the launch traced here: 80.5 us
  Pallas kernels  30.7 us (38%)
  starting transfers between devices  30.3 us (38%)
  waiting for transfers between devices  15.8 us (20%)
  local copies, waits for them, and re-layouts  2.62 us (3%)
  between operations  0.87 us (1%)
    ppermute x19, starting transfers between devices, swap(): return lax.ppermute(value, axis, [(i, i ^ k) for i in range(size)])  22.7 us
    ppermute x19, waiting for transfers between devices, swap(): return lax.ppermute(value, axis, [(i, i ^ k) for i in range(size)])  15.3 us
    pallas_call x1, Pallas kernels, mlp(): pl.pallas_call(functools.partial(mlp_kernel, blocks, count), out_shape=[j...  9.48 us
    ppermute x1, starting transfers between devices, per_device(): got_a = lax.ppermute(edge_a, 'space', pairs_a)  4.94 us
    pallas_call x2, Pallas kernels, make_taps(): pl.pallas_call(functools.partial(taps_kernel, flip, height), out_shape=ja...  4.67 us
    pallas_call x1, Pallas kernels, image_grad(): pl.pallas_call(image_grad_kernel, out_shape=jax.ShapeDtypeStruct((local,...  3.5 us
    pallas_call x1, Pallas kernels, kernel_grad(): pl.pallas_call(kernel_grad_kernel, out_shape=jax.ShapeDtypeStruct((56, lo...  3.01 us
    pallas_call x1, Pallas kernels, conv_forward(): pl.pallas_call(conv_kernel, out_shape=[jax.ShapeDtypeStruct((rows, width)...  2.88 us
  transfers between devices with their start and end apart: 23, of which 8 were waited for; matrix products, arithmetic and copies ran while one was open for 1% of the time, Pallas kernels for 22%

profile of v3, /device:TPU:0, one launch (start us, length us, event | category | flops | bytes accessed | tf_op | source)
XLA Modules:
  0.0 80.5 jit_solution(5784804892875084374)
XLA Ops:
  0.7 0.8 concatenate.3
  1.5 0.1 pad_add_fusion.ids_ref.me_ref.core_ref
  1.5 1.0 %copy-done = bf16[96,8,256]{2,1,0:T(8,128)(2,1)S(1)} copy-done((bf16[96,8,256]{2,1,0:T(8,128)(2,1)S(1)}, bf16[96,8,256]{2,1,0:T(8,128)(2,1)}, u32[]{:S(2)}) %copy-start) | copy-done | bytes 393240
  2.5 1.4 %pack.1 = (bf16[400,256]{1,0:T(8,128)(2,1)S(1)}, bf16[400,256]{1,0:T(8,128)(2,1)S(1)}) custom-call(s32[2]{0:T(128)S(1)} %pad_add_fusion.ids_ref.me_ref.core_ref, bf16[96,8,256]{2,1,0:T(8,128)(2,1)S(1)} %copy-done, f32[1,768]{1,0:T(1,128)S(1)} %broadcast_in_dim.11.vector_ref), custom_call_target="tpu_custom_call" | custom-call | flops 1540000000 | tf_op jit(solution)/shard_map/pack/pallas_call | solution.py:168
  4.0 2.4 %collective-permute-start.4 = (bf16[400,256]{1,0:T(8,128)(2,1)S(1)}, bf16[400,256]{1,0:T(8,128)(2,1)S(1)}, u32[]{:S(2)}, u32[]{:S(2)}) collective-permute-start(bf16[400,256]{1,0:T(8,128)(2,1)S(1)} %get-tuple-element.66), channel_id=1, source_target_pairs={{0,3},{1,2},{2,1},{3,0},{4,7},{5,6},{6,5},{7,4},{8,11},{9,10},{10,... | collective-permute-start | bytes 614408 | tf_op jit(solution)/shard_map/ppermute | solution.py:731
  6.4 0.7 collective-permute-start.2
  7.1 0.1 collective-permute-start.3
  7.2 1.2 %edges.1 = (bf16[288,256]{1,0:T(8,128)(2,1)S(1)}, bf16[288,256]{1,0:T(8,128)(2,1)S(1)}) custom-call(s32[2]{0:T(128)S(1)} %pad_add_fusion.ids_ref.me_ref.core_ref, bf16[96,8,256]{2,1,0:T(8,128)(2,1)S(1)} %copy-done.2), custom_call_target="tpu_custom_call" | custom-call | flops 1320000000 | tf_op jit(solution)/shard_map/edges/pallas_call | solution.py:121
  8.4 0.7 collective-permute-start.1
  9.1 4.9 %collective-permute-start = (bf16[288,256]{1,0:T(8,128)(2,1)S(1)}, bf16[288,256]{1,0:T(8,128)(2,1)S(1)}, u32[]{:S(2)}, u32[]{:S(2)}) collective-permute-start(bf16[288,256]{1,0:T(8,128)(2,1)S(1)} %get-tuple-element.63), channel_id=1, source_target_pairs={{0,4},{4,0},{8,12},{12,8},{1,5},{5,1},{9,13},{13,9},{2,6},{6,2},{1... | collective-permute-start | bytes 442376 | tf_op jit(solution)/shard_map/ppermute | solution.py:771
  14.1 2.2 %taps_forward.1.taps_ref = bf16[5376,128]{1,0:T(8,128)(2,1)S(1)} custom-call(bf16[64,128]{1,0:T(8,128)(2,1)S(1)} %pad.4.weight_ref), custom_call_target="tpu_custom_call" | custom-call | flops 2640000000 | tf_op jit(solution)/shard_map/taps_forward/pallas_call | solution.py:78
  16.3 0.1 collective-permute-start.5
  16.4 0.5 collective-permute-start.6
  16.9 0.6 collective-permute-done.got_a_ref
  17.5 2.9 %conv_forward.1 = (bf16[384,256]{1,0:T(8,128)(2,1)S(1)}, bf16[384,256]{1,0:T(8,128)(2,1)S(1)}, bf16[96,16,256]{2,1,0:T(8,128)(2,1)S(1)}) custom-call(s32[2]{0:T(128)S(1)} %pad_add_fusion.ids_ref.me_ref.core_ref, bf16[96,8,256]{2,1,0:T(8,128)(2,1)S(1)} %copy-done.2, bf16[288,256]{1,0:T(8,128)(2,1)S(1)} %collective-permute-done.got_a_ref, ...), custom_call_target="tpu_custom_call" | custom-call | flops 5500000256 | tf_op jit(solution)/shard_map/conv_forward/pallas_call | solution.py:276
  20.4 1.1 %collective-permute-start.9 = (bf16[384,256]{1,0:T(8,128)(2,1)S(1)}, bf16[384,256]{1,0:T(8,128)(2,1)S(1)}, u32[]{:S(2)}, u32[]{:S(2)}) collective-permute-start(bf16[384,256]{1,0:T(8,128)(2,1)S(1)} %get-tuple-element.73), channel_id=1, source_target_pairs={{0,3},{1,2},{2,1},{3,0},{4,7},{5,6},{6,5},{7,4},{8,11},{9,10},{10,... | collective-permute-start | bytes 589832 | tf_op jit(solution)/shard_map/ppermute | solution.py:731
  21.4 0.6 collective-permute-start.7
  22.0 0.5 collective-permute-start.8
  22.6 2.4 %taps_back.1.taps_ref = bf16[5376,128]{1,0:T(8,128)(2,1)S(1)} custom-call(bf16[64,128]{1,0:T(8,128)(2,1)S(1)} %pad.4.weight_ref), custom_call_target="tpu_custom_call" | custom-call | flops 2640000000 | tf_op jit(solution)/shard_map/taps_back/pallas_call | solution.py:78
  25.0 0.4 turn.1
  25.4 2.2 %collective-permute-done.9.refs_3_ = bf16[384,256]{1,0:T(8,128)(2,1)S(1)} collective-permute-done((bf16[384,256]{1,0:T(8,128)(2,1)S(1)}, bf16[384,256]{1,0:T(8,128)(2,1)S(1)}, u32[]{:S(2)}, u32[]{:S(2)}) %collective-permute-start.9) | collective-permute-done | bytes 196640 | tf_op jit(solution)/shard_map/ppermute | solution.py:731
  27.6 4.3 %collective-permute-done.8.refs_2_ = bf16[384,256]{1,0:T(8,128)(2,1)S(1)} collective-permute-done((bf16[384,256]{1,0:T(8,128)(2,1)S(1)}, bf16[384,256]{1,0:T(8,128)(2,1)S(1)}, u32[]{:S(2)}, u32[]{:S(2)}) %collective-permute-start.8) | collective-permute-done | bytes 196640 | tf_op jit(solution)/shard_map/ppermute | solution.py:731
  31.8 9.5 %mlp.1 = (bf16[4,384,256]{2,1,0:T(8,128)(2,1)S(1)}, bf16[1,832,256]{2,1,0:T(8,128)(2,1)S(1)}, f32[768,256]{1,0:T(8,128)S(1)}, f32[768,256]{1,0:T(8,128)S(1)}, f3...) custom-call(s32[2]{0:T(128)S(1)} %pad_add_fusion.ids_ref.me_ref.core, ...), custom_call_target="tpu_custom_call" | custom-call | flops 8800000000 | tf_op jit(solution)/shard_map/mlp/pallas_call | solution.py:421
  41.3 0.1 collective-permute-start.10
  41.4 1.5 %collective-permute-start.11 = (bf16[1,832,256]{2,1,0:T(8,128)(2,1)S(1)}, bf16[1,832,256]{2,1,0:T(8,128)(2,1)S(1)}, u32[]{:S(2)}, u32[]{:S(2)}) collective-permute-start(bf16[1,832,256]{2,1,0:T(8,128)(2,1)S(1)} %get-tuple-element.95), channel_id=1, source_target_pairs={{0,2},{1,3},{2,0},{3,1},{4,6},{5,7},{6,4},{7,5},{8,10},{9,11},{10,... | collective-permute-start | bytes 1277960 | tf_op jit(solution)/shard_map/ppermute | solution.py:731
  42.9 0.5 collective-permute-done.10.got_ref
  43.3 0.8 merge.1
  44.1 1.8 %collective-permute-start.20 = (bf16[2,96,384]{2,1,0:T(8,128)(2,1)S(1)}, bf16[2,96,384]{2,1,0:T(8,128)(2,1)S(1)}, u32[]{:S(2)}, u32[]{:S(2)}) collective-permute-start(bf16[2,96,384]{2,1,0:T(8,128)(2,1)S(1)} %get-tuple-element.108), channel_id=1, source_target_pairs={{0,4},{4,0},{8,12},{12,8},{1,5},{5,1},{9,13},{13,9},{2,6},{6,2},{1... | collective-permute-start | bytes 442376 | tf_op jit(solution)/shard_map/ppermute | solution.py:731
  45.9 2.2 %collective-permute-start.21 = (bf16[2,96,384]{2,1,0:T(8,128)(2,1)S(1)}, bf16[2,96,384]{2,1,0:T(8,128)(2,1)S(1)}, u32[]{:S(2)}, u32[]{:S(2)}) collective-permute-start(bf16[2,96,384]{2,1,0:T(8,128)(2,1)S(1)} %get-tuple-element.109), channel_id=1, source_target_pairs={{0,8},{4,12},{8,0},{12,4},{1,9},{5,13},{9,1},{13,5},{2,10},{6,14},... | collective-permute-start | bytes 442376 | tf_op jit(solution)/shard_map/ppermute | solution.py:731
  48.2 0.4 collective-permute-start.22
  48.6 5.0 %collective-permute-done.11.refs_7_ = bf16[1,832,256]{2,1,0:T(8,128)(2,1)S(1)} collective-permute-done((bf16[1,832,256]{2,1,0:T(8,128)(2,1)S(1)}, bf16[1,832,256]{2,1,0:T(8,128)(2,1)S(1)}, u32[]{:S(2)}, u32[]{:S(2)}) %collective-permute-start.11) | collective-permute-done | bytes 426016 | tf_op jit(solution)/shard_map/ppermute | solution.py:731
  53.6 1.3 %norm_backward.1 = (bf16[4,96,256]{2,1,0:T(8,128)(2,1)S(1)}, bf16[416,256]{1,0:T(8,128)(2,1)S(1)}, bf16[3,96,256]{2,1,0:T(8,128)(2,1)S(1)}, bf16[3,96,256]{2,1,0:T(8,128)(2,1)S(1)}, f32[8,96]{1,0:T(8,128)S(1)}) custom-call(s32[2]{0:T(128)S(1)} %pad_add_fusion.ids_ref.me_ref.core_ref, f32[768,256]{1,0:T(8,128)S(1)} %get-tuple-element.86.refs_0_, ...), custom_call_target="tpu_custom_call" | custom-call | flops 1430000000 | tf_op jit(solution)/shard_map/norm_backward/pallas_call | solution.py:522
  54.8 1.3 %collective-permute-start.18 = (bf16[3,96,256]{2,1,0:T(8,128)(2,1)S(1)}, bf16[3,96,256]{2,1,0:T(8,128)(2,1)S(1)}, u32[]{:S(2)}, u32[]{:S(2)}) collective-permute-start(bf16[3,96,256]{2,1,0:T(8,128)(2,1)S(1)} %get-tuple-element.103), channel_id=1, source_target_pairs={{1,5},{3,7},{4,0},{5,9},{6,2},{7,11},{8,4},{9,13},{10,6},{11,15},{... | collective-permute-start | bytes 442376 | tf_op jit(solution)/shard_map/ppermute | solution.py:802
  56.1 0.7 collective-permute-start.19
  56.8 4.1 %collective-permute-start.12 = (bf16[416,256]{1,0:T(8,128)(2,1)S(1)}, bf16[416,256]{1,0:T(8,128)(2,1)S(1)}, u32[]{:S(2)}, u32[]{:S(2)}) collective-permute-start(bf16[416,256]{1,0:T(8,128)(2,1)S(1)} %get-tuple-element.97), channel_id=1, source_target_pairs={{0,1},{1,0},{2,3},{3,2},{4,5},{5,4},{6,7},{7,6},{8,9},{9,8},{10,11... | collective-permute-start | bytes 638984 | tf_op jit(solution)/shard_map/ppermute | solution.py:731
  60.9 0.1 add_multiply_fusion
  61.0 0.7 slice_bitcast_fusion.4
  61.7 0.3 collective-permute-done.12.other_ref
  62.0 3.0 %kernel_grad.1 = f32[56,96]{1,0:T(8,128)S(1)} custom-call(s32[2]{0:T(128)S(1)} %pad_add_fusion.ids_ref.me_ref.core_ref, bf16[4,96,256]{2,1,0:T(8,128)(2,1)S(1)} %get-tuple-element.96.own_ref, bf16[416,256]{1,0:T(8,128)(2,1)S(1)} %collective-permute-done.12.other_ref, bf16[96,16,256]{2,1,0:T(8,128)(2,1)S(1)} %get-tuple-element.98.image_ref, ...), custom_call_target="tpu_custom_call" | custom-call | flops 4400000000 | tf_op jit(solution)/shard_map/kernel_grad/pallas_call | solution.py:610
  65.0 1.8 %collective-permute-start.13 = (f32[56,96]{1,0:T(8,128)S(1)}, f32[56,96]{1,0:T(8,128)S(1)}, u32[]{:S(2)}, u32[]{:S(2)}) collective-permute-start(f32[56,96]{1,0:T(8,128)S(1)} %kernel_grad.1), channel_id=1, source_target_pairs={{0,4},{4,0},{8,12},{12,8},{1,5},{5,1},{9,13},{13,9},{2,6},{6,2},{1... | collective-permute-start | bytes 64520 | tf_op jit(solution)/shard_map/ppermute | solution.py:731
  66.8 0.1 slice_bitcast_fusion
  66.9 1.1 %collective-permute-start.17 = (bf16[384,256]{1,0:T(8,128)(2,1)S(1)}, bf16[384,256]{1,0:T(8,128)(2,1)S(1)}, u32[]{:S(2)}, u32[]{:S(2)}) collective-permute-start(bf16[384,256]{1,0:T(8,128)(2,1)S(1)} %get-tuple-element.113), channel_id=1, source_target_pairs={{0,3},{1,2},{2,1},{3,0},{4,7},{5,6},{6,5},{7,4},{8,11},{9,10},{10,... | collective-permute-start | bytes 589832 | tf_op jit(solution)/shard_map/ppermute | solution.py:731
  68.0 0.7 collective-permute-start.16
  68.7 0.3 collective-permute-done.13
  69.0 3.1 %collective-permute-start.14 = (f32[56,96]{1,0:T(8,128)S(1)}, f32[56,96]{1,0:T(8,128)S(1)}, u32[]{:S(2)}, u32[]{:S(2)}) collective-permute-start(f32[56,96]{1,0:T(8,128)S(1)} %add.14.sums_ref), channel_id=1, source_target_pairs={{0,8},{4,12},{8,0},{12,4},{1,9},{5,13},{9,1},{13,5},{2,10},{6,14},... | collective-permute-start | bytes 64520 | tf_op jit(solution)/shard_map/ppermute | solution.py:731
  72.1 3.5 %image_grad.1 = bf16[96,8,256]{2,1,0:T(8,128)(2,1)} custom-call(s32[2]{0:T(128)S(1)} %pad_add_fusion.ids_ref.me_ref.core_ref, bf16[4,96,256]{2,1,0:T(8,128)(2,1)S(1)} %get-tuple-element.96.own_ref, bf16[416,256]{1,0:T(8,128)(2,1)S(1)} %collective-permute-done.12.other_ref, bf16[3,96,256]{2,1,0:T(8,128)(2,1)S(1)} %collective-permute-done.18.same_ref, ...), custom_call_target="tpu_custom_call" | custom-call | flops 5500000256 | tf_op jit(solution)/shard_map/image_grad/pallas_call | solution.py:659
  75.6 2.7 %collective-permute-done.16.refs_2_ = bf16[384,256]{1,0:T(8,128)(2,1)S(1)} collective-permute-done((bf16[384,256]{1,0:T(8,128)(2,1)S(1)}, bf16[384,256]{1,0:T(8,128)(2,1)S(1)}, u32[]{:S(2)}, u32[]{:S(2)}) %collective-permute-start.16) | collective-permute-done | bytes 196640 | tf_op jit(solution)/shard_map/ppermute | solution.py:731
  78.4 2.1 %finish.1 = (bf16[96,8,256]{2,1,0:T(8,128)(2,1)}, f32[49,96]{1,0:T(8,128)}, f32[1,96]{1,0:T(1,128)}, f32[1,96]{1,0:T(1,128)}, f32[1,96]{1,0:T(1,128)}, /*index=5*/f32[3,128]{1,0:T(4,128)}) custom-call(s32[2]{0:T(128)S(1)} %pad_add_fusion.ids_ref.me_ref.core_ref, bf16[96,8,256]{2,1,0:T(8,128)(2,1)S(1)} %copy-done.2, ...), custom_call_target="tpu_custom_call" | custom-call | flops 2200000000 | tf_op jit(solution)/shard_map/finish/pallas_call | solution.py:710
  (32 shorter events, 0.1 us)
Async XLA Ops:
  1.5 1.0 %copy-start = (bf16[96,8,256]{2,1,0:T(8,128)(2,1)S(1)}, bf16[96,8,256]{2,1,0:T(8,128)(2,1)}, u32[]{:S(2)}) copy-start(bf16[96,8,256]{2,1,0:T(8,128)(2,1)} %ct_ref.3) | copy-start | bytes 1179652
  2.5 4.6 %copy-start.2 = (bf16[96,8,256]{2,1,0:T(8,128)(2,1)S(1)}, bf16[96,8,256]{2,1,0:T(8,128)(2,1)}, u32[]{:S(2)}) copy-start(bf16[96,8,256]{2,1,0:T(8,128)(2,1)} %image_ref.4) | copy-start | bytes 1179652
  4.0 12.3 %collective-permute-start.4 = (bf16[400,256]{1,0:T(8,128)(2,1)S(1)}, bf16[400,256]{1,0:T(8,128)(2,1)S(1)}, u32[]{:S(2)}, u32[]{:S(2)}) collective-permute-start(bf16[400,256]{1,0:T(8,128)(2,1)S(1)} %get-tuple-element.66), channel_id=1, source_target_pairs={{0,3},{1,2},{2,1},{3,0},{4,7},{5,6},{6,5},{7,4},{8,11},{9,10},{10,... | collective-permute-start | bytes 614408 | tf_op jit(solution)/shard_map/ppermute | solution.py:731
  6.4 10.0 %collective-permute-start.2 = (bf16[400,256]{1,0:T(8,128)(2,1)S(1)}, bf16[400,256]{1,0:T(8,128)(2,1)S(1)}, u32[]{:S(2)}, u32[]{:S(2)}) collective-permute-start(bf16[400,256]{1,0:T(8,128)(2,1)S(1)} %get-tuple-element.66), channel_id=1, source_target_pairs={{0,1},{1,0},{2,3},{3,2},{4,5},{5,4},{6,7},{7,6},{8,9},{9,8},{10,11... | collective-permute-start | bytes 614408 | tf_op jit(solution)/shard_map/ppermute | solution.py:731
  7.1 6.9 %copy-start.5 = (bf16[96,49]{0,1:T(8,128)(2,1)S(1)}, bf16[96,49]{0,1:T(8,128)(2,1)}, u32[]{:S(2)}) copy-start(bf16[96,49]{0,1:T(8,128)(2,1)} %param.10) | copy-start | bytes 28228
  7.1 9.8 %collective-permute-start.3 = (bf16[400,256]{1,0:T(8,128)(2,1)S(1)}, bf16[400,256]{1,0:T(8,128)(2,1)S(1)}, u32[]{:S(2)}, u32[]{:S(2)}) collective-permute-start(bf16[400,256]{1,0:T(8,128)(2,1)S(1)} %get-tuple-element.74.refs_4_.refs_3_), channel_id=1, source_target_pairs={{0,2},{1,3},{2,0},{3,1},{4,6},{5,7},{6,4},{7,5},{8,10},{9,11},{10,... | collective-permute-start | bytes 614408 | tf_op jit(solution)/shard_map/ppermute | solution.py:731
  8.4 8.5 %collective-permute-start.1 = (bf16[288,256]{1,0:T(8,128)(2,1)S(1)}, bf16[288,256]{1,0:T(8,128)(2,1)S(1)}, u32[]{:S(2)}, u32[]{:S(2)}) collective-permute-start(bf16[288,256]{1,0:T(8,128)(2,1)S(1)} %get-tuple-element.64), channel_id=1, source_target_pairs={{4,8},{8,4},{5,9},{9,5},{6,10},{10,6},{7,11},{11,7},{20,24},{24,20... | collective-permute-start | bytes 442376 | tf_op jit(solution)/shard_map/ppermute | solution.py:772
  9.1 8.4 %collective-permute-start = (bf16[288,256]{1,0:T(8,128)(2,1)S(1)}, bf16[288,256]{1,0:T(8,128)(2,1)S(1)}, u32[]{:S(2)}, u32[]{:S(2)}) collective-permute-start(bf16[288,256]{1,0:T(8,128)(2,1)S(1)} %get-tuple-element.63), channel_id=1, source_target_pairs={{0,4},{4,0},{8,12},{12,8},{1,5},{5,1},{9,13},{13,9},{2,6},{6,2},{1... | collective-permute-start | bytes 442376 | tf_op jit(solution)/shard_map/ppermute | solution.py:771
  14.0 2.3 %copy-start.3 = (bf16[384,384]{1,0:T(8,128)(2,1)S(1)}, bf16[384,384]{1,0:T(8,128)(2,1)}, u32[]{:S(2)}) copy-start(bf16[384,384]{1,0:T(8,128)(2,1)} %refs_8_) | copy-start | bytes 884740
  14.0 2.4 %copy-start.4 = (bf16[384,384]{1,0:T(8,128)(2,1)S(1)}, bf16[384,384]{1,0:T(8,128)(2,1)}, u32[]{:S(2)}) copy-start(bf16[384,384]{1,0:T(8,128)(2,1)} %refs_12_) | copy-start | bytes 884740
  16.3 6.2 %collective-permute-start.5 = (bf16[384,384]{1,0:T(8,128)(2,1)S(1)}, bf16[384,384]{1,0:T(8,128)(2,1)S(1)}, u32[]{:S(2)}, u32[]{:S(2)}) collective-permute-start(bf16[384,384]{1,0:T(8,128)(2,1)S(1)} %copy-done.3), channel_id=1, source_target_pairs={{0,1},{1,0},{2,3},{3,2},{4,5},{5,4},{6,7},{7,6},{8,9},{9,8},{10,11... | collective-permute-start | bytes 884744 | tf_op jit(solution)/shard_map/ppermute | solution.py:731
  16.4 6.1 %collective-permute-start.6 = (bf16[384,384]{1,0:T(8,128)(2,1)S(1)}, bf16[384,384]{1,0:T(8,128)(2,1)S(1)}, u32[]{:S(2)}, u32[]{:S(2)}) collective-permute-start(bf16[384,384]{1,0:T(8,128)(2,1)S(1)} %copy-done.4), channel_id=1, source_target_pairs={{0,1},{1,0},{2,3},{3,2},{4,5},{5,4},{6,7},{7,6},{8,9},{9,8},{10,11... | collective-permute-start | bytes 884744 | tf_op jit(solution)/shard_map/ppermute | solution.py:731
  20.4 7.2 %collective-permute-start.9 = (bf16[384,256]{1,0:T(8,128)(2,1)S(1)}, bf16[384,256]{1,0:T(8,128)(2,1)S(1)}, u32[]{:S(2)}, u32[]{:S(2)}) collective-permute-start(bf16[384,256]{1,0:T(8,128)(2,1)S(1)} %get-tuple-element.73), channel_id=1, source_target_pairs={{0,3},{1,2},{2,1},{3,0},{4,7},{5,6},{6,5},{7,4},{8,11},{9,10},{10,... | collective-permute-start | bytes 589832 | tf_op jit(solution)/shard_map/ppermute | solution.py:731
  21.4 6.2 %collective-permute-start.7 = (bf16[384,256]{1,0:T(8,128)(2,1)S(1)}, bf16[384,256]{1,0:T(8,128)(2,1)S(1)}, u32[]{:S(2)}, u32[]{:S(2)}) collective-permute-start(bf16[384,256]{1,0:T(8,128)(2,1)S(1)} %get-tuple-element.73), channel_id=1, source_target_pairs={{0,1},{1,0},{2,3},{3,2},{4,5},{5,4},{6,7},{7,6},{8,9},{9,8},{10,11... | collective-permute-start | bytes 589832 | tf_op jit(solution)/shard_map/ppermute | solution.py:731
  22.0 9.8 %collective-permute-start.8 = (bf16[384,256]{1,0:T(8,128)(2,1)S(1)}, bf16[384,256]{1,0:T(8,128)(2,1)S(1)}, u32[]{:S(2)}, u32[]{:S(2)}) collective-permute-start(bf16[384,256]{1,0:T(8,128)(2,1)S(1)} %get-tuple-element.72.refs_0_), channel_id=1, source_target_pairs={{0,2},{1,3},{2,0},{3,1},{4,6},{5,7},{6,4},{7,5},{8,10},{9,11},{10,... | collective-permute-start | bytes 589832 | tf_op jit(solution)/shard_map/ppermute | solution.py:731
  41.3 2.0 %collective-permute-start.10 = (bf16[2,384,384]{2,1,0:T(8,128)(2,1)S(1)}, bf16[2,384,384]{2,1,0:T(8,128)(2,1)S(1)}, u32[]{:S(2)}, u32[]{:S(2)}) collective-permute-start(bf16[2,384,384]{2,1,0:T(8,128)(2,1)S(1)} %get-tuple-element.90), channel_id=1, source_target_pairs={{0,1},{1,0},{2,3},{3,2},{4,5},{5,4},{6,7},{7,6},{8,9},{9,8},{10,11... | collective-permute-start | bytes 1769480 | tf_op jit(solution)/shard_map/ppermute | solution.py:731
  41.4 12.2 %collective-permute-start.11 = (bf16[1,832,256]{2,1,0:T(8,128)(2,1)S(1)}, bf16[1,832,256]{2,1,0:T(8,128)(2,1)S(1)}, u32[]{:S(2)}, u32[]{:S(2)}) collective-permute-start(bf16[1,832,256]{2,1,0:T(8,128)(2,1)S(1)} %get-tuple-element.95), channel_id=1, source_target_pairs={{0,2},{1,3},{2,0},{3,1},{4,6},{5,7},{6,4},{7,5},{8,10},{9,11},{10,... | collective-permute-start | bytes 1277960 | tf_op jit(solution)/shard_map/ppermute | solution.py:731
  44.1 12.7 %collective-permute-start.20 = (bf16[2,96,384]{2,1,0:T(8,128)(2,1)S(1)}, bf16[2,96,384]{2,1,0:T(8,128)(2,1)S(1)}, u32[]{:S(2)}, u32[]{:S(2)}) collective-permute-start(bf16[2,96,384]{2,1,0:T(8,128)(2,1)S(1)} %get-tuple-element.108), channel_id=1, source_target_pairs={{0,4},{4,0},{8,12},{12,8},{1,5},{5,1},{9,13},{13,9},{2,6},{6,2},{1... | collective-permute-start | bytes 442376 | tf_op jit(solution)/shard_map/ppermute | solution.py:731
  45.9 15.0 %collective-permute-start.21 = (bf16[2,96,384]{2,1,0:T(8,128)(2,1)S(1)}, bf16[2,96,384]{2,1,0:T(8,128)(2,1)S(1)}, u32[]{:S(2)}, u32[]{:S(2)}) collective-permute-start(bf16[2,96,384]{2,1,0:T(8,128)(2,1)S(1)} %get-tuple-element.109), channel_id=1, source_target_pairs={{0,8},{4,12},{8,0},{12,4},{1,9},{5,13},{9,1},{13,5},{2,10},{6,14},... | collective-permute-start | bytes 442376 | tf_op jit(solution)/shard_map/ppermute | solution.py:731
  48.2 12.7 %collective-permute-start.22 = (bf16[2,96,384]{2,1,0:T(8,128)(2,1)S(1)}, bf16[2,96,384]{2,1,0:T(8,128)(2,1)S(1)}, u32[]{:S(2)}, u32[]{:S(2)}) collective-permute-start(bf16[2,96,384]{2,1,0:T(8,128)(2,1)S(1)} %get-tuple-element.110), channel_id=1, source_target_pairs={{0,12},{4,8},{8,4},{12,0},{1,13},{5,9},{9,5},{13,1},{2,14},{6,10},... | collective-permute-start | bytes 442376 | tf_op jit(solution)/shard_map/ppermute | solution.py:731
  54.8 14.1 %collective-permute-start.18 = (bf16[3,96,256]{2,1,0:T(8,128)(2,1)S(1)}, bf16[3,96,256]{2,1,0:T(8,128)(2,1)S(1)}, u32[]{:S(2)}, u32[]{:S(2)}) collective-permute-start(bf16[3,96,256]{2,1,0:T(8,128)(2,1)S(1)} %get-tuple-element.103), channel_id=1, source_target_pairs={{1,5},{3,7},{4,0},{5,9},{6,2},{7,11},{8,4},{9,13},{10,6},{11,15},{... | collective-permute-start | bytes 442376 | tf_op jit(solution)/shard_map/ppermute | solution.py:802
  56.1 16.0 %collective-permute-start.19 = (bf16[3,96,256]{2,1,0:T(8,128)(2,1)S(1)}, bf16[3,96,256]{2,1,0:T(8,128)(2,1)S(1)}, u32[]{:S(2)}, u32[]{:S(2)}) collective-permute-start(bf16[3,96,256]{2,1,0:T(8,128)(2,1)S(1)} %get-tuple-element.104), channel_id=1, source_target_pairs={{1,4},{3,6},{4,1},{5,8},{6,3},{7,10},{8,5},{9,12},{10,7},{11,14},{... | collective-permute-start | bytes 442376 | tf_op jit(solution)/shard_map/ppermute | solution.py:803
  56.8 5.2 %collective-permute-start.12 = (bf16[416,256]{1,0:T(8,128)(2,1)S(1)}, bf16[416,256]{1,0:T(8,128)(2,1)S(1)}, u32[]{:S(2)}, u32[]{:S(2)}) collective-permute-start(bf16[416,256]{1,0:T(8,128)(2,1)S(1)} %get-tuple-element.97), channel_id=1, source_target_pairs={{0,1},{1,0},{2,3},{3,2},{4,5},{5,4},{6,7},{7,6},{8,9},{9,8},{10,11... | collective-permute-start | bytes 638984 | tf_op jit(solution)/shard_map/ppermute | solution.py:731
  65.0 7.1 %copy-start.1 = (bf16[96,8,256]{2,1,0:T(8,128)(2,1)S(1)}, bf16[96,8,256]{2,1,0:T(8,128)(2,1)}, u32[]{:S(2)}) copy-start(bf16[96,8,256]{2,1,0:T(8,128)(2,1)} %ct_ref.3) | copy-start | bytes 1179652
  65.0 4.0 %collective-permute-start.13 = (f32[56,96]{1,0:T(8,128)S(1)}, f32[56,96]{1,0:T(8,128)S(1)}, u32[]{:S(2)}, u32[]{:S(2)}) collective-permute-start(f32[56,96]{1,0:T(8,128)S(1)} %kernel_grad.1), channel_id=1, source_target_pairs={{0,4},{4,0},{8,12},{12,8},{1,5},{5,1},{9,13},{13,9},{2,6},{6,2},{1... | collective-permute-start | bytes 64520 | tf_op jit(solution)/shard_map/ppermute | solution.py:731
  66.9 8.7 %collective-permute-start.17 = (bf16[384,256]{1,0:T(8,128)(2,1)S(1)}, bf16[384,256]{1,0:T(8,128)(2,1)S(1)}, u32[]{:S(2)}, u32[]{:S(2)}) collective-permute-start(bf16[384,256]{1,0:T(8,128)(2,1)S(1)} %get-tuple-element.113), channel_id=1, source_target_pairs={{0,3},{1,2},{2,1},{3,0},{4,7},{5,6},{6,5},{7,4},{8,11},{9,10},{10,... | collective-permute-start | bytes 589832 | tf_op jit(solution)/shard_map/ppermute | solution.py:731
  68.0 10.4 %collective-permute-start.16 = (bf16[384,256]{1,0:T(8,128)(2,1)S(1)}, bf16[384,256]{1,0:T(8,128)(2,1)S(1)}, u32[]{:S(2)}, u32[]{:S(2)}) collective-permute-start(bf16[384,256]{1,0:T(8,128)(2,1)S(1)} %get-tuple-element.114), channel_id=1, source_target_pairs={{0,2},{1,3},{2,0},{3,1},{4,6},{5,7},{6,4},{7,5},{8,10},{9,11},{10,... | collective-permute-start | bytes 589832 | tf_op jit(solution)/shard_map/ppermute | solution.py:731
  69.0 9.4 %collective-permute-start.15 = (bf16[384,256]{1,0:T(8,128)(2,1)S(1)}, bf16[384,256]{1,0:T(8,128)(2,1)S(1)}, u32[]{:S(2)}, u32[]{:S(2)}) collective-permute-start(bf16[384,256]{1,0:T(8,128)(2,1)S(1)} %get-tuple-element.115), channel_id=1, source_target_pairs={{0,1},{1,0},{2,3},{3,2},{4,5},{5,4},{6,7},{7,6},{8,9},{9,8},{10,11... | collective-permute-start | bytes 589832 | tf_op jit(solution)/shard_map/ppermute | solution.py:731
  69.0 6.6 %collective-permute-start.14 = (f32[56,96]{1,0:T(8,128)S(1)}, f32[56,96]{1,0:T(8,128)S(1)}, u32[]{:S(2)}, u32[]{:S(2)}) collective-permute-start(f32[56,96]{1,0:T(8,128)S(1)} %add.14.sums_ref), channel_id=1, source_target_pairs={{0,8},{4,12},{8,0},{12,4},{1,9},{5,13},{9,1},{13,5},{2,10},{6,14},... | collective-permute-start | bytes 64520 | tf_op jit(solution)/shard_map/ppermute | solution.py:731

commit v4 on v3

--- a/solution.py
+++ b/solution.py
@@ -406,7 +406,8 @@
             dn_ref[k - 1, pl.ds(dn_ref.shape[1] - 16, 16), :] = jnp.concatenate(extra, axis=0).astype(BF)
     small_ref[0] = jnp.concatenate([scale_line, jnp.zeros((7, width), F32)], axis=0)
     for part in range(2):
-        lines = [lane_sums(bias_ref[part, pl.ds(r * local, local), :]) for r in range(hid // local)]
+        line = lane_sums(bias_ref[part])
+        lines = [line[:, r * local : (r + 1) * local] for r in range(hid // local)]
         lines = jnp.concatenate(lines + [jnp.zeros((8 - len(lines), local), F32)], axis=0)
         small_ref[1 + part] = jnp.concatenate([lines, jnp.zeros((8, width - local), F32)], axis=1)
 
@@ -668,16 +669,9 @@
     )(core, own, other, same, cross, ct, taps)
 
 
-def finish_kernel(blocks, core_ref, image_ref, vector_ref, sums_ref, sums_got_ref, *refs):
+def finish_kernel(blocks, core_ref, image_ref, vector_ref, *refs):
     part_refs = refs[:blocks]
-    out_ref, dkernel_ref, shift_ref, gain_ref, scale_ref, bias_ref, rows_ref, col_ref = refs[blocks:]
-    sums = sums_ref[...] + sums_got_ref[...]
-    dkernel_ref[...] = sums[:49]
-    shift_ref[...], gain_ref[...], scale_ref[...] = sums[49:50], sums[50:51], sums[51:52]
-    bias = jnp.concatenate([sums[52 + i : 53 + i] for i in range(4)], axis=1)
-    lanes = bias_ref.shape[1]
-    bias_ref[...] = jnp.concatenate(
-        [bias[:, i * lanes : (i + 1) * lanes] for i in range(bias_ref.shape[0])], axis=0)
+    out_ref, rows_ref, col_ref = refs[blocks:]
     local, height, width = image_ref.shape
     half = height // 2
     core = core_ref[0] & 1
@@ -705,18 +699,13 @@
     lax.fori_loop(0, local // 8, body, 0, unroll=6)
 
 
-def finish(core, image, vector, sums, sums_got, parts):
+def finish(core, image, vector, parts):
     local, height, width = image.shape
     return pl.pallas_call(
         functools.partial(finish_kernel, len(parts)),
-        out_shape=[
-            jax.ShapeDtypeStruct((local, height, width), BF),
-            jax.ShapeDtypeStruct((49, local), F32),
-            *[jax.ShapeDtypeStruct((1, local), F32)] * 3,
-            jax.ShapeDtypeStruct((local // 32, 128) if local % 32 == 0 else (1, 4 * local), F32),
-        ],
-        in_specs=[SMEM] + [VMEM] * (4 + len(parts)),
-        out_specs=[VMEM] * 6,
+        out_shape=jax.ShapeDtypeStruct((local, height, width), BF),
+        in_specs=[SMEM] + [VMEM] * (2 + len(parts)),
+        out_specs=VMEM,
         scratch_shapes=[
             pltpu.VMEM((2, height * local, 128), F32),
             pltpu.VMEM((vector.shape[1], 1), F32),
@@ -724,7 +713,34 @@
         compiler_params=grant(5),
         cost_estimate=cost(2),
         name="finish",
-    )(core, image, vector, sums, sums_got, *parts)
+    )(core, image, vector, *parts)
+
+
+def totals_kernel(sums_ref, sums_got_ref, dkernel_ref, shift_ref, gain_ref, scale_ref, bias_ref):
+    sums = sums_ref[...] + sums_got_ref[...]
+    dkernel_ref[...] = sums[:49]
+    shift_ref[...], gain_ref[...], scale_ref[...] = sums[49:50], sums[50:51], sums[51:52]
+    bias = jnp.concatenate([sums[52 + i : 53 + i] for i in range(4)], axis=1)
+    lanes = bias_ref.shape[1]
+    bias_ref[...] = jnp.concatenate(
+        [bias[:, i * lanes : (i + 1) * lanes] for i in range(bias_ref.shape[0])], axis=0)
+
+
+def totals(sums, sums_got):
+    local = sums.shape[1]
+    return pl.pallas_call(
+        totals_kernel,
+        out_shape=[
+            jax.ShapeDtypeStruct((49, local), F32),
+            *[jax.ShapeDtypeStruct((1, local), F32)] * 3,
+            jax.ShapeDtypeStruct((local // 32, 128) if local % 32 == 0 else (1, 4 * local), F32),
+        ],
+        in_specs=[VMEM, VMEM],
+        out_specs=[VMEM] * 5,
+        compiler_params=grant(2),
+        cost_estimate=cost(0.4),
+        name="totals",
+    )(sums, sums_got)
 
 
 def swap(value, axis, size, k):
@@ -740,7 +756,7 @@
     while 2 * k < size:
         value = value + swap(value, "space", size, k)
         k *= 2
-    return value, swap(value, "space", size, k)
+    return value, k
 
 
 def scatter_over_space(ids, own, got, size):
@@ -806,10 +822,13 @@
     branch = after(branch, other)
     parts = [branch[0]] + [swap(branch[k], "chan", n_chan, k) for k in range(1, n_chan)]
 
-    sums = kernel_grad(ids, dconv, other, image16, packed, sums)
-    sums, sums_got = sum_over_space(sums, n_space)
+    sums = kernel_grad(ids, dconv, other, image16, packed, after(sums, parts[1]))
+    sums, last = sum_over_space(sums, n_space)
     d_image = image_grad(ids, dconv, other, same, cross, cotangent, taps_back)
-    output, d_kernel, d_shift, d_gain, d_scale, d_b_in = finish(ids, image, packed, sums, sums_got, parts)
+    sums = after(sums, d_image)
+    sums_got = swap(sums, "space", n_space, last)
+    output = finish(ids, image, packed, parts)
+    d_kernel, d_shift, d_gain, d_scale, d_b_in = totals(sums, sums_got)
     flat = [v.reshape(-1) for v in (d_gain, d_shift, d_b_in, d_scale)]
     return (output, d_image, d_kernel.T, *flat[:2], dw[0], flat[2], dw[1].T, flat[3])
 

time: 80.7 us -> 79 us (0.979)
  starting transfers between devices: 30.3 us -> 29.2 us
  waiting for transfers between devices: 15.8 us -> 14.7 us
    ppermute x19, waiting for transfers between devices: 15.3 us -> 14.2 us  [swap(): return lax.ppermute(value, axis, [(i, i ^ k) for i in range(size)])]
    ppermute x19, starting transfers between devices: 22.7 us -> 21.6 us  [swap(): return lax.ppermute(value, axis, [(i, i ^ k) for i in range(size)])]
    pallas_call x1 -> x2, Pallas kernels: 2.11 us -> 2.74 us  [the longest x1 2.09 us: finish(): pl.pallas_call(functools.partial(finish_kernel, len(parts)), out_shape=ja...]
  transfers between devices with their start and end apart: 23 -> 23, of which waited for: 8 -> 7; matrix products, arithmetic and copies ran while one was open for 1% -> 1% of each run, Pallas kernels for 22% -> 25%
where the time goes in v4:
time: 79 us; the launch traced here: 78.8 us
  Pallas kernels  31.2 us (39%)
  starting transfers between devices  29.2 us (37%)
  waiting for transfers between devices  14.7 us (19%)
  local copies, waits for them, and re-layouts  2.62 us (3%)
  between operations  0.86 us (1%)
    ppermute x19, starting transfers between devices, swap(): return lax.ppermute(value, axis, [(i, i ^ k) for i in range(size)])  21.6 us
    ppermute x19, waiting for transfers between devices, swap(): return lax.ppermute(value, axis, [(i, i ^ k) for i in range(size)])  14.2 us
    pallas_call x1, Pallas kernels, mlp(): pl.pallas_call(functools.partial(mlp_kernel, blocks, count), out_shape=[j...  9.33 us
    ppermute x1, starting transfers between devices, per_device(): got_a = lax.ppermute(edge_a, 'space', pairs_a)  4.94 us
    pallas_call x2, Pallas kernels, make_taps(): pl.pallas_call(functools.partial(taps_kernel, flip, height), out_shape=ja...  4.67 us
    pallas_call x1, Pallas kernels, image_grad(): pl.pallas_call(image_grad_kernel, out_shape=jax.ShapeDtypeStruct((local,...  3.5 us
    pallas_call x1, Pallas kernels, kernel_grad(): pl.pallas_call(kernel_grad_kernel, out_shape=jax.ShapeDtypeStruct((56, lo...  3.01 us
    pallas_call x1, Pallas kernels, conv_forward(): pl.pallas_call(conv_kernel, out_shape=[jax.ShapeDtypeStruct((rows, width)...  2.88 us
  transfers between devices with their start and end apart: 23, of which 7 were waited for; matrix products, arithmetic and copies ran while one was open for 1% of the time, Pallas kernels for 25%

profile of v4, /device:TPU:0, one launch (start us, length us, event | category | flops | bytes accessed | tf_op | source)
XLA Modules:
  0.0 78.8 jit_solution(17889673073079916510)
XLA Ops:
  0.7 0.8 %concatenate.3 = f32[768]{0:T(1024)S(1)} concatenate(f32[96]{0:T(128)} %param.11, f32[96]{0:T(128)} %param.12, f32[384]{0:T(512)} %param.14, f32[64]{0:T(128)S(1)} %broadcast_in_dim.9, f32[96]{0:T(128)} %param.16, f32[32]{0:T(128)S(1)} %broadcast_in_dim.10), dimensions={0} | concatenate | bytes 6144 | tf_op jit(solution)/shard_map/concatenate | solution.py:779
  1.5 0.1 pad_add_fusion.ids_ref.me_ref.core_ref
  1.5 1.0 %copy-done = bf16[96,8,256]{2,1,0:T(8,128)(2,1)S(1)} copy-done((bf16[96,8,256]{2,1,0:T(8,128)(2,1)S(1)}, bf16[96,8,256]{2,1,0:T(8,128)(2,1)}, u32[]{:S(2)}) %copy-start) | copy-done | bytes 393240
  2.5 1.4 %pack.1 = (bf16[400,256]{1,0:T(8,128)(2,1)S(1)}, bf16[400,256]{1,0:T(8,128)(2,1)S(1)}) custom-call(s32[2]{0:T(128)S(1)} %pad_add_fusion.ids_ref.me_ref.core_ref, bf16[96,8,256]{2,1,0:T(8,128)(2,1)S(1)} %copy-done, f32[1,768]{1,0:T(1,128)S(1)} %broadcast_in_dim.11.vector_ref), custom_call_target="tpu_custom_call" | custom-call | flops 1540000000 | tf_op jit(solution)/shard_map/pack/pallas_call | solution.py:168
  4.0 2.4 %collective-permute-start.4 = (bf16[400,256]{1,0:T(8,128)(2,1)S(1)}, bf16[400,256]{1,0:T(8,128)(2,1)S(1)}, u32[]{:S(2)}, u32[]{:S(2)}) collective-permute-start(bf16[400,256]{1,0:T(8,128)(2,1)S(1)} %get-tuple-element.67), channel_id=1, source_target_pairs={{0,3},{1,2},{2,1},{3,0},{4,7},{5,6},{6,5},{7,4},{8,11},{9,10},{10,... | collective-permute-start | bytes 614408 | tf_op jit(solution)/shard_map/ppermute | solution.py:747
  6.4 0.7 collective-permute-start.2
  7.1 0.1 collective-permute-start.3
  7.2 1.2 %edges.1 = (bf16[288,256]{1,0:T(8,128)(2,1)S(1)}, bf16[288,256]{1,0:T(8,128)(2,1)S(1)}) custom-call(s32[2]{0:T(128)S(1)} %pad_add_fusion.ids_ref.me_ref.core_ref, bf16[96,8,256]{2,1,0:T(8,128)(2,1)S(1)} %copy-done.2), custom_call_target="tpu_custom_call" | custom-call | flops 1320000000 | tf_op jit(solution)/shard_map/edges/pallas_call | solution.py:121
  8.4 0.7 collective-permute-start.1
  9.1 4.9 %collective-permute-start = (bf16[288,256]{1,0:T(8,128)(2,1)S(1)}, bf16[288,256]{1,0:T(8,128)(2,1)S(1)}, u32[]{:S(2)}, u32[]{:S(2)}) collective-permute-start(bf16[288,256]{1,0:T(8,128)(2,1)S(1)} %get-tuple-element.64), channel_id=1, source_target_pairs={{0,4},{4,0},{8,12},{12,8},{1,5},{5,1},{9,13},{13,9},{2,6},{6,2},{1... | collective-permute-start | bytes 442376 | tf_op jit(solution)/shard_map/ppermute | solution.py:787
  14.1 2.2 %taps_forward.1.taps_ref = bf16[5376,128]{1,0:T(8,128)(2,1)S(1)} custom-call(bf16[64,128]{1,0:T(8,128)(2,1)S(1)} %pad.4.weight_ref), custom_call_target="tpu_custom_call" | custom-call | flops 2640000000 | tf_op jit(solution)/shard_map/taps_forward/pallas_call | solution.py:78
  16.3 0.1 collective-permute-start.5
  16.4 0.5 collective-permute-start.6
  16.9 0.6 collective-permute-done.got_a_ref
  17.5 2.9 %conv_forward.1 = (bf16[384,256]{1,0:T(8,128)(2,1)S(1)}, bf16[384,256]{1,0:T(8,128)(2,1)S(1)}, bf16[96,16,256]{2,1,0:T(8,128)(2,1)S(1)}) custom-call(s32[2]{0:T(128)S(1)} %pad_add_fusion.ids_ref.me_ref.core_ref, bf16[96,8,256]{2,1,0:T(8,128)(2,1)S(1)} %copy-done.2, bf16[288,256]{1,0:T(8,128)(2,1)S(1)} %collective-permute-done.got_a_ref, ...), custom_call_target="tpu_custom_call" | custom-call | flops 5500000256 | tf_op jit(solution)/shard_map/conv_forward/pallas_call | solution.py:276
  20.4 1.1 %collective-permute-start.9 = (bf16[384,256]{1,0:T(8,128)(2,1)S(1)}, bf16[384,256]{1,0:T(8,128)(2,1)S(1)}, u32[]{:S(2)}, u32[]{:S(2)}) collective-permute-start(bf16[384,256]{1,0:T(8,128)(2,1)S(1)} %get-tuple-element.74), channel_id=1, source_target_pairs={{0,3},{1,2},{2,1},{3,0},{4,7},{5,6},{6,5},{7,4},{8,11},{9,10},{10,... | collective-permute-start | bytes 589832 | tf_op jit(solution)/shard_map/ppermute | solution.py:747
  21.4 0.6 collective-permute-start.7
  22.0 0.5 collective-permute-start.8
  22.6 2.4 %taps_back.1.taps_ref = bf16[5376,128]{1,0:T(8,128)(2,1)S(1)} custom-call(bf16[64,128]{1,0:T(8,128)(2,1)S(1)} %pad.4.weight_ref), custom_call_target="tpu_custom_call" | custom-call | flops 2640000000 | tf_op jit(solution)/shard_map/taps_back/pallas_call | solution.py:78
  25.0 0.4 turn.1
  25.4 2.2 %collective-permute-done.9.refs_3_ = bf16[384,256]{1,0:T(8,128)(2,1)S(1)} collective-permute-done((bf16[384,256]{1,0:T(8,128)(2,1)S(1)}, bf16[384,256]{1,0:T(8,128)(2,1)S(1)}, u32[]{:S(2)}, u32[]{:S(2)}) %collective-permute-start.9) | collective-permute-done | bytes 196640 | tf_op jit(solution)/shard_map/ppermute | solution.py:747
  27.6 4.3 %collective-permute-done.8.refs_2_ = bf16[384,256]{1,0:T(8,128)(2,1)S(1)} collective-permute-done((bf16[384,256]{1,0:T(8,128)(2,1)S(1)}, bf16[384,256]{1,0:T(8,128)(2,1)S(1)}, u32[]{:S(2)}, u32[]{:S(2)}) %collective-permute-start.8) | collective-permute-done | bytes 196640 | tf_op jit(solution)/shard_map/ppermute | solution.py:747
  31.8 9.3 %mlp.1 = (bf16[4,384,256]{2,1,0:T(8,128)(2,1)S(1)}, bf16[1,832,256]{2,1,0:T(8,128)(2,1)S(1)}, f32[768,256]{1,0:T(8,128)S(1)}, f32[768,256]{1,0:T(8,128)S(1)}, f3...) custom-call(s32[2]{0:T(128)S(1)} %pad_add_fusion.ids_ref.me_ref.core, ...), custom_call_target="tpu_custom_call" | custom-call | flops 8800000000 | tf_op jit(solution)/shard_map/mlp/pallas_call | solution.py:422
  41.2 0.1 collective-permute-start.10
  41.3 1.5 %collective-permute-start.11 = (bf16[1,832,256]{2,1,0:T(8,128)(2,1)S(1)}, bf16[1,832,256]{2,1,0:T(8,128)(2,1)S(1)}, u32[]{:S(2)}, u32[]{:S(2)}) collective-permute-start(bf16[1,832,256]{2,1,0:T(8,128)(2,1)S(1)} %get-tuple-element.97), channel_id=1, source_target_pairs={{0,2},{1,3},{2,0},{3,1},{4,6},{5,7},{6,4},{7,5},{8,10},{9,11},{10,... | collective-permute-start | bytes 1277960 | tf_op jit(solution)/shard_map/ppermute | solution.py:747
  42.8 0.4 collective-permute-done.10.got_ref
  43.2 0.8 merge.1
  44.0 1.8 %collective-permute-start.20 = (bf16[2,96,384]{2,1,0:T(8,128)(2,1)S(1)}, bf16[2,96,384]{2,1,0:T(8,128)(2,1)S(1)}, u32[]{:S(2)}, u32[]{:S(2)}) collective-permute-start(bf16[2,96,384]{2,1,0:T(8,128)(2,1)S(1)} %get-tuple-element.110), channel_id=1, source_target_pairs={{0,4},{4,0},{8,12},{12,8},{1,5},{5,1},{9,13},{13,9},{2,6},{6,2},{1... | collective-permute-start | bytes 442376 | tf_op jit(solution)/shard_map/ppermute | solution.py:747
  45.8 2.2 %collective-permute-start.21 = (bf16[2,96,384]{2,1,0:T(8,128)(2,1)S(1)}, bf16[2,96,384]{2,1,0:T(8,128)(2,1)S(1)}, u32[]{:S(2)}, u32[]{:S(2)}) collective-permute-start(bf16[2,96,384]{2,1,0:T(8,128)(2,1)S(1)} %get-tuple-element.111), channel_id=1, source_target_pairs={{0,8},{4,12},{8,0},{12,4},{1,9},{5,13},{9,1},{13,5},{2,10},{6,14},... | collective-permute-start | bytes 442376 | tf_op jit(solution)/shard_map/ppermute | solution.py:747
  48.1 0.4 collective-permute-start.22
  48.5 5.0 %collective-permute-done.11.refs_7_ = bf16[1,832,256]{2,1,0:T(8,128)(2,1)S(1)} collective-permute-done((bf16[1,832,256]{2,1,0:T(8,128)(2,1)S(1)}, bf16[1,832,256]{2,1,0:T(8,128)(2,1)S(1)}, u32[]{:S(2)}, u32[]{:S(2)}) %collective-permute-start.11) | collective-permute-done | bytes 426016 | tf_op jit(solution)/shard_map/ppermute | solution.py:747
  53.5 1.3 %norm_backward.1 = (bf16[4,96,256]{2,1,0:T(8,128)(2,1)S(1)}, bf16[416,256]{1,0:T(8,128)(2,1)S(1)}, bf16[3,96,256]{2,1,0:T(8,128)(2,1)S(1)}, bf16[3,96,256]{2,1,0:T(8,128)(2,1)S(1)}, f32[8,96]{1,0:T(8,128)S(1)}) custom-call(s32[2]{0:T(128)S(1)} %pad_add_fusion.ids_ref.me_ref.core_ref, f32[768,256]{1,0:T(8,128)S(1)} %get-tuple-element.88.refs_0_, ...), custom_call_target="tpu_custom_call" | custom-call | flops 1430000000 | tf_op jit(solution)/shard_map/norm_backward/pallas_call | solution.py:523
  54.8 1.3 %collective-permute-start.16 = (bf16[3,96,256]{2,1,0:T(8,128)(2,1)S(1)}, bf16[3,96,256]{2,1,0:T(8,128)(2,1)S(1)}, u32[]{:S(2)}, u32[]{:S(2)}) collective-permute-start(bf16[3,96,256]{2,1,0:T(8,128)(2,1)S(1)} %get-tuple-element.101), channel_id=1, source_target_pairs={{1,5},{3,7},{4,0},{5,9},{6,2},{7,11},{8,4},{9,13},{10,6},{11,15},{... | collective-permute-start | bytes 442376 | tf_op jit(solution)/shard_map/ppermute | solution.py:818
  56.1 0.7 collective-permute-start.17
  56.7 4.1 %collective-permute-start.12 = (bf16[416,256]{1,0:T(8,128)(2,1)S(1)}, bf16[416,256]{1,0:T(8,128)(2,1)S(1)}, u32[]{:S(2)}, u32[]{:S(2)}) collective-permute-start(bf16[416,256]{1,0:T(8,128)(2,1)S(1)} %get-tuple-element.98), channel_id=1, source_target_pairs={{0,1},{1,0},{2,3},{3,2},{4,5},{5,4},{6,7},{7,6},{8,9},{9,8},{10,11... | collective-permute-start | bytes 638984 | tf_op jit(solution)/shard_map/ppermute | solution.py:747
  60.8 0.1 add_multiply_fusion
  60.9 1.0 %collective-permute-done.12.other_ref = bf16[416,256]{1,0:T(8,128)(2,1)S(1)} collective-permute-done((bf16[416,256]{1,0:T(8,128)(2,1)S(1)}, bf16[416,256]{1,0:T(8,128)(2,1)S(1)}, u32[]{:S(2)}, u32[]{:S(2)}) %collective-permute-start.12) | collective-permute-done | bytes 213024 | tf_op jit(solution)/shard_map/ppermute | solution.py:747
  61.9 0.4 collective-permute-start.13
  62.4 0.7 slice_bitcast_fusion.4
  63.1 1.2 %collective-permute-start.15 = (bf16[384,256]{1,0:T(8,128)(2,1)S(1)}, bf16[384,256]{1,0:T(8,128)(2,1)S(1)}, u32[]{:S(2)}, u32[]{:S(2)}) collective-permute-start(bf16[384,256]{1,0:T(8,128)(2,1)S(1)} %get-tuple-element.115), channel_id=1, source_target_pairs={{0,3},{1,2},{2,1},{3,0},{4,7},{5,6},{6,5},{7,4},{8,11},{9,10},{10,... | collective-permute-start | bytes 589832 | tf_op jit(solution)/shard_map/ppermute | solution.py:747
  64.3 0.6 collective-permute-start.14
  64.9 3.0 %kernel_grad.1 = f32[56,96]{1,0:T(8,128)S(1)} custom-call(s32[2]{0:T(128)S(1)} %pad_add_fusion.ids_ref.me_ref.core_ref, bf16[4,96,256]{2,1,0:T(8,128)(2,1)S(1)} %get-tuple-element.100.own_ref, bf16[416,256]{1,0:T(8,128)(2,1)S(1)} %collective-permute-done.12.other_ref, bf16[96,16,256]{2,1,0:T(8,128)(2,1)S(1)} %get-tuple-element.103.image_ref, ...), custom_call_target="tpu_custom_call" | custom-call | flops 4400000000 | tf_op jit(solution)/shard_map/kernel_grad/pallas_call | solution.py:611
  67.9 1.8 %collective-permute-start.18 = (f32[56,96]{1,0:T(8,128)S(1)}, f32[56,96]{1,0:T(8,128)S(1)}, u32[]{:S(2)}, u32[]{:S(2)}) collective-permute-start(f32[56,96]{1,0:T(8,128)S(1)} %kernel_grad.1), channel_id=1, source_target_pairs={{0,4},{4,0},{8,12},{12,8},{1,5},{5,1},{9,13},{13,9},{2,6},{6,2},{1... | collective-permute-start | bytes 64520 | tf_op jit(solution)/shard_map/ppermute | solution.py:747
  69.7 3.5 %image_grad.1 = bf16[96,8,256]{2,1,0:T(8,128)(2,1)} custom-call(s32[2]{0:T(128)S(1)} %pad_add_fusion.ids_ref.me_ref.core_ref, bf16[4,96,256]{2,1,0:T(8,128)(2,1)S(1)} %get-tuple-element.100.own_ref, bf16[416,256]{1,0:T(8,128)(2,1)S(1)} %collective-permute-done.12.other_ref, bf16[3,96,256]{2,1,0:T(8,128)(2,1)S(1)} %collective-permute-done.16.same_ref, ...), custom_call_target="tpu_custom_call" | custom-call | flops 5500000256 | tf_op jit(solution)/shard_map/image_grad/pallas_call | solution.py:660
  73.3 1.5 %collective-permute-start.19 = (f32[56,96]{1,0:T(8,128)S(1)}, f32[56,96]{1,0:T(8,128)S(1)}, u32[]{:S(2)}, u32[]{:S(2)}) collective-permute-start(f32[56,96]{1,0:T(8,128)S(1)} %add.14.sums_ref), channel_id=1, source_target_pairs={{0,8},{4,12},{8,0},{12,4},{1,9},{5,13},{9,1},{13,5},{2,10},{6,14},... | collective-permute-start | bytes 64520 | tf_op jit(solution)/shard_map/ppermute | solution.py:747
  74.8 2.1 %finish.1 = bf16[96,8,256]{2,1,0:T(8,128)(2,1)} custom-call(s32[2]{0:T(128)S(1)} %pad_add_fusion.ids_ref.me_ref.core_ref, bf16[96,8,256]{2,1,0:T(8,128)(2,1)S(1)} %copy-done.2, f32[1,768]{1,0:T(1,128)S(1)} %broadcast_in_dim.11.vector_ref, bf16[384,256]{1,0:T(8,128)(2,1)S(1)} %get-tuple-element.118.refs_0_, ...), custom_call_target="tpu_custom_call" | custom-call | flops 2200000000 | tf_op jit(solution)/shard_map/finish/pallas_call | solution.py:704
  76.9 1.2 %collective-permute-done.19.sums_got_ref = f32[56,96]{1,0:T(8,128)S(1)} collective-permute-done((f32[56,96]{1,0:T(8,128)S(1)}, f32[56,96]{1,0:T(8,128)S(1)}, u32[]{:S(2)}, u32[]{:S(2)}) %collective-permute-start.19) | collective-permute-done | bytes 21536 | tf_op jit(solution)/shard_map/ppermute | solution.py:747
  78.1 0.7 totals.1
  (33 shorter events, 0.1 us)
Async XLA Ops:
  1.5 1.0 %copy-start = (bf16[96,8,256]{2,1,0:T(8,128)(2,1)S(1)}, bf16[96,8,256]{2,1,0:T(8,128)(2,1)}, u32[]{:S(2)}) copy-start(bf16[96,8,256]{2,1,0:T(8,128)(2,1)} %ct_ref.3) | copy-start | bytes 1179652
  2.5 4.6 %copy-start.2 = (bf16[96,8,256]{2,1,0:T(8,128)(2,1)S(1)}, bf16[96,8,256]{2,1,0:T(8,128)(2,1)}, u32[]{:S(2)}) copy-start(bf16[96,8,256]{2,1,0:T(8,128)(2,1)} %image_ref.4) | copy-start | bytes 1179652
  4.0 12.3 %collective-permute-start.4 = (bf16[400,256]{1,0:T(8,128)(2,1)S(1)}, bf16[400,256]{1,0:T(8,128)(2,1)S(1)}, u32[]{:S(2)}, u32[]{:S(2)}) collective-permute-start(bf16[400,256]{1,0:T(8,128)(2,1)S(1)} %get-tuple-element.67), channel_id=1, source_target_pairs={{0,3},{1,2},{2,1},{3,0},{4,7},{5,6},{6,5},{7,4},{8,11},{9,10},{10,... | collective-permute-start | bytes 614408 | tf_op jit(solution)/shard_map/ppermute | solution.py:747
  6.4 10.0 %collective-permute-start.2 = (bf16[400,256]{1,0:T(8,128)(2,1)S(1)}, bf16[400,256]{1,0:T(8,128)(2,1)S(1)}, u32[]{:S(2)}, u32[]{:S(2)}) collective-permute-start(bf16[400,256]{1,0:T(8,128)(2,1)S(1)} %get-tuple-element.67), channel_id=1, source_target_pairs={{0,1},{1,0},{2,3},{3,2},{4,5},{5,4},{6,7},{7,6},{8,9},{9,8},{10,11... | collective-permute-start | bytes 614408 | tf_op jit(solution)/shard_map/ppermute | solution.py:747
  7.1 6.9 %copy-start.5 = (bf16[96,49]{0,1:T(8,128)(2,1)S(1)}, bf16[96,49]{0,1:T(8,128)(2,1)}, u32[]{:S(2)}) copy-start(bf16[96,49]{0,1:T(8,128)(2,1)} %param.10) | copy-start | bytes 28228
  7.1 9.8 %collective-permute-start.3 = (bf16[400,256]{1,0:T(8,128)(2,1)S(1)}, bf16[400,256]{1,0:T(8,128)(2,1)S(1)}, u32[]{:S(2)}, u32[]{:S(2)}) collective-permute-start(bf16[400,256]{1,0:T(8,128)(2,1)S(1)} %get-tuple-element.75.refs_4_.refs_3_), channel_id=1, source_target_pairs={{0,2},{1,3},{2,0},{3,1},{4,6},{5,7},{6,4},{7,5},{8,10},{9,11},{10,... | collective-permute-start | bytes 614408 | tf_op jit(solution)/shard_map/ppermute | solution.py:747
  8.4 8.5 %collective-permute-start.1 = (bf16[288,256]{1,0:T(8,128)(2,1)S(1)}, bf16[288,256]{1,0:T(8,128)(2,1)S(1)}, u32[]{:S(2)}, u32[]{:S(2)}) collective-permute-start(bf16[288,256]{1,0:T(8,128)(2,1)S(1)} %get-tuple-element.65), channel_id=1, source_target_pairs={{4,8},{8,4},{5,9},{9,5},{6,10},{10,6},{7,11},{11,7},{20,24},{24,20... | collective-permute-start | bytes 442376 | tf_op jit(solution)/shard_map/ppermute | solution.py:788
  9.1 8.4 %collective-permute-start = (bf16[288,256]{1,0:T(8,128)(2,1)S(1)}, bf16[288,256]{1,0:T(8,128)(2,1)S(1)}, u32[]{:S(2)}, u32[]{:S(2)}) collective-permute-start(bf16[288,256]{1,0:T(8,128)(2,1)S(1)} %get-tuple-element.64), channel_id=1, source_target_pairs={{0,4},{4,0},{8,12},{12,8},{1,5},{5,1},{9,13},{13,9},{2,6},{6,2},{1... | collective-permute-start | bytes 442376 | tf_op jit(solution)/shard_map/ppermute | solution.py:787
  14.0 2.3 %copy-start.3 = (bf16[384,384]{1,0:T(8,128)(2,1)S(1)}, bf16[384,384]{1,0:T(8,128)(2,1)}, u32[]{:S(2)}) copy-start(bf16[384,384]{1,0:T(8,128)(2,1)} %refs_8_) | copy-start | bytes 884740
  14.0 2.4 %copy-start.4 = (bf16[384,384]{1,0:T(8,128)(2,1)S(1)}, bf16[384,384]{1,0:T(8,128)(2,1)}, u32[]{:S(2)}) copy-start(bf16[384,384]{1,0:T(8,128)(2,1)} %refs_12_) | copy-start | bytes 884740
  16.3 6.2 %collective-permute-start.5 = (bf16[384,384]{1,0:T(8,128)(2,1)S(1)}, bf16[384,384]{1,0:T(8,128)(2,1)S(1)}, u32[]{:S(2)}, u32[]{:S(2)}) collective-permute-start(bf16[384,384]{1,0:T(8,128)(2,1)S(1)} %copy-done.3), channel_id=1, source_target_pairs={{0,1},{1,0},{2,3},{3,2},{4,5},{5,4},{6,7},{7,6},{8,9},{9,8},{10,11... | collective-permute-start | bytes 884744 | tf_op jit(solution)/shard_map/ppermute | solution.py:747
  16.4 6.1 %collective-permute-start.6 = (bf16[384,384]{1,0:T(8,128)(2,1)S(1)}, bf16[384,384]{1,0:T(8,128)(2,1)S(1)}, u32[]{:S(2)}, u32[]{:S(2)}) collective-permute-start(bf16[384,384]{1,0:T(8,128)(2,1)S(1)} %copy-done.4), channel_id=1, source_target_pairs={{0,1},{1,0},{2,3},{3,2},{4,5},{5,4},{6,7},{7,6},{8,9},{9,8},{10,11... | collective-permute-start | bytes 884744 | tf_op jit(solution)/shard_map/ppermute | solution.py:747
  20.4 7.2 %collective-permute-start.9 = (bf16[384,256]{1,0:T(8,128)(2,1)S(1)}, bf16[384,256]{1,0:T(8,128)(2,1)S(1)}, u32[]{:S(2)}, u32[]{:S(2)}) collective-permute-start(bf16[384,256]{1,0:T(8,128)(2,1)S(1)} %get-tuple-element.74), channel_id=1, source_target_pairs={{0,3},{1,2},{2,1},{3,0},{4,7},{5,6},{6,5},{7,4},{8,11},{9,10},{10,... | collective-permute-start | bytes 589832 | tf_op jit(solution)/shard_map/ppermute | solution.py:747
  21.4 6.2 %collective-permute-start.7 = (bf16[384,256]{1,0:T(8,128)(2,1)S(1)}, bf16[384,256]{1,0:T(8,128)(2,1)S(1)}, u32[]{:S(2)}, u32[]{:S(2)}) collective-permute-start(bf16[384,256]{1,0:T(8,128)(2,1)S(1)} %get-tuple-element.74), channel_id=1, source_target_pairs={{0,1},{1,0},{2,3},{3,2},{4,5},{5,4},{6,7},{7,6},{8,9},{9,8},{10,11... | collective-permute-start | bytes 589832 | tf_op jit(solution)/shard_map/ppermute | solution.py:747
  22.0 9.8 %collective-permute-start.8 = (bf16[384,256]{1,0:T(8,128)(2,1)S(1)}, bf16[384,256]{1,0:T(8,128)(2,1)S(1)}, u32[]{:S(2)}, u32[]{:S(2)}) collective-permute-start(bf16[384,256]{1,0:T(8,128)(2,1)S(1)} %get-tuple-element.73.refs_0_), channel_id=1, source_target_pairs={{0,2},{1,3},{2,0},{3,1},{4,6},{5,7},{6,4},{7,5},{8,10},{9,11},{10,... | collective-permute-start | bytes 589832 | tf_op jit(solution)/shard_map/ppermute | solution.py:747
  41.2 2.1 %collective-permute-start.10 = (bf16[2,384,384]{2,1,0:T(8,128)(2,1)S(1)}, bf16[2,384,384]{2,1,0:T(8,128)(2,1)S(1)}, u32[]{:S(2)}, u32[]{:S(2)}) collective-permute-start(bf16[2,384,384]{2,1,0:T(8,128)(2,1)S(1)} %get-tuple-element.92), channel_id=1, source_target_pairs={{0,1},{1,0},{2,3},{3,2},{4,5},{5,4},{6,7},{7,6},{8,9},{9,8},{10,11... | collective-permute-start | bytes 1769480 | tf_op jit(solution)/shard_map/ppermute | solution.py:747
  41.3 12.2 %collective-permute-start.11 = (bf16[1,832,256]{2,1,0:T(8,128)(2,1)S(1)}, bf16[1,832,256]{2,1,0:T(8,128)(2,1)S(1)}, u32[]{:S(2)}, u32[]{:S(2)}) collective-permute-start(bf16[1,832,256]{2,1,0:T(8,128)(2,1)S(1)} %get-tuple-element.97), channel_id=1, source_target_pairs={{0,2},{1,3},{2,0},{3,1},{4,6},{5,7},{6,4},{7,5},{8,10},{9,11},{10,... | collective-permute-start | bytes 1277960 | tf_op jit(solution)/shard_map/ppermute | solution.py:747
  44.0 12.7 %collective-permute-start.20 = (bf16[2,96,384]{2,1,0:T(8,128)(2,1)S(1)}, bf16[2,96,384]{2,1,0:T(8,128)(2,1)S(1)}, u32[]{:S(2)}, u32[]{:S(2)}) collective-permute-start(bf16[2,96,384]{2,1,0:T(8,128)(2,1)S(1)} %get-tuple-element.110), channel_id=1, source_target_pairs={{0,4},{4,0},{8,12},{12,8},{1,5},{5,1},{9,13},{13,9},{2,6},{6,2},{1... | collective-permute-start | bytes 442376 | tf_op jit(solution)/shard_map/ppermute | solution.py:747
  45.8 15.0 %collective-permute-start.21 = (bf16[2,96,384]{2,1,0:T(8,128)(2,1)S(1)}, bf16[2,96,384]{2,1,0:T(8,128)(2,1)S(1)}, u32[]{:S(2)}, u32[]{:S(2)}) collective-permute-start(bf16[2,96,384]{2,1,0:T(8,128)(2,1)S(1)} %get-tuple-element.111), channel_id=1, source_target_pairs={{0,8},{4,12},{8,0},{12,4},{1,9},{5,13},{9,1},{13,5},{2,10},{6,14},... | collective-permute-start | bytes 442376 | tf_op jit(solution)/shard_map/ppermute | solution.py:747
  48.1 12.8 %collective-permute-start.22 = (bf16[2,96,384]{2,1,0:T(8,128)(2,1)S(1)}, bf16[2,96,384]{2,1,0:T(8,128)(2,1)S(1)}, u32[]{:S(2)}, u32[]{:S(2)}) collective-permute-start(bf16[2,96,384]{2,1,0:T(8,128)(2,1)S(1)} %get-tuple-element.112), channel_id=1, source_target_pairs={{0,12},{4,8},{8,4},{12,0},{1,13},{5,9},{9,5},{13,1},{2,14},{6,10},... | collective-permute-start | bytes 442376 | tf_op jit(solution)/shard_map/ppermute | solution.py:747
  54.8 15.0 %collective-permute-start.16 = (bf16[3,96,256]{2,1,0:T(8,128)(2,1)S(1)}, bf16[3,96,256]{2,1,0:T(8,128)(2,1)S(1)}, u32[]{:S(2)}, u32[]{:S(2)}) collective-permute-start(bf16[3,96,256]{2,1,0:T(8,128)(2,1)S(1)} %get-tuple-element.101), channel_id=1, source_target_pairs={{1,5},{3,7},{4,0},{5,9},{6,2},{7,11},{8,4},{9,13},{10,6},{11,15},{... | collective-permute-start | bytes 442376 | tf_op jit(solution)/shard_map/ppermute | solution.py:818
  56.1 13.7 %collective-permute-start.17 = (bf16[3,96,256]{2,1,0:T(8,128)(2,1)S(1)}, bf16[3,96,256]{2,1,0:T(8,128)(2,1)S(1)}, u32[]{:S(2)}, u32[]{:S(2)}) collective-permute-start(bf16[3,96,256]{2,1,0:T(8,128)(2,1)S(1)} %get-tuple-element.102), channel_id=1, source_target_pairs={{1,4},{3,6},{4,1},{5,8},{6,3},{7,10},{8,5},{9,12},{10,7},{11,14},{... | collective-permute-start | bytes 442376 | tf_op jit(solution)/shard_map/ppermute | solution.py:819
  56.7 5.2 %collective-permute-start.12 = (bf16[416,256]{1,0:T(8,128)(2,1)S(1)}, bf16[416,256]{1,0:T(8,128)(2,1)S(1)}, u32[]{:S(2)}, u32[]{:S(2)}) collective-permute-start(bf16[416,256]{1,0:T(8,128)(2,1)S(1)} %get-tuple-element.98), channel_id=1, source_target_pairs={{0,1},{1,0},{2,3},{3,2},{4,5},{5,4},{6,7},{7,6},{8,9},{9,8},{10,11... | collective-permute-start | bytes 638984 | tf_op jit(solution)/shard_map/ppermute | solution.py:747
  61.9 3.0 %collective-permute-start.13 = (bf16[384,256]{1,0:T(8,128)(2,1)S(1)}, bf16[384,256]{1,0:T(8,128)(2,1)S(1)}, u32[]{:S(2)}, u32[]{:S(2)}) collective-permute-start(bf16[384,256]{1,0:T(8,128)(2,1)S(1)} %get-tuple-element.117), channel_id=1, source_target_pairs={{0,1},{1,0},{2,3},{3,2},{4,5},{5,4},{6,7},{7,6},{8,9},{9,8},{10,11... | collective-permute-start | bytes 589832 | tf_op jit(solution)/shard_map/ppermute | solution.py:747
  63.1 11.7 %collective-permute-start.15 = (bf16[384,256]{1,0:T(8,128)(2,1)S(1)}, bf16[384,256]{1,0:T(8,128)(2,1)S(1)}, u32[]{:S(2)}, u32[]{:S(2)}) collective-permute-start(bf16[384,256]{1,0:T(8,128)(2,1)S(1)} %get-tuple-element.115), channel_id=1, source_target_pairs={{0,3},{1,2},{2,1},{3,0},{4,7},{5,6},{6,5},{7,4},{8,11},{9,10},{10,... | collective-permute-start | bytes 589832 | tf_op jit(solution)/shard_map/ppermute | solution.py:747
  64.3 10.4 %collective-permute-start.14 = (bf16[384,256]{1,0:T(8,128)(2,1)S(1)}, bf16[384,256]{1,0:T(8,128)(2,1)S(1)}, u32[]{:S(2)}, u32[]{:S(2)}) collective-permute-start(bf16[384,256]{1,0:T(8,128)(2,1)S(1)} %get-tuple-element.116), channel_id=1, source_target_pairs={{0,2},{1,3},{2,0},{3,1},{4,6},{5,7},{6,4},{7,5},{8,10},{9,11},{10,... | collective-permute-start | bytes 589832 | tf_op jit(solution)/shard_map/ppermute | solution.py:747
  64.9 4.8 %copy-start.1 = (bf16[96,8,256]{2,1,0:T(8,128)(2,1)S(1)}, bf16[96,8,256]{2,1,0:T(8,128)(2,1)}, u32[]{:S(2)}) copy-start(bf16[96,8,256]{2,1,0:T(8,128)(2,1)} %ct_ref.3) | copy-start | bytes 1179652
  67.9 5.3 %collective-permute-start.18 = (f32[56,96]{1,0:T(8,128)S(1)}, f32[56,96]{1,0:T(8,128)S(1)}, u32[]{:S(2)}, u32[]{:S(2)}) collective-permute-start(f32[56,96]{1,0:T(8,128)S(1)} %kernel_grad.1), channel_id=1, source_target_pairs={{0,4},{4,0},{8,12},{12,8},{1,5},{5,1},{9,13},{13,9},{2,6},{6,2},{1... | collective-permute-start | bytes 64520 | tf_op jit(solution)/shard_map/ppermute | solution.py:747
  73.3 4.9 %collective-permute-start.19 = (f32[56,96]{1,0:T(8,128)S(1)}, f32[56,96]{1,0:T(8,128)S(1)}, u32[]{:S(2)}, u32[]{:S(2)}) collective-permute-start(f32[56,96]{1,0:T(8,128)S(1)} %add.14.sums_ref), channel_id=1, source_target_pairs={{0,8},{4,12},{8,0},{12,4},{1,9},{5,13},{9,1},{13,5},{2,10},{6,14},... | collective-permute-start | bytes 64520 | tf_op jit(solution)/shard_map/ppermute | solution.py:747

commit v5 on v4

--- a/solution.py
+++ b/solution.py
@@ -261,7 +261,7 @@
                 acc_ref[half, pl.ds(g * 8 + u, height, stride=local), :] = pair[half]
         return carry
 
-    lax.fori_loop(0, local // 8, body, 0, unroll=6)
+    lax.fori_loop(0, local // 8, body, 0, unroll=True)
     for half in range(2):
         lanes = slice(half * 128, half * 128 + 128)
         mine = pl.multiple_of(core * rows, 16)
@@ -652,7 +652,7 @@
             out_ref[ch] = (ct_ref[ch].astype(F32) + jnp.concatenate(left_right, axis=1)).astype(BF)
         return carry
 
-    lax.fori_loop(0, local // 8, body, 0, unroll=6)
+    lax.fori_loop(0, local // 8, body, 0, unroll=True)
 
 
 def image_grad(core, own, other, same, cross, ct, taps):

time: 79 us -> 78.8 us (level)
  no operation moved by 1% of the time
where the time goes in v5:
time: 78.8 us; the launch traced here: 78.6 us
  Pallas kernels  30.9 us (39%)
  starting transfers between devices  29.2 us (37%)
  waiting for transfers between devices  14.8 us (19%)
  local copies, waits for them, and re-layouts  2.62 us (3%)
  between operations  0.86 us (1%)
    ppermute x19, starting transfers between devices, swap(): return lax.ppermute(value, axis, [(i, i ^ k) for i in range(size)])  21.6 us
    ppermute x19, waiting for transfers between devices, swap(): return lax.ppermute(value, axis, [(i, i ^ k) for i in range(size)])  14.2 us
    pallas_call x1, Pallas kernels, mlp(): pl.pallas_call(functools.partial(mlp_kernel, blocks, count), out_shape=[j...  9.33 us
    ppermute x1, starting transfers between devices, per_device(): got_a = lax.ppermute(edge_a, 'space', pairs_a)  4.94 us
    pallas_call x2, Pallas kernels, make_taps(): pl.pallas_call(functools.partial(taps_kernel, flip, height), out_shape=ja...  4.68 us
    pallas_call x1, Pallas kernels, image_grad(): pl.pallas_call(image_grad_kernel, out_shape=jax.ShapeDtypeStruct((local,...  3.42 us
    pallas_call x1, Pallas kernels, kernel_grad(): pl.pallas_call(kernel_grad_kernel, out_shape=jax.ShapeDtypeStruct((56, lo...  3.01 us
    pallas_call x1, Pallas kernels, conv_forward(): pl.pallas_call(conv_kernel, out_shape=[jax.ShapeDtypeStruct((rows, width)...  2.67 us
  transfers between devices with their start and end apart: 23, of which 7 were waited for; matrix products, arithmetic and copies ran while one was open for 1% of the time, Pallas kernels for 25%

profile of v5, /device:TPU:0, one launch (start us, length us, event | category | flops | bytes accessed | tf_op | source)
XLA Modules:
  0.0 78.6 jit_solution(17945891829231255251)
XLA Ops:
  0.7 0.8 %concatenate.3 = f32[768]{0:T(1024)S(1)} concatenate(f32[96]{0:T(128)} %param.11, f32[96]{0:T(128)} %param.12, f32[384]{0:T(512)} %param.14, f32[64]{0:T(128)S(1)} %broadcast_in_dim.9, f32[96]{0:T(128)} %param.16, f32[32]{0:T(128)S(1)} %broadcast_in_dim.10), dimensions={0} | concatenate | bytes 6144 | tf_op jit(solution)/shard_map/concatenate | solution.py:779
  1.5 0.1 pad_add_fusion.ids_ref.me_ref.core_ref
  1.5 1.0 %copy-done = bf16[96,8,256]{2,1,0:T(8,128)(2,1)S(1)} copy-done((bf16[96,8,256]{2,1,0:T(8,128)(2,1)S(1)}, bf16[96,8,256]{2,1,0:T(8,128)(2,1)}, u32[]{:S(2)}) %copy-start) | copy-done | bytes 393240
  2.5 1.4 %pack.1 = (bf16[400,256]{1,0:T(8,128)(2,1)S(1)}, bf16[400,256]{1,0:T(8,128)(2,1)S(1)}) custom-call(s32[2]{0:T(128)S(1)} %pad_add_fusion.ids_ref.me_ref.core_ref, bf16[96,8,256]{2,1,0:T(8,128)(2,1)S(1)} %copy-done, f32[1,768]{1,0:T(1,128)S(1)} %broadcast_in_dim.11.vector_ref), custom_call_target="tpu_custom_call" | custom-call | flops 1540000000 | tf_op jit(solution)/shard_map/pack/pallas_call | solution.py:168
  4.0 2.4 %collective-permute-start.4 = (bf16[400,256]{1,0:T(8,128)(2,1)S(1)}, bf16[400,256]{1,0:T(8,128)(2,1)S(1)}, u32[]{:S(2)}, u32[]{:S(2)}) collective-permute-start(bf16[400,256]{1,0:T(8,128)(2,1)S(1)} %get-tuple-element.67), channel_id=1, source_target_pairs={{0,3},{1,2},{2,1},{3,0},{4,7},{5,6},{6,5},{7,4},{8,11},{9,10},{10,... | collective-permute-start | bytes 614408 | tf_op jit(solution)/shard_map/ppermute | solution.py:747
  6.4 0.7 collective-permute-start.2
  7.1 0.1 collective-permute-start.3
  7.2 1.2 %edges.1 = (bf16[288,256]{1,0:T(8,128)(2,1)S(1)}, bf16[288,256]{1,0:T(8,128)(2,1)S(1)}) custom-call(s32[2]{0:T(128)S(1)} %pad_add_fusion.ids_ref.me_ref.core_ref, bf16[96,8,256]{2,1,0:T(8,128)(2,1)S(1)} %copy-done.2), custom_call_target="tpu_custom_call" | custom-call | flops 1320000000 | tf_op jit(solution)/shard_map/edges/pallas_call | solution.py:121
  8.4 0.7 collective-permute-start.1
  9.1 4.9 %collective-permute-start = (bf16[288,256]{1,0:T(8,128)(2,1)S(1)}, bf16[288,256]{1,0:T(8,128)(2,1)S(1)}, u32[]{:S(2)}, u32[]{:S(2)}) collective-permute-start(bf16[288,256]{1,0:T(8,128)(2,1)S(1)} %get-tuple-element.64), channel_id=1, source_target_pairs={{0,4},{4,0},{8,12},{12,8},{1,5},{5,1},{9,13},{13,9},{2,6},{6,2},{1... | collective-permute-start | bytes 442376 | tf_op jit(solution)/shard_map/ppermute | solution.py:787
  14.1 2.2 %taps_forward.1.taps_ref = bf16[5376,128]{1,0:T(8,128)(2,1)S(1)} custom-call(bf16[64,128]{1,0:T(8,128)(2,1)S(1)} %pad.4.weight_ref), custom_call_target="tpu_custom_call" | custom-call | flops 2640000000 | tf_op jit(solution)/shard_map/taps_forward/pallas_call | solution.py:78
  16.3 0.1 collective-permute-start.5
  16.4 0.5 collective-permute-start.6
  16.9 0.6 collective-permute-done.got_a_ref
  17.5 2.7 %conv_forward.1 = (bf16[384,256]{1,0:T(8,128)(2,1)S(1)}, bf16[384,256]{1,0:T(8,128)(2,1)S(1)}, bf16[96,16,256]{2,1,0:T(8,128)(2,1)S(1)}) custom-call(s32[2]{0:T(128)S(1)} %pad_add_fusion.ids_ref.me_ref.core_ref, bf16[96,8,256]{2,1,0:T(8,128)(2,1)S(1)} %copy-done.2, bf16[288,256]{1,0:T(8,128)(2,1)S(1)} %collective-permute-done.got_a_ref, ...), custom_call_target="tpu_custom_call" | custom-call | flops 5500000256 | tf_op jit(solution)/shard_map/conv_forward/pallas_call | solution.py:276
  20.1 1.1 %collective-permute-start.9 = (bf16[384,256]{1,0:T(8,128)(2,1)S(1)}, bf16[384,256]{1,0:T(8,128)(2,1)S(1)}, u32[]{:S(2)}, u32[]{:S(2)}) collective-permute-start(bf16[384,256]{1,0:T(8,128)(2,1)S(1)} %get-tuple-element.74), channel_id=1, source_target_pairs={{0,3},{1,2},{2,1},{3,0},{4,7},{5,6},{6,5},{7,4},{8,11},{9,10},{10,... | collective-permute-start | bytes 589832 | tf_op jit(solution)/shard_map/ppermute | solution.py:747
  21.2 0.6 collective-permute-start.7
  21.8 0.5 collective-permute-start.8
  22.4 2.4 %taps_back.1.taps_ref = bf16[5376,128]{1,0:T(8,128)(2,1)S(1)} custom-call(bf16[64,128]{1,0:T(8,128)(2,1)S(1)} %pad.4.weight_ref), custom_call_target="tpu_custom_call" | custom-call | flops 2640000000 | tf_op jit(solution)/shard_map/taps_back/pallas_call | solution.py:78
  24.8 0.4 turn.1
  25.2 2.2 %collective-permute-done.9.refs_3_ = bf16[384,256]{1,0:T(8,128)(2,1)S(1)} collective-permute-done((bf16[384,256]{1,0:T(8,128)(2,1)S(1)}, bf16[384,256]{1,0:T(8,128)(2,1)S(1)}, u32[]{:S(2)}, u32[]{:S(2)}) %collective-permute-start.9) | collective-permute-done | bytes 196640 | tf_op jit(solution)/shard_map/ppermute | solution.py:747
  27.4 4.3 %collective-permute-done.8.refs_2_ = bf16[384,256]{1,0:T(8,128)(2,1)S(1)} collective-permute-done((bf16[384,256]{1,0:T(8,128)(2,1)S(1)}, bf16[384,256]{1,0:T(8,128)(2,1)S(1)}, u32[]{:S(2)}, u32[]{:S(2)}) %collective-permute-start.8) | collective-permute-done | bytes 196640 | tf_op jit(solution)/shard_map/ppermute | solution.py:747
  31.6 9.3 %mlp.1 = (bf16[4,384,256]{2,1,0:T(8,128)(2,1)S(1)}, bf16[1,832,256]{2,1,0:T(8,128)(2,1)S(1)}, f32[768,256]{1,0:T(8,128)S(1)}, f32[768,256]{1,0:T(8,128)S(1)}, f3...) custom-call(s32[2]{0:T(128)S(1)} %pad_add_fusion.ids_ref.me_ref.core, ...), custom_call_target="tpu_custom_call" | custom-call | flops 8800000000 | tf_op jit(solution)/shard_map/mlp/pallas_call | solution.py:422
  41.0 0.1 collective-permute-start.10
  41.1 1.5 %collective-permute-start.11 = (bf16[1,832,256]{2,1,0:T(8,128)(2,1)S(1)}, bf16[1,832,256]{2,1,0:T(8,128)(2,1)S(1)}, u32[]{:S(2)}, u32[]{:S(2)}) collective-permute-start(bf16[1,832,256]{2,1,0:T(8,128)(2,1)S(1)} %get-tuple-element.97), channel_id=1, source_target_pairs={{0,2},{1,3},{2,0},{3,1},{4,6},{5,7},{6,4},{7,5},{8,10},{9,11},{10,... | collective-permute-start | bytes 1277960 | tf_op jit(solution)/shard_map/ppermute | solution.py:747
  42.6 0.4 collective-permute-done.10.got_ref
  43.0 0.8 merge.1
  43.8 1.8 %collective-permute-start.20 = (bf16[2,96,384]{2,1,0:T(8,128)(2,1)S(1)}, bf16[2,96,384]{2,1,0:T(8,128)(2,1)S(1)}, u32[]{:S(2)}, u32[]{:S(2)}) collective-permute-start(bf16[2,96,384]{2,1,0:T(8,128)(2,1)S(1)} %get-tuple-element.110), channel_id=1, source_target_pairs={{0,4},{4,0},{8,12},{12,8},{1,5},{5,1},{9,13},{13,9},{2,6},{6,2},{1... | collective-permute-start | bytes 442376 | tf_op jit(solution)/shard_map/ppermute | solution.py:747
  45.6 2.2 %collective-permute-start.21 = (bf16[2,96,384]{2,1,0:T(8,128)(2,1)S(1)}, bf16[2,96,384]{2,1,0:T(8,128)(2,1)S(1)}, u32[]{:S(2)}, u32[]{:S(2)}) collective-permute-start(bf16[2,96,384]{2,1,0:T(8,128)(2,1)S(1)} %get-tuple-element.111), channel_id=1, source_target_pairs={{0,8},{4,12},{8,0},{12,4},{1,9},{5,13},{9,1},{13,5},{2,10},{6,14},... | collective-permute-start | bytes 442376 | tf_op jit(solution)/shard_map/ppermute | solution.py:747
  47.9 0.4 collective-permute-start.22
  48.3 5.0 %collective-permute-done.11.refs_7_ = bf16[1,832,256]{2,1,0:T(8,128)(2,1)S(1)} collective-permute-done((bf16[1,832,256]{2,1,0:T(8,128)(2,1)S(1)}, bf16[1,832,256]{2,1,0:T(8,128)(2,1)S(1)}, u32[]{:S(2)}, u32[]{:S(2)}) %collective-permute-start.11) | collective-permute-done | bytes 426016 | tf_op jit(solution)/shard_map/ppermute | solution.py:747
  53.3 1.3 %norm_backward.1 = (bf16[4,96,256]{2,1,0:T(8,128)(2,1)S(1)}, bf16[416,256]{1,0:T(8,128)(2,1)S(1)}, bf16[3,96,256]{2,1,0:T(8,128)(2,1)S(1)}, bf16[3,96,256]{2,1,0:T(8,128)(2,1)S(1)}, f32[8,96]{1,0:T(8,128)S(1)}) custom-call(s32[2]{0:T(128)S(1)} %pad_add_fusion.ids_ref.me_ref.core_ref, f32[768,256]{1,0:T(8,128)S(1)} %get-tuple-element.88.refs_0_, ...), custom_call_target="tpu_custom_call" | custom-call | flops 1430000000 | tf_op jit(solution)/shard_map/norm_backward/pallas_call | solution.py:523
  54.5 1.3 %collective-permute-start.16 = (bf16[3,96,256]{2,1,0:T(8,128)(2,1)S(1)}, bf16[3,96,256]{2,1,0:T(8,128)(2,1)S(1)}, u32[]{:S(2)}, u32[]{:S(2)}) collective-permute-start(bf16[3,96,256]{2,1,0:T(8,128)(2,1)S(1)} %get-tuple-element.101), channel_id=1, source_target_pairs={{1,5},{3,7},{4,0},{5,9},{6,2},{7,11},{8,4},{9,13},{10,6},{11,15},{... | collective-permute-start | bytes 442376 | tf_op jit(solution)/shard_map/ppermute | solution.py:818
  55.8 0.7 collective-permute-start.17
  56.5 4.1 %collective-permute-start.12 = (bf16[416,256]{1,0:T(8,128)(2,1)S(1)}, bf16[416,256]{1,0:T(8,128)(2,1)S(1)}, u32[]{:S(2)}, u32[]{:S(2)}) collective-permute-start(bf16[416,256]{1,0:T(8,128)(2,1)S(1)} %get-tuple-element.98), channel_id=1, source_target_pairs={{0,1},{1,0},{2,3},{3,2},{4,5},{5,4},{6,7},{7,6},{8,9},{9,8},{10,11... | collective-permute-start | bytes 638984 | tf_op jit(solution)/shard_map/ppermute | solution.py:747
  60.6 0.1 add_multiply_fusion
  60.7 1.0 %collective-permute-done.12.other_ref = bf16[416,256]{1,0:T(8,128)(2,1)S(1)} collective-permute-done((bf16[416,256]{1,0:T(8,128)(2,1)S(1)}, bf16[416,256]{1,0:T(8,128)(2,1)S(1)}, u32[]{:S(2)}, u32[]{:S(2)}) %collective-permute-start.12) | collective-permute-done | bytes 213024 | tf_op jit(solution)/shard_map/ppermute | solution.py:747
  61.7 0.4 collective-permute-start.13
  62.2 0.7 slice_bitcast_fusion.4
  62.9 1.2 %collective-permute-start.15 = (bf16[384,256]{1,0:T(8,128)(2,1)S(1)}, bf16[384,256]{1,0:T(8,128)(2,1)S(1)}, u32[]{:S(2)}, u32[]{:S(2)}) collective-permute-start(bf16[384,256]{1,0:T(8,128)(2,1)S(1)} %get-tuple-element.115), channel_id=1, source_target_pairs={{0,3},{1,2},{2,1},{3,0},{4,7},{5,6},{6,5},{7,4},{8,11},{9,10},{10,... | collective-permute-start | bytes 589832 | tf_op jit(solution)/shard_map/ppermute | solution.py:747
  64.1 0.6 collective-permute-start.14
  64.7 3.0 %kernel_grad.1 = f32[56,96]{1,0:T(8,128)S(1)} custom-call(s32[2]{0:T(128)S(1)} %pad_add_fusion.ids_ref.me_ref.core_ref, bf16[4,96,256]{2,1,0:T(8,128)(2,1)S(1)} %get-tuple-element.100.own_ref, bf16[416,256]{1,0:T(8,128)(2,1)S(1)} %collective-permute-done.12.other_ref, bf16[96,16,256]{2,1,0:T(8,128)(2,1)S(1)} %get-tuple-element.103.image_ref, ...), custom_call_target="tpu_custom_call" | custom-call | flops 4400000000 | tf_op jit(solution)/shard_map/kernel_grad/pallas_call | solution.py:611
  67.7 1.8 %collective-permute-start.18 = (f32[56,96]{1,0:T(8,128)S(1)}, f32[56,96]{1,0:T(8,128)S(1)}, u32[]{:S(2)}, u32[]{:S(2)}) collective-permute-start(f32[56,96]{1,0:T(8,128)S(1)} %kernel_grad.1), channel_id=1, source_target_pairs={{0,4},{4,0},{8,12},{12,8},{1,5},{5,1},{9,13},{13,9},{2,6},{6,2},{1... | collective-permute-start | bytes 64520 | tf_op jit(solution)/shard_map/ppermute | solution.py:747
  69.5 3.4 %image_grad.1 = bf16[96,8,256]{2,1,0:T(8,128)(2,1)} custom-call(s32[2]{0:T(128)S(1)} %pad_add_fusion.ids_ref.me_ref.core_ref, bf16[4,96,256]{2,1,0:T(8,128)(2,1)S(1)} %get-tuple-element.100.own_ref, bf16[416,256]{1,0:T(8,128)(2,1)S(1)} %collective-permute-done.12.other_ref, bf16[3,96,256]{2,1,0:T(8,128)(2,1)S(1)} %collective-permute-done.16.same_ref, ...), custom_call_target="tpu_custom_call" | custom-call | flops 5500000256 | tf_op jit(solution)/shard_map/image_grad/pallas_call | solution.py:660
  73.0 1.5 %collective-permute-start.19 = (f32[56,96]{1,0:T(8,128)S(1)}, f32[56,96]{1,0:T(8,128)S(1)}, u32[]{:S(2)}, u32[]{:S(2)}) collective-permute-start(f32[56,96]{1,0:T(8,128)S(1)} %add.14.sums_ref), channel_id=1, source_target_pairs={{0,8},{4,12},{8,0},{12,4},{1,9},{5,13},{9,1},{13,5},{2,10},{6,14},... | collective-permute-start | bytes 64520 | tf_op jit(solution)/shard_map/ppermute | solution.py:747
  74.5 2.1 %finish.1 = bf16[96,8,256]{2,1,0:T(8,128)(2,1)} custom-call(s32[2]{0:T(128)S(1)} %pad_add_fusion.ids_ref.me_ref.core_ref, bf16[96,8,256]{2,1,0:T(8,128)(2,1)S(1)} %copy-done.2, f32[1,768]{1,0:T(1,128)S(1)} %broadcast_in_dim.11.vector_ref, bf16[384,256]{1,0:T(8,128)(2,1)S(1)} %get-tuple-element.118.refs_0_, ...), custom_call_target="tpu_custom_call" | custom-call | flops 2200000000 | tf_op jit(solution)/shard_map/finish/pallas_call | solution.py:704
  76.6 1.3 %collective-permute-done.19.sums_got_ref = f32[56,96]{1,0:T(8,128)S(1)} collective-permute-done((f32[56,96]{1,0:T(8,128)S(1)}, f32[56,96]{1,0:T(8,128)S(1)}, u32[]{:S(2)}, u32[]{:S(2)}) %collective-permute-start.19) | collective-permute-done | bytes 21536 | tf_op jit(solution)/shard_map/ppermute | solution.py:747
  77.9 0.7 totals.1
  (33 shorter events, 0.1 us)
Async XLA Ops:
  1.5 1.0 %copy-start = (bf16[96,8,256]{2,1,0:T(8,128)(2,1)S(1)}, bf16[96,8,256]{2,1,0:T(8,128)(2,1)}, u32[]{:S(2)}) copy-start(bf16[96,8,256]{2,1,0:T(8,128)(2,1)} %ct_ref.3) | copy-start | bytes 1179652
  2.5 4.6 %copy-start.2 = (bf16[96,8,256]{2,1,0:T(8,128)(2,1)S(1)}, bf16[96,8,256]{2,1,0:T(8,128)(2,1)}, u32[]{:S(2)}) copy-start(bf16[96,8,256]{2,1,0:T(8,128)(2,1)} %image_ref.4) | copy-start | bytes 1179652
  4.0 12.3 %collective-permute-start.4 = (bf16[400,256]{1,0:T(8,128)(2,1)S(1)}, bf16[400,256]{1,0:T(8,128)(2,1)S(1)}, u32[]{:S(2)}, u32[]{:S(2)}) collective-permute-start(bf16[400,256]{1,0:T(8,128)(2,1)S(1)} %get-tuple-element.67), channel_id=1, source_target_pairs={{0,3},{1,2},{2,1},{3,0},{4,7},{5,6},{6,5},{7,4},{8,11},{9,10},{10,... | collective-permute-start | bytes 614408 | tf_op jit(solution)/shard_map/ppermute | solution.py:747
  6.4 10.0 %collective-permute-start.2 = (bf16[400,256]{1,0:T(8,128)(2,1)S(1)}, bf16[400,256]{1,0:T(8,128)(2,1)S(1)}, u32[]{:S(2)}, u32[]{:S(2)}) collective-permute-start(bf16[400,256]{1,0:T(8,128)(2,1)S(1)} %get-tuple-element.67), channel_id=1, source_target_pairs={{0,1},{1,0},{2,3},{3,2},{4,5},{5,4},{6,7},{7,6},{8,9},{9,8},{10,11... | collective-permute-start | bytes 614408 | tf_op jit(solution)/shard_map/ppermute | solution.py:747
  7.1 6.9 %copy-start.5 = (bf16[96,49]{0,1:T(8,128)(2,1)S(1)}, bf16[96,49]{0,1:T(8,128)(2,1)}, u32[]{:S(2)}) copy-start(bf16[96,49]{0,1:T(8,128)(2,1)} %param.10) | copy-start | bytes 28228
  7.1 9.8 %collective-permute-start.3 = (bf16[400,256]{1,0:T(8,128)(2,1)S(1)}, bf16[400,256]{1,0:T(8,128)(2,1)S(1)}, u32[]{:S(2)}, u32[]{:S(2)}) collective-permute-start(bf16[400,256]{1,0:T(8,128)(2,1)S(1)} %get-tuple-element.75.refs_4_.refs_3_), channel_id=1, source_target_pairs={{0,2},{1,3},{2,0},{3,1},{4,6},{5,7},{6,4},{7,5},{8,10},{9,11},{10,... | collective-permute-start | bytes 614408 | tf_op jit(solution)/shard_map/ppermute | solution.py:747
  8.4 8.5 %collective-permute-start.1 = (bf16[288,256]{1,0:T(8,128)(2,1)S(1)}, bf16[288,256]{1,0:T(8,128)(2,1)S(1)}, u32[]{:S(2)}, u32[]{:S(2)}) collective-permute-start(bf16[288,256]{1,0:T(8,128)(2,1)S(1)} %get-tuple-element.65), channel_id=1, source_target_pairs={{4,8},{8,4},{5,9},{9,5},{6,10},{10,6},{7,11},{11,7},{20,24},{24,20... | collective-permute-start | bytes 442376 | tf_op jit(solution)/shard_map/ppermute | solution.py:788
  9.1 8.4 %collective-permute-start = (bf16[288,256]{1,0:T(8,128)(2,1)S(1)}, bf16[288,256]{1,0:T(8,128)(2,1)S(1)}, u32[]{:S(2)}, u32[]{:S(2)}) collective-permute-start(bf16[288,256]{1,0:T(8,128)(2,1)S(1)} %get-tuple-element.64), channel_id=1, source_target_pairs={{0,4},{4,0},{8,12},{12,8},{1,5},{5,1},{9,13},{13,9},{2,6},{6,2},{1... | collective-permute-start | bytes 442376 | tf_op jit(solution)/shard_map/ppermute | solution.py:787
  14.0 2.3 %copy-start.3 = (bf16[384,384]{1,0:T(8,128)(2,1)S(1)}, bf16[384,384]{1,0:T(8,128)(2,1)}, u32[]{:S(2)}) copy-start(bf16[384,384]{1,0:T(8,128)(2,1)} %refs_8_) | copy-start | bytes 884740
  14.0 2.4 %copy-start.4 = (bf16[384,384]{1,0:T(8,128)(2,1)S(1)}, bf16[384,384]{1,0:T(8,128)(2,1)}, u32[]{:S(2)}) copy-start(bf16[384,384]{1,0:T(8,128)(2,1)} %refs_12_) | copy-start | bytes 884740
  16.3 6.0 %collective-permute-start.5 = (bf16[384,384]{1,0:T(8,128)(2,1)S(1)}, bf16[384,384]{1,0:T(8,128)(2,1)S(1)}, u32[]{:S(2)}, u32[]{:S(2)}) collective-permute-start(bf16[384,384]{1,0:T(8,128)(2,1)S(1)} %copy-done.3), channel_id=1, source_target_pairs={{0,1},{1,0},{2,3},{3,2},{4,5},{5,4},{6,7},{7,6},{8,9},{9,8},{10,11... | collective-permute-start | bytes 884744 | tf_op jit(solution)/shard_map/ppermute | solution.py:747
  16.4 5.9 %collective-permute-start.6 = (bf16[384,384]{1,0:T(8,128)(2,1)S(1)}, bf16[384,384]{1,0:T(8,128)(2,1)S(1)}, u32[]{:S(2)}, u32[]{:S(2)}) collective-permute-start(bf16[384,384]{1,0:T(8,128)(2,1)S(1)} %copy-done.4), channel_id=1, source_target_pairs={{0,1},{1,0},{2,3},{3,2},{4,5},{5,4},{6,7},{7,6},{8,9},{9,8},{10,11... | collective-permute-start | bytes 884744 | tf_op jit(solution)/shard_map/ppermute | solution.py:747
  20.1 7.2 %collective-permute-start.9 = (bf16[384,256]{1,0:T(8,128)(2,1)S(1)}, bf16[384,256]{1,0:T(8,128)(2,1)S(1)}, u32[]{:S(2)}, u32[]{:S(2)}) collective-permute-start(bf16[384,256]{1,0:T(8,128)(2,1)S(1)} %get-tuple-element.74), channel_id=1, source_target_pairs={{0,3},{1,2},{2,1},{3,0},{4,7},{5,6},{6,5},{7,4},{8,11},{9,10},{10,... | collective-permute-start | bytes 589832 | tf_op jit(solution)/shard_map/ppermute | solution.py:747
  21.2 6.2 %collective-permute-start.7 = (bf16[384,256]{1,0:T(8,128)(2,1)S(1)}, bf16[384,256]{1,0:T(8,128)(2,1)S(1)}, u32[]{:S(2)}, u32[]{:S(2)}) collective-permute-start(bf16[384,256]{1,0:T(8,128)(2,1)S(1)} %get-tuple-element.74), channel_id=1, source_target_pairs={{0,1},{1,0},{2,3},{3,2},{4,5},{5,4},{6,7},{7,6},{8,9},{9,8},{10,11... | collective-permute-start | bytes 589832 | tf_op jit(solution)/shard_map/ppermute | solution.py:747
  21.8 9.8 %collective-permute-start.8 = (bf16[384,256]{1,0:T(8,128)(2,1)S(1)}, bf16[384,256]{1,0:T(8,128)(2,1)S(1)}, u32[]{:S(2)}, u32[]{:S(2)}) collective-permute-start(bf16[384,256]{1,0:T(8,128)(2,1)S(1)} %get-tuple-element.73.refs_0_), channel_id=1, source_target_pairs={{0,2},{1,3},{2,0},{3,1},{4,6},{5,7},{6,4},{7,5},{8,10},{9,11},{10,... | collective-permute-start | bytes 589832 | tf_op jit(solution)/shard_map/ppermute | solution.py:747
  41.0 2.1 %collective-permute-start.10 = (bf16[2,384,384]{2,1,0:T(8,128)(2,1)S(1)}, bf16[2,384,384]{2,1,0:T(8,128)(2,1)S(1)}, u32[]{:S(2)}, u32[]{:S(2)}) collective-permute-start(bf16[2,384,384]{2,1,0:T(8,128)(2,1)S(1)} %get-tuple-element.92), channel_id=1, source_target_pairs={{0,1},{1,0},{2,3},{3,2},{4,5},{5,4},{6,7},{7,6},{8,9},{9,8},{10,11... | collective-permute-start | bytes 1769480 | tf_op jit(solution)/shard_map/ppermute | solution.py:747
  41.1 12.2 %collective-permute-start.11 = (bf16[1,832,256]{2,1,0:T(8,128)(2,1)S(1)}, bf16[1,832,256]{2,1,0:T(8,128)(2,1)S(1)}, u32[]{:S(2)}, u32[]{:S(2)}) collective-permute-start(bf16[1,832,256]{2,1,0:T(8,128)(2,1)S(1)} %get-tuple-element.97), channel_id=1, source_target_pairs={{0,2},{1,3},{2,0},{3,1},{4,6},{5,7},{6,4},{7,5},{8,10},{9,11},{10,... | collective-permute-start | bytes 1277960 | tf_op jit(solution)/shard_map/ppermute | solution.py:747
  43.8 12.7 %collective-permute-start.20 = (bf16[2,96,384]{2,1,0:T(8,128)(2,1)S(1)}, bf16[2,96,384]{2,1,0:T(8,128)(2,1)S(1)}, u32[]{:S(2)}, u32[]{:S(2)}) collective-permute-start(bf16[2,96,384]{2,1,0:T(8,128)(2,1)S(1)} %get-tuple-element.110), channel_id=1, source_target_pairs={{0,4},{4,0},{8,12},{12,8},{1,5},{5,1},{9,13},{13,9},{2,6},{6,2},{1... | collective-permute-start | bytes 442376 | tf_op jit(solution)/shard_map/ppermute | solution.py:747
  45.6 15.0 %collective-permute-start.21 = (bf16[2,96,384]{2,1,0:T(8,128)(2,1)S(1)}, bf16[2,96,384]{2,1,0:T(8,128)(2,1)S(1)}, u32[]{:S(2)}, u32[]{:S(2)}) collective-permute-start(bf16[2,96,384]{2,1,0:T(8,128)(2,1)S(1)} %get-tuple-element.111), channel_id=1, source_target_pairs={{0,8},{4,12},{8,0},{12,4},{1,9},{5,13},{9,1},{13,5},{2,10},{6,14},... | collective-permute-start | bytes 442376 | tf_op jit(solution)/shard_map/ppermute | solution.py:747
  47.9 12.7 %collective-permute-start.22 = (bf16[2,96,384]{2,1,0:T(8,128)(2,1)S(1)}, bf16[2,96,384]{2,1,0:T(8,128)(2,1)S(1)}, u32[]{:S(2)}, u32[]{:S(2)}) collective-permute-start(bf16[2,96,384]{2,1,0:T(8,128)(2,1)S(1)} %get-tuple-element.112), channel_id=1, source_target_pairs={{0,12},{4,8},{8,4},{12,0},{1,13},{5,9},{9,5},{13,1},{2,14},{6,10},... | collective-permute-start | bytes 442376 | tf_op jit(solution)/shard_map/ppermute | solution.py:747
  54.5 15.0 %collective-permute-start.16 = (bf16[3,96,256]{2,1,0:T(8,128)(2,1)S(1)}, bf16[3,96,256]{2,1,0:T(8,128)(2,1)S(1)}, u32[]{:S(2)}, u32[]{:S(2)}) collective-permute-start(bf16[3,96,256]{2,1,0:T(8,128)(2,1)S(1)} %get-tuple-element.101), channel_id=1, source_target_pairs={{1,5},{3,7},{4,0},{5,9},{6,2},{7,11},{8,4},{9,13},{10,6},{11,15},{... | collective-permute-start | bytes 442376 | tf_op jit(solution)/shard_map/ppermute | solution.py:818
  55.8 13.7 %collective-permute-start.17 = (bf16[3,96,256]{2,1,0:T(8,128)(2,1)S(1)}, bf16[3,96,256]{2,1,0:T(8,128)(2,1)S(1)}, u32[]{:S(2)}, u32[]{:S(2)}) collective-permute-start(bf16[3,96,256]{2,1,0:T(8,128)(2,1)S(1)} %get-tuple-element.102), channel_id=1, source_target_pairs={{1,4},{3,6},{4,1},{5,8},{6,3},{7,10},{8,5},{9,12},{10,7},{11,14},{... | collective-permute-start | bytes 442376 | tf_op jit(solution)/shard_map/ppermute | solution.py:819
  56.5 5.2 %collective-permute-start.12 = (bf16[416,256]{1,0:T(8,128)(2,1)S(1)}, bf16[416,256]{1,0:T(8,128)(2,1)S(1)}, u32[]{:S(2)}, u32[]{:S(2)}) collective-permute-start(bf16[416,256]{1,0:T(8,128)(2,1)S(1)} %get-tuple-element.98), channel_id=1, source_target_pairs={{0,1},{1,0},{2,3},{3,2},{4,5},{5,4},{6,7},{7,6},{8,9},{9,8},{10,11... | collective-permute-start | bytes 638984 | tf_op jit(solution)/shard_map/ppermute | solution.py:747
  61.7 3.0 %collective-permute-start.13 = (bf16[384,256]{1,0:T(8,128)(2,1)S(1)}, bf16[384,256]{1,0:T(8,128)(2,1)S(1)}, u32[]{:S(2)}, u32[]{:S(2)}) collective-permute-start(bf16[384,256]{1,0:T(8,128)(2,1)S(1)} %get-tuple-element.117), channel_id=1, source_target_pairs={{0,1},{1,0},{2,3},{3,2},{4,5},{5,4},{6,7},{7,6},{8,9},{9,8},{10,11... | collective-permute-start | bytes 589832 | tf_op jit(solution)/shard_map/ppermute | solution.py:747
  62.9 11.6 %collective-permute-start.15 = (bf16[384,256]{1,0:T(8,128)(2,1)S(1)}, bf16[384,256]{1,0:T(8,128)(2,1)S(1)}, u32[]{:S(2)}, u32[]{:S(2)}) collective-permute-start(bf16[384,256]{1,0:T(8,128)(2,1)S(1)} %get-tuple-element.115), channel_id=1, source_target_pairs={{0,3},{1,2},{2,1},{3,0},{4,7},{5,6},{6,5},{7,4},{8,11},{9,10},{10,... | collective-permute-start | bytes 589832 | tf_op jit(solution)/shard_map/ppermute | solution.py:747
  64.1 10.4 %collective-permute-start.14 = (bf16[384,256]{1,0:T(8,128)(2,1)S(1)}, bf16[384,256]{1,0:T(8,128)(2,1)S(1)}, u32[]{:S(2)}, u32[]{:S(2)}) collective-permute-start(bf16[384,256]{1,0:T(8,128)(2,1)S(1)} %get-tuple-element.116), channel_id=1, source_target_pairs={{0,2},{1,3},{2,0},{3,1},{4,6},{5,7},{6,4},{7,5},{8,10},{9,11},{10,... | collective-permute-start | bytes 589832 | tf_op jit(solution)/shard_map/ppermute | solution.py:747
  64.7 4.8 %copy-start.1 = (bf16[96,8,256]{2,1,0:T(8,128)(2,1)S(1)}, bf16[96,8,256]{2,1,0:T(8,128)(2,1)}, u32[]{:S(2)}) copy-start(bf16[96,8,256]{2,1,0:T(8,128)(2,1)} %ct_ref.3) | copy-start | bytes 1179652
  67.7 5.2 %collective-permute-start.18 = (f32[56,96]{1,0:T(8,128)S(1)}, f32[56,96]{1,0:T(8,128)S(1)}, u32[]{:S(2)}, u32[]{:S(2)}) collective-permute-start(f32[56,96]{1,0:T(8,128)S(1)} %kernel_grad.1), channel_id=1, source_target_pairs={{0,4},{4,0},{8,12},{12,8},{1,5},{5,1},{9,13},{13,9},{2,6},{6,2},{1... | collective-permute-start | bytes 64520 | tf_op jit(solution)/shard_map/ppermute | solution.py:747
  73.0 5.0 %collective-permute-start.19 = (f32[56,96]{1,0:T(8,128)S(1)}, f32[56,96]{1,0:T(8,128)S(1)}, u32[]{:S(2)}, u32[]{:S(2)}) collective-permute-start(f32[56,96]{1,0:T(8,128)S(1)} %add.14.sums_ref), channel_id=1, source_target_pairs={{0,8},{4,12},{8,0},{12,4},{1,9},{5,13},{9,1},{13,5},{2,10},{6,14},... | collective-permute-start | bytes 64520 | tf_op jit(solution)/shard_map/ppermute | solution.py:747
